TPU v7x, 128 devices: a whole 4x4x4 slice. The times are simulated.
128 devices in a mesh: blk: 16 (over x_hi, y, core), bal: 8 (over x_lo, z).
Axes of the slice: x: 4 (x_hi: 2, x_lo: 2; x = x_hi * 2 + x_lo), y: 4, z: 4, core: 2. Of those that a mesh axis runs over, the one named last changes fastest.
Arguments:
- features: bfloat16 [131072, 512], P('blk', 'bal'), may hold values from -6 to 6
- tile_values: bfloat16 [16, 16, 32, 128, 128], P('blk'), may hold values from 0.049804688 to 1
- tile_rows: int32 [16, 16, 32], P('blk'), may hold values from 0 to 63
- tile_cols: int32 [16, 16, 32], P('blk'), may hold values from 0 to 63
- tile_counts: int32 [16, 16], P('blk'), may hold values from 8 to 32, as said below
- w_self: bfloat16 [512, 512], replicated, may hold values from -0.25 to 0.25
- w_neigh: bfloat16 [512, 512], replicated, may hold values from -6 to 6
- bias: float32 [512], replicated, may hold values from -3 to 3
- part_map: int32 [16, 64], P('blk'), may hold values from 0 to 7, as said below
Outputs:
- next_rows: bfloat16 [16, 8, 2048, 512], P('blk', 'bal')
Inputs may be any that keep to these rules, and one draw needn't show every extreme that they name: `tile_counts`: live slots of one pair of vertex blocks; the most, 32, is reached by some pair in every draw. `part_map`: within one block of vertex rows at most 16 tiles go to any one value, and exactly 16 to some value.
All inputs are finite; a program needn't handle non-finite values.
Results may differ from a plain program's by a relative error of at most 0.0036.
Values may be sent and summed in bfloat16 or wider, within the bound.
No kernel may reach another device: no remote copies, remote signals or barrier semaphores. Data moves between devices by JAX's collectives and lax.ppermute only.
A program may use at most 128 MiB of HBM per device.

v0:
```python
import jax
import jax.numpy as jnp
from jax import lax
from jax.sharding import PartitionSpec as P

TILE = 128


def from_behind(block, axis, distance):
    devices = range(lax.axis_size(axis))
    route = [((i - distance) % len(devices), i) for i in devices]
    return lax.ppermute(block, axis, route)


def advance(block, steps_by):
    return from_behind(block, "blk", steps_by)


def on_device(
    features, tile_values, tile_rows, tile_cols, tile_counts, w_self, w_neigh, bias, part_map
):
    n_blk = lax.axis_size("blk")
    n_bal = lax.axis_size("bal")
    here = lax.axis_index("blk")
    column = lax.axis_index("bal")
    width = features.shape[1]
    tiles_per = part_map.shape[1]
    values = tile_values[0]
    rows_idx = tile_rows[0]
    cols_idx = tile_cols[0]
    counts = tile_counts[0]
    slots = values.shape[1]
    live = jnp.arange(slots)[None, :] < counts[:, None]
    row_hot = (
        (rows_idx[:, :, None] == jnp.arange(tiles_per)[None, None, :]) & live[:, :, None]
    ).astype(jnp.float32)
    row_mass = jnp.einsum(
        "csij,j->csi", values, jnp.ones((TILE,), jnp.bfloat16), preferred_element_type=jnp.float32
    )
    degree = 1.0 + jnp.einsum("cst,csi->ti", row_hot, row_mass, precision=lax.Precision.HIGHEST)

    def absorb(total, block, source):
        tiles = block.reshape(tiles_per, TILE, width)
        vals = lax.dynamic_index_in_dim(values, source, 0, keepdims=False)
        picks = lax.dynamic_index_in_dim(cols_idx, source, 0, keepdims=False)
        targets = lax.dynamic_index_in_dim(rows_idx, source, 0, keepdims=False)
        alive = lax.dynamic_index_in_dim(live, source, 0, keepdims=False)
        gathered = jnp.take(tiles, picks, axis=0)
        prod = jnp.einsum("sij,sjf->sif", vals, gathered, preferred_element_type=jnp.float32)
        masked = jnp.where(alive[:, None, None], prod, 0.0)
        return total.at[targets].add(masked)

    empty = jnp.zeros((tiles_per, TILE, width), jnp.float32)

    def step_one(index, carry):
        total, block = carry
        total = absorb(total, block, (here - index) % n_blk)
        block = advance(block, 1)
        return (total, block)

    total, block = lax.fori_loop(0, n_blk - 1, step_one, (empty, features))
    total = absorb(total, block, (here - (n_blk - 1)) % n_blk)
    mean_agg = (total / degree[:, :, None]).astype(jnp.bfloat16).reshape(tiles_per * TILE, width)
    capacity = 2 * tiles_per // n_bal
    mapping = part_map[0]
    dest_hot = (mapping[:, None] == jnp.arange(n_bal)[None, :]).astype(jnp.int32)
    ranks = jnp.cumsum(dest_hot, axis=0) - dest_hot
    place = mapping * capacity + jnp.sum(ranks * dest_hot, axis=1)
    select = (jnp.arange(n_bal * capacity)[:, None] == place[None, :]).astype(jnp.bfloat16)
    col_start = column * width
    zeros_out = jnp.zeros((tiles_per * TILE, width), jnp.float32)
    carry = zeros_out
    mean_piece = lax.all_gather(mean_agg, "bal", axis=1, tiled=True)
    feat_piece = lax.all_gather(features, "bal", axis=1, tiled=True)
    count = mean_piece.shape[1]
    neigh_part = lax.dynamic_slice(w_neigh, (0, col_start), (count, width))
    self_part = lax.dynamic_slice(w_self, (0, col_start), (count, width))
    carry = jnp.dot(mean_piece, neigh_part, preferred_element_type=jnp.float32)
    pre = carry + jnp.dot(feat_piece, self_part, preferred_element_type=jnp.float32)
    pre = pre + lax.dynamic_slice_in_dim(bias, col_start, width)
    hidden = jnp.maximum(pre, 0.0).astype(jnp.bfloat16)
    tiles = hidden.reshape(tiles_per, TILE, width)
    placed = jnp.einsum("kt,tif->kif", select, tiles, preferred_element_type=jnp.float32)
    result = lax.all_to_all(
        placed.astype(jnp.bfloat16).reshape(n_bal, capacity * TILE, width),
        "bal",
        split_axis=0,
        concat_axis=2,
        tiled=True,
    )
    return result[None]


def solution(mesh):
    placed = (
        P("blk", "bal"),
        P("blk", None, None, None, None),
        P("blk", None, None),
        P("blk", None, None),
        P("blk", None),
        P(),
        P(),
        P(),
        P("blk", None),
    )
    return jax.shard_map(
        on_device,
        mesh=mesh,
        in_specs=placed,
        out_specs=P("blk", "bal", None, None),
        check_vma=False,
    )
```

profile of v0, /device:TPU:1, one launch (start us, length us, event | category | flops | bytes accessed | tf_op | source)
XLA Modules:
  0.0 527.4 jit_solution(13366378268195812882)
XLA Ops:
  12.0 328.9 %while.17 = (s32[]{:T(128)}, f32[64,128,64]{1,2,0:T(8,128)}, bf16[8192,64]{0,1:T(8,128)(2,1)}, s32[]{:T(128)}, s32[16,32]{1,0:T(8,128)S(1)}, /*index=5*/pred[16,...) while((s32[]{:T(128)}, f32[64,128,64]{1,2,0:T(8,128)}, ...), condition=%wide.region_4.6_spmd, body=%wide.region_2.5_spmd.sunk | while | flops 67896624 | bytes 15209832 | solution.py:61
  19.7 4.8 scatter_fusion
  35.3 4.8 scatter_fusion
  40.1 6.8 %collective-permute-done = bf16[8192,64]{0,1:T(8,128)(2,1)} collective-permute-done((bf16[8192,64]{0,1:T(8,128)(2,1)S(1)}, bf16[8192,64]{0,1:T(8,128)(2,1)}, u32[]{:S(2)}, u32[]{:S(2)}) %collective-permute-start) | collective-permute-done | bytes 1048608 | tf_op jit(solution)/shard_map/while/body/eval_jaxpr/ppermute | solution.py:12
  51.9 4.8 scatter_fusion
  56.7 31.8 %collective-permute-done = bf16[8192,64]{0,1:T(8,128)(2,1)} collective-permute-done((bf16[8192,64]{0,1:T(8,128)(2,1)S(1)}, bf16[8192,64]{0,1:T(8,128)(2,1)}, u32[]{:S(2)}, u32[]{:S(2)}) %collective-permute-start) | collective-permute-done | bytes 1048608 | tf_op jit(solution)/shard_map/while/body/eval_jaxpr/ppermute | solution.py:12
  93.5 4.8 scatter_fusion
  98.3 31.8 %collective-permute-done = bf16[8192,64]{0,1:T(8,128)(2,1)} collective-permute-done((bf16[8192,64]{0,1:T(8,128)(2,1)S(1)}, bf16[8192,64]{0,1:T(8,128)(2,1)}, u32[]{:S(2)}, u32[]{:S(2)}) %collective-permute-start) | collective-permute-done | bytes 1048608 | tf_op jit(solution)/shard_map/while/body/eval_jaxpr/ppermute | solution.py:12
  139.9 9.4 %collective-permute-done = bf16[8192,64]{0,1:T(8,128)(2,1)} collective-permute-done((bf16[8192,64]{0,1:T(8,128)(2,1)S(1)}, bf16[8192,64]{0,1:T(8,128)(2,1)}, u32[]{:S(2)}, u32[]{:S(2)}) %collective-permute-start) | collective-permute-done | bytes 1048608 | tf_op jit(solution)/shard_map/while/body/eval_jaxpr/ppermute | solution.py:12
  159.0 9.4 %collective-permute-done = bf16[8192,64]{0,1:T(8,128)(2,1)} collective-permute-done((bf16[8192,64]{0,1:T(8,128)(2,1)S(1)}, bf16[8192,64]{0,1:T(8,128)(2,1)}, u32[]{:S(2)}, u32[]{:S(2)}) %collective-permute-start) | collective-permute-done | bytes 1048608 | tf_op jit(solution)/shard_map/while/body/eval_jaxpr/ppermute | solution.py:12
  178.2 9.4 %collective-permute-done = bf16[8192,64]{0,1:T(8,128)(2,1)} collective-permute-done((bf16[8192,64]{0,1:T(8,128)(2,1)S(1)}, bf16[8192,64]{0,1:T(8,128)(2,1)}, u32[]{:S(2)}, u32[]{:S(2)}) %collective-permute-start) | collective-permute-done | bytes 1048608 | tf_op jit(solution)/shard_map/while/body/eval_jaxpr/ppermute | solution.py:12
  197.4 9.4 %collective-permute-done = bf16[8192,64]{0,1:T(8,128)(2,1)} collective-permute-done((bf16[8192,64]{0,1:T(8,128)(2,1)S(1)}, bf16[8192,64]{0,1:T(8,128)(2,1)}, u32[]{:S(2)}, u32[]{:S(2)}) %collective-permute-start) | collective-permute-done | bytes 1048608 | tf_op jit(solution)/shard_map/while/body/eval_jaxpr/ppermute | solution.py:12
  216.5 9.4 %collective-permute-done = bf16[8192,64]{0,1:T(8,128)(2,1)} collective-permute-done((bf16[8192,64]{0,1:T(8,128)(2,1)S(1)}, bf16[8192,64]{0,1:T(8,128)(2,1)}, u32[]{:S(2)}, u32[]{:S(2)}) %collective-permute-start) | collective-permute-done | bytes 1048608 | tf_op jit(solution)/shard_map/while/body/eval_jaxpr/ppermute | solution.py:12
  235.7 9.4 %collective-permute-done = bf16[8192,64]{0,1:T(8,128)(2,1)} collective-permute-done((bf16[8192,64]{0,1:T(8,128)(2,1)S(1)}, bf16[8192,64]{0,1:T(8,128)(2,1)}, u32[]{:S(2)}, u32[]{:S(2)}) %collective-permute-start) | collective-permute-done | bytes 1048608 | tf_op jit(solution)/shard_map/while/body/eval_jaxpr/ppermute | solution.py:12
  254.9 9.4 %collective-permute-done = bf16[8192,64]{0,1:T(8,128)(2,1)} collective-permute-done((bf16[8192,64]{0,1:T(8,128)(2,1)S(1)}, bf16[8192,64]{0,1:T(8,128)(2,1)}, u32[]{:S(2)}, u32[]{:S(2)}) %collective-permute-start) | collective-permute-done | bytes 1048608 | tf_op jit(solution)/shard_map/while/body/eval_jaxpr/ppermute | solution.py:12
  274.0 9.4 %collective-permute-done = bf16[8192,64]{0,1:T(8,128)(2,1)} collective-permute-done((bf16[8192,64]{0,1:T(8,128)(2,1)S(1)}, bf16[8192,64]{0,1:T(8,128)(2,1)}, u32[]{:S(2)}, u32[]{:S(2)}) %collective-permute-start) | collective-permute-done | bytes 1048608 | tf_op jit(solution)/shard_map/while/body/eval_jaxpr/ppermute | solution.py:12
  293.2 9.4 %collective-permute-done = bf16[8192,64]{0,1:T(8,128)(2,1)} collective-permute-done((bf16[8192,64]{0,1:T(8,128)(2,1)S(1)}, bf16[8192,64]{0,1:T(8,128)(2,1)}, u32[]{:S(2)}, u32[]{:S(2)}) %collective-permute-start) | collective-permute-done | bytes 1048608 | tf_op jit(solution)/shard_map/while/body/eval_jaxpr/ppermute | solution.py:12
  312.4 9.4 %collective-permute-done = bf16[8192,64]{0,1:T(8,128)(2,1)} collective-permute-done((bf16[8192,64]{0,1:T(8,128)(2,1)S(1)}, bf16[8192,64]{0,1:T(8,128)(2,1)}, u32[]{:S(2)}, u32[]{:S(2)}) %collective-permute-start) | collective-permute-done | bytes 1048608 | tf_op jit(solution)/shard_map/while/body/eval_jaxpr/ppermute | solution.py:12
  331.6 9.4 %collective-permute-done = bf16[8192,64]{0,1:T(8,128)(2,1)} collective-permute-done((bf16[8192,64]{0,1:T(8,128)(2,1)S(1)}, bf16[8192,64]{0,1:T(8,128)(2,1)}, u32[]{:S(2)}, u32[]{:S(2)}) %collective-permute-start) | collective-permute-done | bytes 1048608 | tf_op jit(solution)/shard_map/while/body/eval_jaxpr/ppermute | solution.py:12
  352.4 10.2 %fusion.38 = f32[1,16,32,128]{3,0,2,1:T(1,128)S(1)} fusion(bf16[1,16,32,128,128]{4,3,2,1,0:T(8,128)(2,1)} %bitcast.106), kind=kOutput, calls=%fused_computation.70 | convolution fusion | flops 16777216 | bytes 17039360 | tf_op jit(solution)/shard_map/csij,j->csi/dot_general | solution.py:37
  365.4 5.1 convolution_bitcast_fusion
  370.5 108.0 %all-gather.3.cloned.1.call-done = bf16[8192,512]{0,1:T(8,128)(2,1)} async-done(((bf16[8192,64]{0,1:T(8,128)(2,1)}), bf16[8192,512]{0,1:T(8,128)(2,1)}) %all-gather.3.cloned.1.call-update) | async-done | bytes 8388624 | tf_op jit(solution)/shard_map/all_gather | solution.py:73
  478.6 5.2 fusion.13
  489.9 28.2 %all_to_all.15 = bf16[8,2048,64]{1,2,0:T(8,128)(2,1)S(1)} all-to-all(bf16[8,2048,64]{1,2,0:T(8,128)(2,1)S(1)} %copy.17), channel_id=1, replica_groups=mesh['blk'=16,'bal'=8] {'bal'}, dimensions={0} | all-to-all | bytes 4194304 | tf_op jit(solution)/shard_map/all_to_all | solution.py:84
  (185 shorter events, 163.8 us)
Async XLA Ops:
  6.5 358.9 %copy-start = (bf16[512,512]{1,0:T(8,128)(2,1)S(1)}, bf16[512,512]{1,0:T(8,128)(2,1)}, u32[]{:S(2)}) copy-start(bf16[512,512]{1,0:T(8,128)(2,1)} %param.18) | copy-start | bytes 1572868
  6.5 3.1 copy-start.3
  6.5 358.9 %all-gather.5.cloned.1.call-start = ((), (), s32[]{:S(2)}) async-start(), calls=%async_computation.2 | async-start | bytes 9437184 | tf_op jit(solution)/shard_map/all_gather | solution.py:74
  7.3 471.3 %all-gather.3.cloned.1.call-start = ((), (), s32[]{:S(2)}) async-start(), calls=%async_computation.1 | async-start | bytes 9437184 | tf_op jit(solution)/shard_map/all_gather | solution.py:73
  7.3 4.7 copy-start.4
  13.3 14.4 %collective-permute-start = (bf16[8192,64]{0,1:T(8,128)(2,1)S(1)}, bf16[8192,64]{0,1:T(8,128)(2,1)}, u32[]{:S(2)}, u32[]{:S(2)}) collective-permute-start(bf16[8192,64]{0,1:T(8,128)(2,1)S(1)} %copy.36), channel_id=1, source_target_pairs={{120,0},{0,8},{8,16},{16,24},{24,32},{32,40},{40,48},{48,56},{56,6... | collective-permute-start | bytes 3145736 | tf_op jit(solution)/shard_map/while/body/eval_jaxpr/ppermute | solution.py:12
  28.9 17.9 %collective-permute-start = (bf16[8192,64]{0,1:T(8,128)(2,1)S(1)}, bf16[8192,64]{0,1:T(8,128)(2,1)}, u32[]{:S(2)}, u32[]{:S(2)}) collective-permute-start(bf16[8192,64]{0,1:T(8,128)(2,1)S(1)} %copy.36), channel_id=1, source_target_pairs={{120,0},{0,8},{8,16},{16,24},{24,32},{32,40},{40,48},{48,56},{56,6... | collective-permute-start | bytes 3145736 | tf_op jit(solution)/shard_map/while/body/eval_jaxpr/ppermute | solution.py:12
  48.1 40.4 %collective-permute-start = (bf16[8192,64]{0,1:T(8,128)(2,1)S(1)}, bf16[8192,64]{0,1:T(8,128)(2,1)}, u32[]{:S(2)}, u32[]{:S(2)}) collective-permute-start(bf16[8192,64]{0,1:T(8,128)(2,1)S(1)} %copy.36), channel_id=1, source_target_pairs={{120,0},{0,8},{8,16},{16,24},{24,32},{32,40},{40,48},{48,56},{56,6... | collective-permute-start | bytes 3145736 | tf_op jit(solution)/shard_map/while/body/eval_jaxpr/ppermute | solution.py:12
  89.7 40.4 %collective-permute-start = (bf16[8192,64]{0,1:T(8,128)(2,1)S(1)}, bf16[8192,64]{0,1:T(8,128)(2,1)}, u32[]{:S(2)}, u32[]{:S(2)}) collective-permute-start(bf16[8192,64]{0,1:T(8,128)(2,1)S(1)} %copy.36), channel_id=1, source_target_pairs={{120,0},{0,8},{8,16},{16,24},{24,32},{32,40},{40,48},{48,56},{56,6... | collective-permute-start | bytes 3145736 | tf_op jit(solution)/shard_map/while/body/eval_jaxpr/ppermute | solution.py:12
  131.3 17.9 %collective-permute-start = (bf16[8192,64]{0,1:T(8,128)(2,1)S(1)}, bf16[8192,64]{0,1:T(8,128)(2,1)}, u32[]{:S(2)}, u32[]{:S(2)}) collective-permute-start(bf16[8192,64]{0,1:T(8,128)(2,1)S(1)} %copy.36), channel_id=1, source_target_pairs={{120,0},{0,8},{8,16},{16,24},{24,32},{32,40},{40,48},{48,56},{56,6... | collective-permute-start | bytes 3145736 | tf_op jit(solution)/shard_map/while/body/eval_jaxpr/ppermute | solution.py:12
  150.5 17.9 %collective-permute-start = (bf16[8192,64]{0,1:T(8,128)(2,1)S(1)}, bf16[8192,64]{0,1:T(8,128)(2,1)}, u32[]{:S(2)}, u32[]{:S(2)}) collective-permute-start(bf16[8192,64]{0,1:T(8,128)(2,1)S(1)} %copy.36), channel_id=1, source_target_pairs={{120,0},{0,8},{8,16},{16,24},{24,32},{32,40},{40,48},{48,56},{56,6... | collective-permute-start | bytes 3145736 | tf_op jit(solution)/shard_map/while/body/eval_jaxpr/ppermute | solution.py:12
  169.6 17.9 %collective-permute-start = (bf16[8192,64]{0,1:T(8,128)(2,1)S(1)}, bf16[8192,64]{0,1:T(8,128)(2,1)}, u32[]{:S(2)}, u32[]{:S(2)}) collective-permute-start(bf16[8192,64]{0,1:T(8,128)(2,1)S(1)} %copy.36), channel_id=1, source_target_pairs={{120,0},{0,8},{8,16},{16,24},{24,32},{32,40},{40,48},{48,56},{56,6... | collective-permute-start | bytes 3145736 | tf_op jit(solution)/shard_map/while/body/eval_jaxpr/ppermute | solution.py:12
  188.8 17.9 %collective-permute-start = (bf16[8192,64]{0,1:T(8,128)(2,1)S(1)}, bf16[8192,64]{0,1:T(8,128)(2,1)}, u32[]{:S(2)}, u32[]{:S(2)}) collective-permute-start(bf16[8192,64]{0,1:T(8,128)(2,1)S(1)} %copy.36), channel_id=1, source_target_pairs={{120,0},{0,8},{8,16},{16,24},{24,32},{32,40},{40,48},{48,56},{56,6... | collective-permute-start | bytes 3145736 | tf_op jit(solution)/shard_map/while/body/eval_jaxpr/ppermute | solution.py:12
  208.0 17.9 %collective-permute-start = (bf16[8192,64]{0,1:T(8,128)(2,1)S(1)}, bf16[8192,64]{0,1:T(8,128)(2,1)}, u32[]{:S(2)}, u32[]{:S(2)}) collective-permute-start(bf16[8192,64]{0,1:T(8,128)(2,1)S(1)} %copy.36), channel_id=1, source_target_pairs={{120,0},{0,8},{8,16},{16,24},{24,32},{32,40},{40,48},{48,56},{56,6... | collective-permute-start | bytes 3145736 | tf_op jit(solution)/shard_map/while/body/eval_jaxpr/ppermute | solution.py:12
  227.2 17.9 %collective-permute-start = (bf16[8192,64]{0,1:T(8,128)(2,1)S(1)}, bf16[8192,64]{0,1:T(8,128)(2,1)}, u32[]{:S(2)}, u32[]{:S(2)}) collective-permute-start(bf16[8192,64]{0,1:T(8,128)(2,1)S(1)} %copy.36), channel_id=1, source_target_pairs={{120,0},{0,8},{8,16},{16,24},{24,32},{32,40},{40,48},{48,56},{56,6... | collective-permute-start | bytes 3145736 | tf_op jit(solution)/shard_map/while/body/eval_jaxpr/ppermute | solution.py:12
  246.3 17.9 %collective-permute-start = (bf16[8192,64]{0,1:T(8,128)(2,1)S(1)}, bf16[8192,64]{0,1:T(8,128)(2,1)}, u32[]{:S(2)}, u32[]{:S(2)}) collective-permute-start(bf16[8192,64]{0,1:T(8,128)(2,1)S(1)} %copy.36), channel_id=1, source_target_pairs={{120,0},{0,8},{8,16},{16,24},{24,32},{32,40},{40,48},{48,56},{56,6... | collective-permute-start | bytes 3145736 | tf_op jit(solution)/shard_map/while/body/eval_jaxpr/ppermute | solution.py:12
  265.5 17.9 %collective-permute-start = (bf16[8192,64]{0,1:T(8,128)(2,1)S(1)}, bf16[8192,64]{0,1:T(8,128)(2,1)}, u32[]{:S(2)}, u32[]{:S(2)}) collective-permute-start(bf16[8192,64]{0,1:T(8,128)(2,1)S(1)} %copy.36), channel_id=1, source_target_pairs={{120,0},{0,8},{8,16},{16,24},{24,32},{32,40},{40,48},{48,56},{56,6... | collective-permute-start | bytes 3145736 | tf_op jit(solution)/shard_map/while/body/eval_jaxpr/ppermute | solution.py:12
  284.7 17.9 %collective-permute-start = (bf16[8192,64]{0,1:T(8,128)(2,1)S(1)}, bf16[8192,64]{0,1:T(8,128)(2,1)}, u32[]{:S(2)}, u32[]{:S(2)}) collective-permute-start(bf16[8192,64]{0,1:T(8,128)(2,1)S(1)} %copy.36), channel_id=1, source_target_pairs={{120,0},{0,8},{8,16},{16,24},{24,32},{32,40},{40,48},{48,56},{56,6... | collective-permute-start | bytes 3145736 | tf_op jit(solution)/shard_map/while/body/eval_jaxpr/ppermute | solution.py:12
  303.8 17.9 %collective-permute-start = (bf16[8192,64]{0,1:T(8,128)(2,1)S(1)}, bf16[8192,64]{0,1:T(8,128)(2,1)}, u32[]{:S(2)}, u32[]{:S(2)}) collective-permute-start(bf16[8192,64]{0,1:T(8,128)(2,1)S(1)} %copy.36), channel_id=1, source_target_pairs={{120,0},{0,8},{8,16},{16,24},{24,32},{32,40},{40,48},{48,56},{56,6... | collective-permute-start | bytes 3145736 | tf_op jit(solution)/shard_map/while/body/eval_jaxpr/ppermute | solution.py:12
  323.0 17.9 %collective-permute-start = (bf16[8192,64]{0,1:T(8,128)(2,1)S(1)}, bf16[8192,64]{0,1:T(8,128)(2,1)}, u32[]{:S(2)}, u32[]{:S(2)}) collective-permute-start(bf16[8192,64]{0,1:T(8,128)(2,1)S(1)} %copy.36), channel_id=1, source_target_pairs={{120,0},{0,8},{8,16},{16,24},{24,32},{32,40},{40,48},{48,56},{56,6... | collective-permute-start | bytes 3145736 | tf_op jit(solution)/shard_map/while/body/eval_jaxpr/ppermute | solution.py:12
  343.4 5.2 copy-start.1
  363.1 1.2 copy-start.2
Sparse Core Ops, SparseCore 0:
  9.0 95.3 all-gather.4
  364.4 114.1 all-gather.2
where the time goes:
time: 533 us; the launch traced here: 527 us
  waiting for transfers between devices  286 us (54%)
  other arithmetic  88.4 us (17%)
  matrix products  56 us (11%)
  local copies, waits for them, and re-layouts  49.7 us (9%)
  blocking collectives  28.2 us (5%)
  between operations  13.5 us (3%)
  starting transfers between devices  5.36 us (1%)
    ppermute x15, waiting for transfers between devices, from_behind(): return lax.ppermute(block, axis, route)  177 us
    all_gather x1, waiting for transfers between devices, on_device(): mean_piece = lax.all_gather(mean_agg, 'bal', axis=1, tiled=True)  108 us
    scatter-add x16, other arithmetic, absorb(): return total.at[targets].add(masked)  75.5 us
    dot_general x16, matrix products, absorb(): jnp.einsum('sij,sjf->sif', vals, gathered, preferred_element_type=jnp.flo...  34.2 us
    all_to_all x1, blocking collectives, on_device(): lax.all_to_all(placed.astype(jnp.bfloat16).reshape(n_bal, capacity * TILE...  28.2 us
    another operation x15, local copies, waits for them, and re-layouts  18.4 us
    gather x16, local copies, waits for them, and re-layouts, absorb(): gathered = jnp.take(tiles, picks, axis=0)  11.8 us
    and x16, other arithmetic, absorb(): gathered = jnp.take(tiles, picks, axis=0)  11.2 us
  transfers between devices with their start and end apart: 17, of which 16 were waited for; matrix products, arithmetic and copies ran while one was open for 34% of the time, Pallas kernels for 0%

commit v1 on v0

v1 whole, which is shorter than its diff:
```python
import functools

import jax
import jax.numpy as jnp
from jax import lax
from jax.experimental import pallas as pl
from jax.experimental.pallas import tpu as pltpu
from jax.sharding import PartitionSpec as P

TILE = 128
CHUNKS = 1
ONES = 16
UNROLL = 8


def spot(position):
    return position // 8, (position // 2) % 4, position % 2


def route(block, dx, dy, dc):
    pairs = []
    for source in range(16):
        x, y, c = spot(source)
        pairs.append((source, ((x + dx) % 2) * 8 + ((y + dy) % 4) * 2 + (c + dc) % 2))
    return lax.ppermute(block, "blk", pairs)


def absorb(acc_ref, halves, source, counts, rows, cols, v_ref, with_ones):
    live = counts[source]
    dummy = acc_ref.shape[0] - 1

    def step(group, carry):
        found = []
        for u in range(UNROLL):
            slot = group * UNROLL + u
            start = pl.multiple_of(cols[source, slot] * TILE, TILE)
            parts = [ref[:, pl.ds(start, TILE)] for ref in halves]
            if with_ones:
                parts.append(jnp.ones((ONES, TILE), jnp.bfloat16))
            left = parts[0] if len(parts) == 1 else jnp.concatenate(parts, axis=0)
            prod = lax.dot_general(
                left, v_ref[slot], (((1,), (1,)), ((), ())), preferred_element_type=jnp.float32
            )
            found.append((jnp.where(slot < live, rows[source, slot], dummy), prod))
        for target, prod in found:
            acc_ref[target] += prod
        return carry

    lax.fori_loop(0, (live + UNROLL - 1) // UNROLL, step, 0)


def seat(here, dx, dy, dc):
    x, y, c = here // 8, (here // 2) % 4, here % 2
    return ((x + dx) % 2) * 8 + ((y + dy) % 4) * 2 + (c + dc) % 2


def gather_kernel(layout, offsets, first, with_ones, here, counts, rows, cols, v_hbm, *refs):
    n_blocks = sum(layout)
    n = len(layout)
    blocks = refs[:n_blocks]
    acc_ref, v_ref, v_sem, b_sem = refs[n_blocks + (0 if first else 1) :][:4]
    staged = refs[-n_blocks:]
    places = [seat(here[0], *offsets[i]) for i in range(n)]
    copies = []
    at = 0
    for i, width in enumerate(layout):
        mine = [pltpu.make_async_copy(v_hbm.at[places[i]], v_ref.at[i], v_sem.at[i])]
        for j in range(at, at + width):
            mine.append(pltpu.make_async_copy(blocks[j], staged[j], b_sem.at[j]))
        at += width
        copies.append(mine)
        for copy in mine:
            copy.start()
    if first:
        acc_ref[...] = jnp.zeros_like(acc_ref)
    else:
        acc_ref[...] = refs[n_blocks][...]
    at = 0
    for i, width in enumerate(layout):
        for copy in copies[i]:
            copy.wait()
        absorb(
            acc_ref, staged[at : at + width], places[i], counts, rows, cols, v_ref.at[i], with_ones
        )
        at += width


def accumulate(acc, groups, offsets, here, tables, values, height, tiles_per, with_ones):
    counts, rows, cols = tables
    layout = tuple(len(g) for g in groups)
    blocks = [b for g in groups for b in g]
    first = acc is None
    vmem = pl.BlockSpec(memory_space=pltpu.VMEM)
    smem = pl.BlockSpec(memory_space=pltpu.SMEM)
    anywhere = pl.BlockSpec(memory_space=pl.ANY)
    operands = [here.reshape(1), counts, rows, cols, values] + blocks
    specs = [smem] * 4 + [anywhere] * (1 + len(blocks))
    if not first:
        operands.append(acc)
        specs.append(vmem)
    return pl.pallas_call(
        functools.partial(gather_kernel, layout, tuple(offsets), first, with_ones),
        in_specs=specs,
        out_specs=vmem,
        out_shape=jax.ShapeDtypeStruct(
            (tiles_per + 1, height + (ONES if with_ones else 0), TILE), jnp.float32
        ),
        scratch_shapes=[
            pltpu.VMEM((len(groups),) + values.shape[1:], values.dtype),
            pltpu.SemaphoreType.DMA((len(groups),)),
            pltpu.SemaphoreType.DMA((len(blocks),)),
        ]
        + [pltpu.VMEM(b.shape, b.dtype) for b in blocks],
        name="aggregate",
    )(*operands)


def place_into(out_ref, mapping, used, tiles_per, tile_of):
    n_bal = out_ref.shape[0]
    out_ref[...] = jnp.zeros_like(out_ref)
    for d in range(n_bal):
        used[d] = 0

    def step(t, carry):
        d = mapping[0, t]
        k = used[d]
        used[d] = k + 1
        out_ref[d, :, pl.ds(pl.multiple_of(k * TILE, TILE), TILE)] = tile_of(t)
        return carry

    lax.fori_loop(0, tiles_per, step, 0)


def place_kernel(mapping, x_ref, out_ref, used):
    tiles_per = mapping.shape[1]
    place_into(
        out_ref, mapping, used, tiles_per,
        lambda t: x_ref[:, pl.ds(pl.multiple_of(t * TILE, TILE), TILE)],
    )


def place_features(block, mapping, n_bal, capacity):
    return pl.pallas_call(
        place_kernel,
        in_specs=[pl.BlockSpec(memory_space=pltpu.SMEM), pl.BlockSpec(memory_space=pltpu.VMEM)],
        out_specs=pl.BlockSpec(memory_space=pltpu.VMEM),
        out_shape=jax.ShapeDtypeStruct((n_bal, block.shape[0], capacity * TILE), block.dtype),
        scratch_shapes=[pltpu.SMEM((n_bal,), jnp.int32)],
        name="place_features",
    )(mapping, block)


def mean_kernel(height, mapping, acc_ref, deg_ref, out_ref, used):
    tiles_per = mapping.shape[1]

    def tile_of(t):
        inverse = 1.0 / (1.0 + deg_ref[t, 0:1, :])
        return (acc_ref[t, 0:height, :] * inverse).astype(jnp.bfloat16)

    place_into(out_ref, mapping, used, tiles_per, tile_of)


def place_means(acc, degree, height, mapping, n_bal, capacity):
    vmem = pl.BlockSpec(memory_space=pltpu.VMEM)
    return pl.pallas_call(
        functools.partial(mean_kernel, height),
        in_specs=[pl.BlockSpec(memory_space=pltpu.SMEM), vmem, vmem],
        out_specs=vmem,
        out_shape=jax.ShapeDtypeStruct((n_bal, height, capacity * TILE), jnp.bfloat16),
        scratch_shapes=[pltpu.SMEM((n_bal,), jnp.int32)],
        name="place_means",
    )(mapping, acc, degree)


def exchange(placed):
    got = lax.all_to_all(placed, "bal", split_axis=0, concat_axis=0, tiled=True)
    return got.reshape(got.shape[0] * got.shape[1], got.shape[2])


def across(left, right):
    return lax.dot_general(
        left, right, (((0,), (0,)), ((), ())), preferred_element_type=jnp.float32
    )


def on_device(
    features, tile_values, tile_rows, tile_cols, tile_counts, w_self, w_neigh, bias, part_map
):
    n_bal = lax.axis_size("bal")
    here = lax.axis_index("blk")
    column = lax.axis_index("bal")
    tiles_per = part_map.shape[1]
    capacity = 2 * tiles_per // n_bal
    width = features.shape[1]
    height = width // CHUNKS
    values = tile_values[0]
    tables = (tile_counts[0], tile_rows[0], tile_cols[0])
    flipped = features.T

    mine = exchange(place_features(flipped, part_map, n_bal, capacity))
    pre = across(mine, w_self)
    degree = None
    w_chunks = w_neigh.reshape(n_bal, CHUNKS, height, w_neigh.shape[1])
    for k in range(CHUNKS):
        own = flipped[k * height : (k + 1) * height]
        half = height // 2
        near = [own, route(own, 1, 0, 0)]
        stages = [[], [], []]
        for dx, block in enumerate(near):
            up = route(block, 0, 1, 0)
            down = route(block, 0, -1, 0)
            top = route(up[:half], 0, 1, 0)
            bottom = route(down[half:], 0, -1, 0)
            stages[0].append(((block,), (dx, 0)))
            stages[1].append(((up,), (dx, -1)))
            stages[1].append(((down,), (dx, 1)))
            stages[2].append(((top, bottom), (dx, 2)))
        acc = None
        with_ones = k == 0
        for stage in stages:
            groups, offsets = [], []
            for dc in range(2):
                for blocks, (dx, dy) in stage:
                    groups.append([b if dc == 0 else route(b, 0, 0, 1) for b in blocks])
                    offsets.append((dx, dy, dc))
            acc = accumulate(
                acc, groups, offsets, here, tables, values, height, tiles_per, with_ones
            )
        if degree is None:
            degree = acc[:, height : height + 8, :]
        means = exchange(place_means(acc, degree, height, part_map, n_bal, capacity))
        weight = w_chunks[:, k].reshape(n_bal * height, w_neigh.shape[1])
        pre = pre + across(means, weight)
    filled = jnp.sum((part_map[0] == column).astype(jnp.int32)) * TILE
    row = lax.broadcasted_iota(jnp.int32, (capacity * TILE, 1), 0)
    hidden = jnp.where(row < filled, jnp.maximum(pre + bias[None, :], 0.0), 0.0)
    return hidden.astype(jnp.bfloat16)[None, None]


def solution(mesh):
    placed = (
        P("blk", "bal"),
        P("blk", None, None, None, None),
        P("blk", None, None),
        P("blk", None, None),
        P("blk", None),
        P(),
        P(),
        P(),
        P("blk", None),
    )
    return jax.shard_map(
        on_device,
        mesh=mesh,
        in_specs=placed,
        out_specs=P("blk", "bal", None, None),
        check_vma=False,
    )
```

time: 533 us -> 167 us (0.31); the launches traced: 527 us -> 167 us
  waiting for transfers between devices: 286 us -> 69.7 us
  other arithmetic: 88.4 us -> 0.64 us
  matrix products: 56 us -> 8.89 us
  local copies, waits for them, and re-layouts: 49.7 us -> 5.84 us
  Pallas kernels: 0 us -> 38.3 us
  starting transfers between devices: 5.36 us -> 42.8 us
  blocking collectives: 28.2 us -> 0 us
  between operations: 13.5 us -> 0.79 us
    ppermute x15 -> x19, waiting for transfers between devices: 177 us -> 48.8 us  [route(): return lax.ppermute(block, 'blk', pairs)]
    all_gather x2 -> x0, waiting for transfers between devices: 108 us -> none  [the longest x1 108 us: on_device(): mean_piece = lax.all_gather(mean_agg, 'bal', axis=1, tiled=True)]
    scatter-add x16 -> x0, other arithmetic: 75.5 us -> none  [absorb(): return total.at[targets].add(masked)]
    dot_general x21 -> x2, matrix products: 56 us -> 8.89 us  [across(): lax.dot_general(left, right, (((0,), (0,)), ((), ())), preferred_element_...]
    pallas_call x0 -> x5, Pallas kernels: none -> 38.3 us  [the longest x3 30.7 us: accumulate(): pl.pallas_call(functools.partial(gather_kernel, layout, tuple(offsets), f...]
    all_to_all x1 -> x0, blocking collectives: 28.2 us -> none  [on_device(): lax.all_to_all(placed.astype(jnp.bfloat16).reshape(n_bal, capacity * TILE...]
    ppermute x15 -> x19, starting transfers between devices: 5.32 us -> 31.7 us  [route(): return lax.ppermute(block, 'blk', pairs)]
    all_to_all x0 -> x2, waiting for transfers between devices: none -> 20.9 us  [exchange(): got = lax.all_to_all(placed, 'bal', split_axis=0, concat_axis=0, tiled=True)]
  transfers between devices with their start and end apart: 17 -> 21, of which waited for: 16 -> 6; matrix products, arithmetic and copies ran while one was open for 34% -> 6% of each run, Pallas kernels for 0% -> 23%
where the time goes in v1:
time: 167 us
  waiting for transfers between devices  69.7 us (42%)
  starting transfers between devices  42.8 us (26%)
  Pallas kernels  38.3 us (23%)
  matrix products  8.89 us (5%)
  local copies, waits for them, and re-layouts  5.84 us (3%)
    ppermute x19, waiting for transfers between devices, route(): return lax.ppermute(block, 'blk', pairs)  48.8 us
    ppermute x19, starting transfers between devices, route(): return lax.ppermute(block, 'blk', pairs)  31.7 us
    pallas_call x3, Pallas kernels, accumulate(): pl.pallas_call(functools.partial(gather_kernel, layout, tuple(offsets), f...  30.7 us
    all_to_all x2, waiting for transfers between devices, exchange(): got = lax.all_to_all(placed, 'bal', split_axis=0, concat_axis=0, tiled=True)  20.9 us
    all_to_all x2, starting transfers between devices, exchange(): got = lax.all_to_all(placed, 'bal', split_axis=0, concat_axis=0, tiled=True)  11.2 us
    dot_general x2, matrix products, across(): lax.dot_general(left, right, (((0,), (0,)), ((), ())), preferred_element_...  8.89 us
    pallas_call x1, Pallas kernels, place_means(): pl.pallas_call(functools.partial(mean_kernel, height), in_specs=[pl.Block...  4.1 us
    pallas_call x1, Pallas kernels, place_features(): pl.pallas_call(place_kernel, in_specs=[pl.BlockSpec(memory_space=pltpu.SM...  3.43 us
  transfers between devices with their start and end apart: 21, of which 6 were waited for; matrix products, arithmetic and copies ran while one was open for 6% of the time, Pallas kernels for 23%

profile of v1, /device:TPU:1, one launch (start us, length us, event | category | flops | bytes accessed | tf_op | source)
XLA Modules:
  0.0 167.0 jit_solution(2929985360363499595)
XLA Ops:
  0.0 3.6 %collective-permute-start.4 = (bf16[64,8192]{1,0:T(8,128)(2,1)}, bf16[64,8192]{1,0:T(8,128)(2,1)}, u32[]{:S(2)}, u32[]{:S(2)}) collective-permute-start(bf16[64,8192]{1,0:T(8,128)(2,1)} %bitcast.18), channel_id=1, source_target_pairs={{0,64},{8,72},{16,80},{24,88},{32,96},{40,104},{48,112},{56,120},{... | collective-permute-start | bytes 3145736 | tf_op jit(solution)/shard_map/ppermute | solution.py:25
  3.6 2.7 %collective-permute-start.2 = (bf16[64,8192]{1,0:T(8,128)(2,1)}, bf16[64,8192]{1,0:T(8,128)(2,1)S(1)}, u32[]{:S(2)}, u32[]{:S(2)}) collective-permute-start(bf16[64,8192]{1,0:T(8,128)(2,1)} %bitcast.19), channel_id=1, source_target_pairs={{0,48},{8,56},{16,0},{24,8},{32,16},{40,24},{48,32},{56,40},{64,11... | collective-permute-start | bytes 3145736 | tf_op jit(solution)/shard_map/ppermute | solution.py:25
  7.6 18.7 %collective-permute-done.4.refs_1_ = bf16[64,8192]{1,0:T(8,128)(2,1)} collective-permute-done((bf16[64,8192]{1,0:T(8,128)(2,1)}, bf16[64,8192]{1,0:T(8,128)(2,1)}, u32[]{:S(2)}, u32[]{:S(2)}) %collective-permute-start.4) | collective-permute-done | bytes 1048608 | tf_op jit(solution)/shard_map/ppermute | solution.py:25
  26.3 1.7 %collective-permute-start.5 = (bf16[64,8192]{1,0:T(8,128)(2,1)}, bf16[64,8192]{1,0:T(8,128)(2,1)}, u32[]{:S(2)}, u32[]{:S(2)}) collective-permute-start(bf16[64,8192]{1,0:T(8,128)(2,1)} %collective-permute-done.4.refs_1_), channel_id=1, source_target_pairs={{0,16},{8,24},{16,32},{24,40},{32,48},{40,56},{48,0},{56,8},{64,80... | collective-permute-start | bytes 3145736 | tf_op jit(solution)/shard_map/ppermute | solution.py:25
  30.3 2.0 %collective-permute-start.3 = (bf16[32,8192]{1,0:T(8,128)(2,1)}, bf16[32,8192]{1,0:T(8,128)(2,1)S(1)}, u32[]{:S(2)}, u32[]{:S(2)}) collective-permute-start(bf16[32,8192]{1,0:T(8,128)(2,1)} %slice.21), channel_id=1, source_target_pairs={{0,48},{8,56},{16,0},{24,8},{32,16},{40,24},{48,32},{56,40},{64,11... | collective-permute-start | bytes 1572872 | tf_op jit(solution)/shard_map/ppermute | solution.py:25
  32.4 2.1 %collective-permute-start.18 = (bf16[64,8192]{1,0:T(8,128)(2,1)}, bf16[64,8192]{1,0:T(8,128)(2,1)}, u32[]{:S(2)}, u32[]{:S(2)}) collective-permute-start(bf16[64,8192]{1,0:T(8,128)(2,1)} %collective-permute-done.4.refs_1_), channel_id=1, source_target_pairs={{0,8},{8,0},{16,24},{24,16},{32,40},{40,32},{48,56},{56,48},{64,72... | collective-permute-start | bytes 3145736 | tf_op jit(solution)/shard_map/ppermute | solution.py:25
  35.0 3.4 %place_features.1 = bf16[8,64,2048]{2,1,0:T(8,128)(2,1)} custom-call(s32[1,64]{1,0:T(1,128)} %mapping.3, bf16[64,8192]{1,0:T(8,128)(2,1)} %bitcast.22), custom_call_target="tpu_custom_call" | custom-call | tf_op jit(solution)/shard_map/place_features/pallas_call | solution.py:143
  38.5 5.2 %all-to-all-start = ((bf16[8,64,2048]{2,1,0:T(8,128)(2,1)}), bf16[8,64,2048]{2,1,0:T(8,128)(2,1)S(1)}, u32[]{:S(2)}, u32[]{:S(2)}) async-start(bf16[8,64,2048]{2,1,0:T(8,128)(2,1)} %place_features.1), calls=%async_computation | async-start | bytes 4194304 | tf_op jit(solution)/shard_map/all_to_all | solution.py:176
  44.8 17.5 %collective-permute-done.3.refs_1_ = bf16[32,8192]{1,0:T(8,128)(2,1)S(1)} collective-permute-done((bf16[32,8192]{1,0:T(8,128)(2,1)}, bf16[32,8192]{1,0:T(8,128)(2,1)S(1)}, u32[]{:S(2)}, u32[]{:S(2)}) %collective-permute-start.3) | collective-permute-done | bytes 524320 | tf_op jit(solution)/shard_map/ppermute | solution.py:25
  63.6 3.0 %collective-permute-start.14 = (bf16[64,8192]{1,0:T(8,128)(2,1)}, bf16[64,8192]{1,0:T(8,128)(2,1)}, u32[]{:S(2)}, u32[]{:S(2)}) collective-permute-start(bf16[64,8192]{1,0:T(8,128)(2,1)} %copy-done.1), channel_id=1, source_target_pairs={{0,8},{8,0},{16,24},{24,16},{32,40},{40,32},{48,56},{56,48},{64,72... | collective-permute-start | bytes 3145736 | tf_op jit(solution)/shard_map/ppermute | solution.py:25
  68.8 5.9 %collective-permute-done.1.refs_0_ = bf16[32,8192]{1,0:T(8,128)(2,1)} collective-permute-done((bf16[32,8192]{1,0:T(8,128)(2,1)S(1)}, bf16[32,8192]{1,0:T(8,128)(2,1)}, u32[]{:S(2)}, u32[]{:S(2)}) %collective-permute-start.1) | collective-permute-done | bytes 524320 | tf_op jit(solution)/shard_map/ppermute | solution.py:25
  74.8 3.5 %collective-permute-start.16 = (bf16[64,8192]{1,0:T(8,128)(2,1)}, bf16[64,8192]{1,0:T(8,128)(2,1)}, u32[]{:S(2)}, u32[]{:S(2)}) collective-permute-start(bf16[64,8192]{1,0:T(8,128)(2,1)} %collective-permute-done.7.refs_3_), channel_id=1, source_target_pairs={{0,8},{8,0},{16,24},{24,16},{32,40},{40,32},{48,56},{56,48},{64,72... | collective-permute-start | bytes 3145736 | tf_op jit(solution)/shard_map/ppermute | solution.py:25
  78.3 2.8 %collective-permute-start.8 = (bf16[32,8192]{1,0:T(8,128)(2,1)S(1)}, bf16[32,8192]{1,0:T(8,128)(2,1)}, u32[]{:S(2)}, u32[]{:S(2)}) collective-permute-start(bf16[32,8192]{1,0:T(8,128)(2,1)S(1)} %slice.23), channel_id=1, source_target_pairs={{0,48},{8,56},{16,0},{24,8},{32,16},{40,24},{48,32},{56,40},{64,11... | collective-permute-start | bytes 1572872 | tf_op jit(solution)/shard_map/ppermute | solution.py:25
  81.5 4.6 %collective-permute-done.6.refs_2_ = bf16[32,8192]{1,0:T(8,128)(2,1)} collective-permute-done((bf16[32,8192]{1,0:T(8,128)(2,1)S(1)}, bf16[32,8192]{1,0:T(8,128)(2,1)}, u32[]{:S(2)}, u32[]{:S(2)}) %collective-permute-start.6) | collective-permute-done | bytes 524320 | tf_op jit(solution)/shard_map/ppermute | solution.py:25
  86.1 4.3 %collective-permute-start.9 = (bf16[32,8192]{1,0:T(8,128)(2,1)}, bf16[32,8192]{1,0:T(8,128)(2,1)}, u32[]{:S(2)}, u32[]{:S(2)}) collective-permute-start(bf16[32,8192]{1,0:T(8,128)(2,1)} %collective-permute-done.1.refs_0_), channel_id=1, source_target_pairs={{0,8},{8,0},{16,24},{24,16},{32,40},{40,32},{48,56},{56,48},{64,72... | collective-permute-start | bytes 1572872 | tf_op jit(solution)/shard_map/ppermute | solution.py:25
  90.4 2.0 %collective-permute-done.8.refs_3_ = bf16[32,8192]{1,0:T(8,128)(2,1)} collective-permute-done((bf16[32,8192]{1,0:T(8,128)(2,1)S(1)}, bf16[32,8192]{1,0:T(8,128)(2,1)}, u32[]{:S(2)}, u32[]{:S(2)}) %collective-permute-start.8) | collective-permute-done | bytes 524320 | tf_op jit(solution)/shard_map/ppermute | solution.py:25
  93.3 8.2 %aggregate.3.refs_8_ = f32[65,80,128]{2,1,0:T(8,128)} custom-call(s32[1]{0:T(128)} %bitcast.2.here, s32[16]{0:T(128)} %bitcast.30, s32[16,32]{1,0:T(8,128)} %bitcast.24, s32[16,32]{1,0:T(8,128)} %bitcast.27, bf16[16,32,128,128]{3,2,1,0:T(8,128)(2,1)} %bitcast.14, bf16[64,8192]{1,0:T(8,128)(2,1)} %bitcast.23, ...), custom_call_target="tpu_custom_call" | custom-call | tf_op jit(solution)/shard_map/aggregate/pallas_call | solution.py:101
  101.5 13.2 %aggregate.4.refs_8_ = f32[65,80,128]{2,1,0:T(8,128)} custom-call(s32[1]{0:T(128)} %bitcast.2.here, s32[16]{0:T(128)} %bitcast.31, s32[16,32]{1,0:T(8,128)} %bitcast.25, s32[16,32]{1,0:T(8,128)} %bitcast.28, bf16[16,32,128,128]{3,2,1,0:T(8,128)(2,1)} %bitcast.15, bf16[64,8192]{1,0:T(8,128)(2,1)} %collective-permute-done.refs_0_, bf16[64,8192]{1,0:T(8,128)(2,1)} %copy-done.1, ...), custom_call_target="tpu_custom_call" | custom-call | tf_op jit(solution)/shard_map/aggregate/pallas_call | solution.py:101
  114.7 9.4 %aggregate.5.acc_ref = f32[65,80,128]{2,1,0:T(8,128)} custom-call(s32[1]{0:T(128)} %bitcast.2.here, s32[16]{0:T(128)} %bitcast.32, s32[16,32]{1,0:T(8,128)} %bitcast.26, s32[16,32]{1,0:T(8,128)} %bitcast.29, bf16[16,32,128,128]{3,2,1,0:T(8,128)(2,1)} %bitcast.16, bf16[32,8192]{1,0:T(8,128)(2,1)} %collective-permute-done.1.refs_0_, ...), custom_call_target="tpu_custom_call" | custom-call | tf_op jit(solution)/shard_map/aggregate/pallas_call | solution.py:101
  125.8 4.1 %place_means.1 = bf16[8,64,2048]{2,1,0:T(8,128)(2,1)} custom-call(s32[1,64]{1,0:T(1,128)} %mapping.3, f32[65,80,128]{2,1,0:T(8,128)} %aggregate.5.acc_ref, f32[65,8,128]{2,1,0:T(8,128)} %slice.24.deg_ref), custom_call_target="tpu_custom_call" | custom-call | tf_op jit(solution)/shard_map/place_means/pallas_call | solution.py:165
  129.9 5.9 %all-to-all-start.1 = ((bf16[8,64,2048]{2,1,0:T(8,128)(2,1)}), bf16[8,64,2048]{2,1,0:T(8,128)(2,1)}, u32[]{:S(2)}, u32[]{:S(2)}) async-start(bf16[8,64,2048]{2,1,0:T(8,128)(2,1)} %place_means.1), calls=%async_computation.1 | async-start | bytes 4194304 | tf_op jit(solution)/shard_map/all_to_all | solution.py:176
  137.2 3.2 %fusion.2 = f32[2048,512]{1,0:T(8,128)} fusion(bf16[512,2048]{1,0:T(8,128)(2,1)S(1)} %bitcast.17, bf16[512,512]{1,0:T(8,128)(2,1)S(1)} %copy-done), kind=kOutput, calls=%fused_computation.5 | convolution fusion | flops 1073741824 | bytes 6815744 | tf_op jit(solution)/shard_map/dot_general | solution.py:181
  140.4 20.9 %all-to-all-done.1 = bf16[8,64,2048]{2,1,0:T(8,128)(2,1)} async-done(((bf16[8,64,2048]{2,1,0:T(8,128)(2,1)}), bf16[8,64,2048]{2,1,0:T(8,128)(2,1)}, u32[]{:S(2)}, u32[]{:S(2)}) %all-to-all-start.1) | async-done | bytes 2097184 | tf_op jit(solution)/shard_map/all_to_all | solution.py:176
  161.3 5.6 %fusion = bf16[1,1,2048,512]{3,2,1,0:T(8,128)(2,1)} fusion(f32[2048,512]{1,0:T(8,128)} %fusion.2, bf16[512,2048]{1,0:T(8,128)(2,1)} %bitcast.7, bf16[512,512]{1,0:T(8,128)(2,1)S(1)} %copy-done.5, f32[512]{0:T(512)S(1)} %copy-done.6, pred[2048]{0:T(1024)(128)(4,1)S(1)} %iota_compare_fusion), kind=kOutput, calls=%fused_computation.1 | convolution fusion | flops 1078984704 | bytes 8916992 | tf_op jit(solution)/shard_map/dot_general | solution.py:181
  (46 shorter events, 12.3 us)
Async XLA Ops:
  0.0 137.1 %copy-start = (bf16[512,512]{1,0:T(8,128)(2,1)S(1)}, bf16[512,512]{1,0:T(8,128)(2,1)}, u32[]{:S(2)}) copy-start(bf16[512,512]{1,0:T(8,128)(2,1)} %param.14) | copy-start | bytes 1572868
  0.0 26.3 %collective-permute-start.4 = (bf16[64,8192]{1,0:T(8,128)(2,1)}, bf16[64,8192]{1,0:T(8,128)(2,1)}, u32[]{:S(2)}, u32[]{:S(2)}) collective-permute-start(bf16[64,8192]{1,0:T(8,128)(2,1)} %bitcast.18), channel_id=1, source_target_pairs={{0,64},{8,72},{16,80},{24,88},{32,96},{40,104},{48,112},{56,120},{... | collective-permute-start | bytes 3145736 | tf_op jit(solution)/shard_map/ppermute | solution.py:25
  3.6 25.8 %collective-permute-start.2 = (bf16[64,8192]{1,0:T(8,128)(2,1)}, bf16[64,8192]{1,0:T(8,128)(2,1)S(1)}, u32[]{:S(2)}, u32[]{:S(2)}) collective-permute-start(bf16[64,8192]{1,0:T(8,128)(2,1)} %bitcast.19), channel_id=1, source_target_pairs={{0,48},{8,56},{16,0},{24,8},{32,16},{40,24},{48,32},{56,40},{64,11... | collective-permute-start | bytes 3145736 | tf_op jit(solution)/shard_map/ppermute | solution.py:25
  6.3 26.1 %collective-permute-start.17 = (bf16[64,8192]{1,0:T(8,128)(2,1)}, bf16[64,8192]{1,0:T(8,128)(2,1)S(1)}, u32[]{:S(2)}, u32[]{:S(2)}) collective-permute-start(bf16[64,8192]{1,0:T(8,128)(2,1)} %bitcast.20), channel_id=1, source_target_pairs={{0,8},{8,0},{16,24},{24,16},{32,40},{40,32},{48,56},{56,48},{64,72... | collective-permute-start | bytes 3145736 | tf_op jit(solution)/shard_map/ppermute | solution.py:25
  7.5 27.0 %collective-permute-start = (bf16[64,8192]{1,0:T(8,128)(2,1)}, bf16[64,8192]{1,0:T(8,128)(2,1)}, u32[]{:S(2)}, u32[]{:S(2)}) collective-permute-start(bf16[64,8192]{1,0:T(8,128)(2,1)} %bitcast.21), channel_id=1, source_target_pairs={{0,16},{8,24},{16,32},{24,40},{32,48},{40,56},{48,0},{56,8},{64,80... | collective-permute-start | bytes 3145736 | tf_op jit(solution)/shard_map/ppermute | solution.py:25
  26.3 37.3 %collective-permute-start.5 = (bf16[64,8192]{1,0:T(8,128)(2,1)}, bf16[64,8192]{1,0:T(8,128)(2,1)}, u32[]{:S(2)}, u32[]{:S(2)}) collective-permute-start(bf16[64,8192]{1,0:T(8,128)(2,1)} %collective-permute-done.4.refs_1_), channel_id=1, source_target_pairs={{0,16},{8,24},{16,32},{24,40},{32,48},{40,56},{48,0},{56,8},{64,80... | collective-permute-start | bytes 3145736 | tf_op jit(solution)/shard_map/ppermute | solution.py:25
  28.0 38.6 %collective-permute-start.7 = (bf16[64,8192]{1,0:T(8,128)(2,1)}, bf16[64,8192]{1,0:T(8,128)(2,1)}, u32[]{:S(2)}, u32[]{:S(2)}) collective-permute-start(bf16[64,8192]{1,0:T(8,128)(2,1)} %collective-permute-done.4.refs_1_), channel_id=1, source_target_pairs={{0,48},{8,56},{16,0},{24,8},{32,16},{40,24},{48,32},{56,40},{64,11... | collective-permute-start | bytes 3145736 | tf_op jit(solution)/shard_map/ppermute | solution.py:25
  30.3 31.9 %collective-permute-start.3 = (bf16[32,8192]{1,0:T(8,128)(2,1)}, bf16[32,8192]{1,0:T(8,128)(2,1)S(1)}, u32[]{:S(2)}, u32[]{:S(2)}) collective-permute-start(bf16[32,8192]{1,0:T(8,128)(2,1)} %slice.21), channel_id=1, source_target_pairs={{0,48},{8,56},{16,0},{24,8},{32,16},{40,24},{48,32},{56,40},{64,11... | collective-permute-start | bytes 1572872 | tf_op jit(solution)/shard_map/ppermute | solution.py:25
  32.4 42.4 %collective-permute-start.18 = (bf16[64,8192]{1,0:T(8,128)(2,1)}, bf16[64,8192]{1,0:T(8,128)(2,1)}, u32[]{:S(2)}, u32[]{:S(2)}) collective-permute-start(bf16[64,8192]{1,0:T(8,128)(2,1)} %collective-permute-done.4.refs_1_), channel_id=1, source_target_pairs={{0,8},{8,0},{16,24},{24,16},{32,40},{40,32},{48,56},{56,48},{64,72... | collective-permute-start | bytes 3145736 | tf_op jit(solution)/shard_map/ppermute | solution.py:25
  34.5 43.8 %collective-permute-start.13 = (bf16[64,8192]{1,0:T(8,128)(2,1)}, bf16[64,8192]{1,0:T(8,128)(2,1)}, u32[]{:S(2)}, u32[]{:S(2)}) collective-permute-start(bf16[64,8192]{1,0:T(8,128)(2,1)} %collective-permute-done.refs_0_), channel_id=1, source_target_pairs={{0,8},{8,0},{16,24},{24,16},{32,40},{40,32},{48,56},{56,48},{64,72... | collective-permute-start | bytes 3145736 | tf_op jit(solution)/shard_map/ppermute | solution.py:25
  38.5 91.4 %all-to-all-start = ((bf16[8,64,2048]{2,1,0:T(8,128)(2,1)}), bf16[8,64,2048]{2,1,0:T(8,128)(2,1)S(1)}, u32[]{:S(2)}, u32[]{:S(2)}) async-start(bf16[8,64,2048]{2,1,0:T(8,128)(2,1)} %place_features.1), calls=%async_computation | async-start | bytes 4194304 | tf_op jit(solution)/shard_map/all_to_all | solution.py:176
  62.2 39.2 %copy-start.3 = (bf16[32,8192]{1,0:T(8,128)(2,1)}, bf16[32,8192]{1,0:T(8,128)(2,1)S(1)}, u32[]{:S(2)}) copy-start(bf16[32,8192]{1,0:T(8,128)(2,1)S(1)} %collective-permute-done.3.refs_1_) | copy-start | bytes 1572868
  62.3 12.5 %collective-permute-start.1 = (bf16[32,8192]{1,0:T(8,128)(2,1)S(1)}, bf16[32,8192]{1,0:T(8,128)(2,1)}, u32[]{:S(2)}, u32[]{:S(2)}) collective-permute-start(bf16[32,8192]{1,0:T(8,128)(2,1)S(1)} %slice.20), channel_id=1, source_target_pairs={{0,16},{8,24},{16,32},{24,40},{32,48},{40,56},{48,0},{56,8},{64,80... | collective-permute-start | bytes 1572872 | tf_op jit(solution)/shard_map/ppermute | solution.py:25
  63.6 17.6 %collective-permute-start.14 = (bf16[64,8192]{1,0:T(8,128)(2,1)}, bf16[64,8192]{1,0:T(8,128)(2,1)}, u32[]{:S(2)}, u32[]{:S(2)}) collective-permute-start(bf16[64,8192]{1,0:T(8,128)(2,1)} %copy-done.1), channel_id=1, source_target_pairs={{0,8},{8,0},{16,24},{24,16},{32,40},{40,32},{48,56},{56,48},{64,72... | collective-permute-start | bytes 3145736 | tf_op jit(solution)/shard_map/ppermute | solution.py:25
  66.6 26.7 %collective-permute-start.15 = (bf16[64,8192]{1,0:T(8,128)(2,1)}, bf16[64,8192]{1,0:T(8,128)(2,1)}, u32[]{:S(2)}, u32[]{:S(2)}) collective-permute-start(bf16[64,8192]{1,0:T(8,128)(2,1)} %collective-permute-done.5.refs_2_), channel_id=1, source_target_pairs={{0,8},{8,0},{16,24},{24,16},{32,40},{40,32},{48,56},{56,48},{64,72... | collective-permute-start | bytes 3145736 | tf_op jit(solution)/shard_map/ppermute | solution.py:25
  74.8 11.3 %collective-permute-start.6 = (bf16[32,8192]{1,0:T(8,128)(2,1)S(1)}, bf16[32,8192]{1,0:T(8,128)(2,1)}, u32[]{:S(2)}, u32[]{:S(2)}) collective-permute-start(bf16[32,8192]{1,0:T(8,128)(2,1)S(1)} %slice.22), channel_id=1, source_target_pairs={{0,16},{8,24},{16,32},{24,40},{32,48},{40,56},{48,0},{56,8},{64,80... | collective-permute-start | bytes 1572872 | tf_op jit(solution)/shard_map/ppermute | solution.py:25
  74.8 26.7 %collective-permute-start.16 = (bf16[64,8192]{1,0:T(8,128)(2,1)}, bf16[64,8192]{1,0:T(8,128)(2,1)}, u32[]{:S(2)}, u32[]{:S(2)}) collective-permute-start(bf16[64,8192]{1,0:T(8,128)(2,1)} %collective-permute-done.7.refs_3_), channel_id=1, source_target_pairs={{0,8},{8,0},{16,24},{24,16},{32,40},{40,32},{48,56},{56,48},{64,72... | collective-permute-start | bytes 3145736 | tf_op jit(solution)/shard_map/ppermute | solution.py:25
  78.3 14.1 %collective-permute-start.8 = (bf16[32,8192]{1,0:T(8,128)(2,1)S(1)}, bf16[32,8192]{1,0:T(8,128)(2,1)}, u32[]{:S(2)}, u32[]{:S(2)}) collective-permute-start(bf16[32,8192]{1,0:T(8,128)(2,1)S(1)} %slice.23), channel_id=1, source_target_pairs={{0,48},{8,56},{16,0},{24,8},{32,16},{40,24},{48,32},{56,40},{64,11... | collective-permute-start | bytes 1572872 | tf_op jit(solution)/shard_map/ppermute | solution.py:25
  81.1 33.5 %collective-permute-start.10 = (bf16[32,8192]{1,0:T(8,128)(2,1)S(1)}, bf16[32,8192]{1,0:T(8,128)(2,1)}, u32[]{:S(2)}, u32[]{:S(2)}) collective-permute-start(bf16[32,8192]{1,0:T(8,128)(2,1)S(1)} %collective-permute-done.3.refs_1_), channel_id=1, source_target_pairs={{0,8},{8,0},{16,24},{24,16},{32,40},{40,32},{48,56},{56,48},{64,72... | collective-permute-start | bytes 1572872 | tf_op jit(solution)/shard_map/ppermute | solution.py:25
  86.1 28.6 %collective-permute-start.9 = (bf16[32,8192]{1,0:T(8,128)(2,1)}, bf16[32,8192]{1,0:T(8,128)(2,1)}, u32[]{:S(2)}, u32[]{:S(2)}) collective-permute-start(bf16[32,8192]{1,0:T(8,128)(2,1)} %collective-permute-done.1.refs_0_), channel_id=1, source_target_pairs={{0,8},{8,0},{16,24},{24,16},{32,40},{40,32},{48,56},{56,48},{64,72... | collective-permute-start | bytes 1572872 | tf_op jit(solution)/shard_map/ppermute | solution.py:25
  92.4 22.3 %collective-permute-start.11 = (bf16[32,8192]{1,0:T(8,128)(2,1)}, bf16[32,8192]{1,0:T(8,128)(2,1)}, u32[]{:S(2)}, u32[]{:S(2)}) collective-permute-start(bf16[32,8192]{1,0:T(8,128)(2,1)} %collective-permute-done.6.refs_2_), channel_id=1, source_target_pairs={{0,8},{8,0},{16,24},{24,16},{32,40},{40,32},{48,56},{56,48},{64,72... | collective-permute-start | bytes 1572872 | tf_op jit(solution)/shard_map/ppermute | solution.py:25
  93.3 21.4 %collective-permute-start.12 = (bf16[32,8192]{1,0:T(8,128)(2,1)}, bf16[32,8192]{1,0:T(8,128)(2,1)}, u32[]{:S(2)}, u32[]{:S(2)}) collective-permute-start(bf16[32,8192]{1,0:T(8,128)(2,1)} %collective-permute-done.8.refs_3_), channel_id=1, source_target_pairs={{0,8},{8,0},{16,24},{24,16},{32,40},{40,32},{48,56},{56,48},{64,72... | collective-permute-start | bytes 1572872 | tf_op jit(solution)/shard_map/ppermute | solution.py:25
  129.9 31.4 %all-to-all-start.1 = ((bf16[8,64,2048]{2,1,0:T(8,128)(2,1)}), bf16[8,64,2048]{2,1,0:T(8,128)(2,1)}, u32[]{:S(2)}, u32[]{:S(2)}) async-start(bf16[8,64,2048]{2,1,0:T(8,128)(2,1)} %place_means.1), calls=%async_computation.1 | async-start | bytes 4194304 | tf_op jit(solution)/shard_map/all_to_all | solution.py:176
  137.1 24.2 %copy-start.5 = (bf16[512,512]{1,0:T(8,128)(2,1)S(1)}, bf16[512,512]{1,0:T(8,128)(2,1)}, u32[]{:S(2)}) copy-start(bf16[512,512]{1,0:T(8,128)(2,1)} %param.15) | copy-start | bytes 1572868
  (4 other events, 45.2 us)

commit v2 on v1

v2 whole, which is shorter than its diff:
```python
import functools

import jax
import jax.numpy as jnp
from jax import lax
from jax.experimental import pallas as pl
from jax.experimental.pallas import tpu as pltpu
from jax.sharding import PartitionSpec as P

TILE = 128
ONES = 16
UNROLL = 8


def spot(position):
    return position // 8, (position // 2) % 4, position % 2


def route(block, dx, dy, dc):
    pairs = []
    for source in range(16):
        x, y, c = spot(source)
        pairs.append((source, ((x + dx) % 2) * 8 + ((y + dy) % 4) * 2 + (c + dc) % 2))
    return lax.ppermute(block, "blk", pairs)


def absorb(acc_ref, halves, source, counts, rows, cols, v_ref, with_ones):
    live = counts[source]
    dummy = acc_ref.shape[0] - 1

    def step(group, carry):
        found = []
        for u in range(UNROLL):
            slot = group * UNROLL + u
            start = pl.multiple_of(cols[source, slot] * TILE, TILE)
            parts = [ref[:, pl.ds(start, TILE)] for ref in halves]
            if with_ones:
                parts.append(jnp.ones((ONES, TILE), jnp.bfloat16))
            left = parts[0] if len(parts) == 1 else jnp.concatenate(parts, axis=0)
            prod = lax.dot_general(
                left, v_ref[slot], (((1,), (1,)), ((), ())), preferred_element_type=jnp.float32
            )
            found.append((jnp.where(slot < live, rows[source, slot], dummy), prod))
        for target, prod in found:
            acc_ref[target] += prod
        return carry

    lax.fori_loop(0, (live + UNROLL - 1) // UNROLL, step, 0)


def seat(here, dx, dy, dc):
    x, y, c = here // 8, (here // 2) % 4, here % 2
    return ((x + dx) % 2) * 8 + ((y + dy) % 4) * 2 + (c + dc) % 2


def gather_kernel(layout, offsets, height, first, last, here, counts, rows, cols, *refs):
    refs = list(refs)
    mapping = refs.pop(0) if last else None
    v_hbm = refs.pop(0)
    n_blocks = sum(layout)
    n = len(layout)
    blocks = [refs.pop(0) for i in range(n_blocks)]
    acc_in = None if first else refs.pop(0)
    out_ref = refs.pop(0)
    v_ref, v_sem, b_sem = refs.pop(0), refs.pop(0), refs.pop(0)
    staged = [refs.pop(0) for i in range(n_blocks)]
    if last:
        acc_ref, a_sem, used = refs
    else:
        acc_ref = out_ref
        (a_sem,) = refs
    places = [seat(here[0], *offsets[i]) for i in range(n)]
    loads = []
    if not first:
        if last:
            at = (last - 1) * height
            pieces = [(at, 0, height), (acc_in.shape[1] - ONES, height, ONES)]
        else:
            pieces = [(0, 0, acc_in.shape[1])]
        for k, (src, dst, size) in enumerate(pieces):
            loads.append(
                pltpu.make_async_copy(
                    acc_in.at[:, pl.ds(src, size), :], acc_ref.at[:, pl.ds(dst, size), :], a_sem.at[k]
                )
            )
    for copy in loads:
        copy.start()
    copies = []
    at = 0
    for i, width in enumerate(layout):
        mine = [pltpu.make_async_copy(v_hbm.at[places[i]], v_ref.at[i], v_sem.at[i])]
        for j in range(at, at + width):
            mine.append(pltpu.make_async_copy(blocks[j], staged[j], b_sem.at[j]))
        at += width
        copies.append(mine)
        for copy in mine:
            copy.start()
    if first:
        acc_ref[...] = jnp.zeros_like(acc_ref)
    if last:
        out_ref[...] = jnp.zeros_like(out_ref)
    for copy in loads:
        copy.wait()
    at = 0
    for i, width in enumerate(layout):
        for copy in copies[i]:
            copy.wait()
        absorb(acc_ref, staged[at : at + width], places[i], counts, rows, cols, v_ref.at[i], True)
        at += width
    if last:

        def tile_of(t):
            inverse = 1.0 / (1.0 + acc_ref[t, height : height + 1, :])
            return (acc_ref[t, 0:height, :] * inverse).astype(jnp.bfloat16)

        place_into(out_ref, mapping, used, mapping.shape[1], tile_of)


def accumulate(acc, groups, offsets, here, tables, values, tiles_per, last=0, mapping=None, out=None):
    counts, rows, cols = tables
    layout = tuple(len(g) for g in groups)
    blocks = [b for g in groups for b in g]
    height = sum(b.shape[0] for b in groups[0])
    first = acc is None
    vmem = pl.BlockSpec(memory_space=pltpu.VMEM)
    smem = pl.BlockSpec(memory_space=pltpu.SMEM)
    anywhere = pl.BlockSpec(memory_space=pl.ANY)
    operands = [here.reshape(1), counts, rows, cols]
    if last:
        operands.append(mapping)
    specs = [smem] * len(operands) + [anywhere] * (1 + len(blocks))
    operands += [values] + blocks
    if not first:
        operands.append(acc)
        specs.append(anywhere)
    shape = (tiles_per + 1, height + ONES, TILE)
    scratch = [
        pltpu.VMEM((len(groups),) + values.shape[1:], values.dtype),
        pltpu.SemaphoreType.DMA((len(groups),)),
        pltpu.SemaphoreType.DMA((len(blocks),)),
    ] + [pltpu.VMEM(b.shape, b.dtype) for b in blocks]
    if last:
        scratch.append(pltpu.VMEM(shape, jnp.float32))
    scratch.append(pltpu.SemaphoreType.DMA((2,)))
    if last:
        scratch.append(pltpu.SMEM((out[0],), jnp.int32))
        result = jax.ShapeDtypeStruct((out[0], height, out[1]), jnp.bfloat16)
    else:
        result = jax.ShapeDtypeStruct(shape, jnp.float32)
    return pl.pallas_call(
        functools.partial(gather_kernel, layout, tuple(offsets), height, first, last),
        in_specs=specs,
        out_specs=vmem,
        out_shape=result,
        scratch_shapes=scratch,
        name="aggregate_last" if last else "aggregate",
    )(*operands)


def place_into(out_ref, mapping, used, tiles_per, tile_of):
    n_bal = out_ref.shape[0]
    out_ref[...] = jnp.zeros_like(out_ref)
    for d in range(n_bal):
        used[d] = 0

    def step(t, carry):
        d = mapping[0, t]
        k = used[d]
        used[d] = k + 1
        out_ref[d, :, pl.ds(pl.multiple_of(k * TILE, TILE), TILE)] = tile_of(t)
        return carry

    lax.fori_loop(0, tiles_per, step, 0)


def place_kernel(mapping, x_ref, out_ref, used):
    tiles_per = mapping.shape[1]
    place_into(
        out_ref, mapping, used, tiles_per,
        lambda t: x_ref[:, pl.ds(pl.multiple_of(t * TILE, TILE), TILE)],
    )


def place_features(block, mapping, n_bal, capacity):
    return pl.pallas_call(
        place_kernel,
        in_specs=[pl.BlockSpec(memory_space=pltpu.SMEM), pl.BlockSpec(memory_space=pltpu.VMEM)],
        out_specs=pl.BlockSpec(memory_space=pltpu.VMEM),
        out_shape=jax.ShapeDtypeStruct((n_bal, block.shape[0], capacity * TILE), block.dtype),
        scratch_shapes=[pltpu.SMEM((n_bal,), jnp.int32)],
        name="place_features",
    )(mapping, block)


def exchange(placed):
    got = lax.all_to_all(placed, "bal", split_axis=0, concat_axis=0, tiled=True)
    return got.reshape(got.shape[0] * got.shape[1], got.shape[2])


def across(left, right):
    return lax.dot_general(
        left, right, (((0,), (0,)), ((), ())), preferred_element_type=jnp.float32
    )


def on_device(
    features, tile_values, tile_rows, tile_cols, tile_counts, w_self, w_neigh, bias, part_map
):
    n_bal = lax.axis_size("bal")
    here = lax.axis_index("blk")
    column = lax.axis_index("bal")
    tiles_per = part_map.shape[1]
    capacity = 2 * tiles_per // n_bal
    width = features.shape[1]
    half = width // 2
    values = tile_values[0]
    tables = (tile_counts[0], tile_rows[0], tile_cols[0])
    own = features.T
    placing = (n_bal, capacity * TILE)

    def gathered(acc, pieces, **extra):
        groups, offsets = [], []
        for dc in range(2):
            for blocks, twins, (dx, dy) in pieces:
                groups.append(list(blocks if dc == 0 else twins))
                offsets.append((dx, dy, dc))
        return accumulate(acc, groups, offsets, here, tables, values, tiles_per, **extra)

    def twin(*blocks):
        return [route(b, 0, 0, 1) for b in blocks]

    side = route(own, 1, 0, 0)
    up = route(own, 0, 1, 0)
    down = route(own, 0, -1, 0)
    own_twin = twin(own)
    mine = exchange(place_features(own, part_map, n_bal, capacity))
    acc = gathered(None, [([own], own_twin, (0, 0))])
    side, up, down, acc = lax.optimization_barrier((side, up, down, acc))
    top = route(up[:half], 0, 1, 0)
    bottom = route(down[half:], 0, -1, 0)
    parts = [side[:half], side[half:]]
    ups = [route(p, 0, 1, 0) for p in parts]
    downs = [route(p, 0, -1, 0) for p in parts]
    acc = gathered(
        acc,
        [
            ([side], twin(side), (1, 0)),
            ([up], twin(up), (0, -1)),
            ([down], twin(down), (0, 1)),
        ],
    )
    top, bottom, acc = lax.optimization_barrier((top, bottom, acc))
    far = [route(top, 1, 0, 0), route(bottom, 1, 0, 0)]
    acc = gathered(acc, [([top, bottom], twin(top, bottom), (0, 2))])
    far[0], ups[1], downs[1], acc = lax.optimization_barrier((far[0], ups[1], downs[1], acc))
    w_parts = w_neigh.reshape(n_bal, 2, half, w_neigh.shape[1])
    pre = across(mine, w_self)
    for k in range(2):
        placed = gathered(
            acc,
            [
                ([ups[k]], twin(ups[k]), (1, -1)),
                ([downs[k]], twin(downs[k]), (1, 1)),
                ([far[k]], twin(far[k]), (1, 2)),
            ],
            last=k + 1,
            mapping=part_map,
            out=placing,
        )
        means = exchange(placed)
        weight = w_parts[:, k].reshape(n_bal * half, w_neigh.shape[1])
        pre = pre + across(means, weight)
    filled = jnp.sum((part_map[0] == column).astype(jnp.int32)) * TILE
    row = lax.broadcasted_iota(jnp.int32, (capacity * TILE, 1), 0)
    hidden = jnp.where(row < filled, jnp.maximum(pre + bias[None, :], 0.0), 0.0)
    return hidden.astype(jnp.bfloat16)[None, None]


def solution(mesh):
    placed = (
        P("blk", "bal"),
        P("blk", None, None, None, None),
        P("blk", None, None),
        P("blk", None, None),
        P("blk", None),
        P(),
        P(),
        P(),
        P("blk", None),
    )
    return jax.shard_map(
        on_device,
        mesh=mesh,
        in_specs=placed,
        out_specs=P("blk", "bal", None, None),
        check_vma=False,
    )
```

time: 167 us -> 143 us (0.86); the launches traced: 167 us -> 141 us
  waiting for transfers between devices: 69.7 us -> 25.7 us
  Pallas kernels: 38.3 us -> 52 us
  matrix products: 8.89 us -> 13.6 us
  starting transfers between devices: 42.8 us -> 39.9 us
  local copies, waits for them, and re-layouts: 5.84 us -> 8.66 us
    ppermute x19 -> x23, waiting for transfers between devices: 48.8 us -> 19.6 us  [route(): return lax.ppermute(block, 'blk', pairs)]
    all_to_all x2 -> x3, waiting for transfers between devices: 20.9 us -> 6.2 us  [exchange(): got = lax.all_to_all(placed, 'bal', split_axis=0, concat_axis=0, tiled=True)]
    pallas_call x4 -> x5, Pallas kernels: 34.8 us -> 48.6 us  [accumulate(): pl.pallas_call(functools.partial(gather_kernel, layout, tuple(offsets), h...]
    ppermute x19 -> x23, starting transfers between devices: 31.7 us -> 24.3 us  [route(): return lax.ppermute(block, 'blk', pairs)]
    dot_general x2 -> x3, matrix products: 8.89 us -> 13.6 us  [across(): lax.dot_general(left, right, (((0,), (0,)), ((), ())), preferred_element_...]
    all_to_all x2 -> x3, starting transfers between devices: 11.2 us -> 15.6 us  [exchange(): got = lax.all_to_all(placed, 'bal', split_axis=0, concat_axis=0, tiled=True)]
  transfers between devices with their start and end apart: 21 -> 26, of which waited for: 6 -> 10; matrix products, arithmetic and copies ran while one was open for 6% -> 11% of each run, Pallas kernels for 23% -> 37%
where the time goes in v2:
time: 143 us; the launch traced here: 141 us
  Pallas kernels  52 us (36%)
  starting transfers between devices  39.9 us (28%)
  waiting for transfers between devices  25.7 us (18%)
  matrix products  13.6 us (10%)
  local copies, waits for them, and re-layouts  8.66 us (6%)
    pallas_call x5, Pallas kernels, accumulate(): pl.pallas_call(functools.partial(gather_kernel, layout, tuple(offsets), h...  48.6 us
    ppermute x23, starting transfers between devices, route(): return lax.ppermute(block, 'blk', pairs)  24.3 us
    ppermute x23, waiting for transfers between devices, route(): return lax.ppermute(block, 'blk', pairs)  19.6 us
    all_to_all x3, starting transfers between devices, exchange(): got = lax.all_to_all(placed, 'bal', split_axis=0, concat_axis=0, tiled=True)  15.6 us
    dot_general x3, matrix products, across(): lax.dot_general(left, right, (((0,), (0,)), ((), ())), preferred_element_...  13.6 us
    all_to_all x3, waiting for transfers between devices, exchange(): got = lax.all_to_all(placed, 'bal', split_axis=0, concat_axis=0, tiled=True)  6.2 us
    pallas_call x1, Pallas kernels, place_features(): pl.pallas_call(place_kernel, in_specs=[pl.BlockSpec(memory_space=pltpu.SM...  3.46 us
  transfers between devices with their start and end apart: 26, of which 10 were waited for; matrix products, arithmetic and copies ran while one was open for 11% of the time, Pallas kernels for 37%

profile of v2, /device:TPU:1, one launch (start us, length us, event | category | flops | bytes accessed | tf_op | source)
XLA Modules:
  0.0 141.2 jit_solution(15739247716042362218)
XLA Ops:
  1.4 2.8 %collective-permute-start = (bf16[64,8192]{1,0:T(8,128)(2,1)}, bf16[64,8192]{1,0:T(8,128)(2,1)}, u32[]{:S(2)}, u32[]{:S(2)}) collective-permute-start(bf16[64,8192]{1,0:T(8,128)(2,1)} %bitcast.27), channel_id=1, source_target_pairs={{0,64},{8,72},{16,80},{24,88},{32,96},{40,104},{48,112},{56,120},{... | collective-permute-start | bytes 3145736 | tf_op jit(solution)/shard_map/ppermute | solution.py:24
  7.0 3.5 %place_features.1 = bf16[8,64,2048]{2,1,0:T(8,128)(2,1)} custom-call(s32[1,64]{1,0:T(1,128)} %refs_0_.3, bf16[64,8192]{1,0:T(8,128)(2,1)} %bitcast.30), custom_call_target="tpu_custom_call" | custom-call | tf_op jit(solution)/shard_map/place_features/pallas_call | solution.py:185
  10.5 5.1 %all-to-all-start = ((bf16[8,64,2048]{2,1,0:T(8,128)(2,1)}), bf16[8,64,2048]{2,1,0:T(8,128)(2,1)S(1)}, u32[]{:S(2)}, u32[]{:S(2)}) async-start(bf16[8,64,2048]{2,1,0:T(8,128)(2,1)} %place_features.1), calls=%async_computation | async-start | bytes 4194304 | tf_op jit(solution)/shard_map/all_to_all | solution.py:196
  15.5 5.9 %aggregate.3.refs_7_ = f32[65,80,128]{2,1,0:T(8,128)} custom-call(s32[1]{0:T(128)} %bitcast.2.here, s32[16]{0:T(128)} %bitcast.45, s32[16,32]{1,0:T(8,128)} %bitcast.35, s32[16,32]{1,0:T(8,128)} %bitcast.40, bf16[16,32,128,128]{3,2,1,0:T(8,128)(2,1)} %bitcast.20, bf16[64,8192]{1,0:T(8,128)(2,1)} %bitcast.31, bf16[64,8192]{1,0:T(8,128)(2,1)} %collective-permute-done.3.refs_2_), custom_call_target="tpu_custom_call" | custom-call | tf_op jit(solution)/shard_map/aggregate/pallas_call | solution.py:150
  21.5 6.6 %collective-permute-done.refs_1_ = bf16[64,8192]{1,0:T(8,128)(2,1)} collective-permute-done((bf16[64,8192]{1,0:T(8,128)(2,1)}, bf16[64,8192]{1,0:T(8,128)(2,1)}, u32[]{:S(2)}, u32[]{:S(2)}) %collective-permute-start) | collective-permute-done | bytes 1048608 | tf_op jit(solution)/shard_map/ppermute | solution.py:24
  28.0 2.4 %collective-permute-done.1.refs_2_ = bf16[64,8192]{1,0:T(8,128)(2,1)} collective-permute-done((bf16[64,8192]{1,0:T(8,128)(2,1)}, bf16[64,8192]{1,0:T(8,128)(2,1)}, u32[]{:S(2)}, u32[]{:S(2)}) %collective-permute-start.1) | collective-permute-done | bytes 1048608 | tf_op jit(solution)/shard_map/ppermute | solution.py:24
  31.5 1.9 %slice.19 = bf16[32,8192]{1,0:T(8,128)(2,1)} slice(bf16[64,8192]{1,0:T(8,128)(2,1)} %collective-permute-done.1.refs_2_), slice={[0:32], [0:8192]} | slice | bytes 1048576 | tf_op jit(solution)/shard_map/slice | solution.py:239
  33.3 1.9 %slice.20 = bf16[32,8192]{1,0:T(8,128)(2,1)} slice(bf16[64,8192]{1,0:T(8,128)(2,1)} %collective-permute-done.2.refs_3_), slice={[32:64], [0:8192]} | slice | bytes 1048576 | tf_op jit(solution)/shard_map/slice | solution.py:240
  38.4 2.2 %fusion.2 = (bf16[32,8192]{1,0:T(8,128)(2,1)}, bf16[32,8192]{1,0:T(8,128)(2,1)}) fusion(bf16[64,8192]{1,0:T(8,128)(2,1)} %collective-permute-done.refs_1_), kind=kLoop, calls=%fused_computation.5 | loop fusion | bytes 2097152 | tf_op jit(solution)/shard_map/slice | solution.py:241
  40.7 2.6 %collective-permute-start.5 = (bf16[32,8192]{1,0:T(8,128)(2,1)}, bf16[32,8192]{1,0:T(8,128)(2,1)}, u32[]{:S(2)}, u32[]{:S(2)}) collective-permute-start(bf16[32,8192]{1,0:T(8,128)(2,1)} %get-tuple-element.27), channel_id=1, source_target_pairs={{0,48},{8,56},{16,0},{24,8},{32,16},{40,24},{48,32},{56,40},{64,11... | collective-permute-start | bytes 1572872 | tf_op jit(solution)/shard_map/ppermute | solution.py:24
  43.3 13.1 %aggregate.4.refs_5_ = f32[65,80,128]{2,1,0:T(8,128)} custom-call(s32[1]{0:T(128)} %bitcast.2.here, s32[16]{0:T(128)} %bitcast.46, s32[16,32]{1,0:T(8,128)} %bitcast.36, s32[16,32]{1,0:T(8,128)} %bitcast.41, bf16[16,32,128,128]{3,2,1,0:T(8,128)(2,1)} %bitcast.21, bf16[64,8192]{1,0:T(8,128)(2,1)} %collective-permute-done.refs_1_, ...), custom_call_target="tpu_custom_call" | custom-call | tf_op jit(solution)/shard_map/aggregate/pallas_call | solution.py:150
  57.2 4.8 %collective-permute-done.4.refs_2_ = bf16[32,8192]{1,0:T(8,128)(2,1)} collective-permute-done((bf16[32,8192]{1,0:T(8,128)(2,1)}, bf16[32,8192]{1,0:T(8,128)(2,1)}, u32[]{:S(2)}, u32[]{:S(2)}) %collective-permute-start.4) | collective-permute-done | bytes 524320 | tf_op jit(solution)/shard_map/ppermute | solution.py:24
  64.2 1.7 %collective-permute-start.16 = (bf16[32,8192]{1,0:T(8,128)(2,1)}, bf16[32,8192]{1,0:T(8,128)(2,1)}, u32[]{:S(2)}, u32[]{:S(2)}) collective-permute-start(bf16[32,8192]{1,0:T(8,128)(2,1)} %collective-permute-done.4.refs_2_), channel_id=1, source_target_pairs={{0,8},{8,0},{16,24},{24,16},{32,40},{40,32},{48,56},{56,48},{64,72... | collective-permute-start | bytes 1572872 | tf_op jit(solution)/shard_map/ppermute | solution.py:24
  67.6 6.6 %aggregate.5.refs_8_ = f32[65,80,128]{2,1,0:T(8,128)} custom-call(s32[1]{0:T(128)} %bitcast.2.here, s32[16]{0:T(128)} %bitcast.47, s32[16,32]{1,0:T(8,128)} %bitcast.37, s32[16,32]{1,0:T(8,128)} %bitcast.42, bf16[16,32,128,128]{3,2,1,0:T(8,128)(2,1)} %bitcast.22, bf16[32,8192]{1,0:T(8,128)(2,1)} %collective-permute-done.6.refs_1_, ...), custom_call_target="tpu_custom_call" | custom-call | tf_op jit(solution)/shard_map/aggregate/pallas_call | solution.py:150
  74.6 2.7 %collective-permute-done.11.refs_4_ = bf16[32,8192]{1,0:T(8,128)(2,1)} collective-permute-done((bf16[32,8192]{1,0:T(8,128)(2,1)}, bf16[32,8192]{1,0:T(8,128)(2,1)}, u32[]{:S(2)}, u32[]{:S(2)}) %collective-permute-start.11) | collective-permute-done | bytes 524320 | tf_op jit(solution)/shard_map/ppermute | solution.py:24
  77.3 2.4 %collective-permute-start.18 = (bf16[32,8192]{1,0:T(8,128)(2,1)}, bf16[32,8192]{1,0:T(8,128)(2,1)S(1)}, u32[]{:S(2)}, u32[]{:S(2)}) collective-permute-start(bf16[32,8192]{1,0:T(8,128)(2,1)} %collective-permute-done.11.refs_4_), channel_id=1, source_target_pairs={{0,8},{8,0},{16,24},{24,16},{32,40},{40,32},{48,56},{56,48},{64,72... | collective-permute-start | bytes 1572872 | tf_op jit(solution)/shard_map/ppermute | solution.py:24
  82.2 11.4 %aggregate_last.2 = bf16[8,32,2048]{2,1,0:T(8,128)(2,1)} custom-call(s32[1]{0:T(128)} %bitcast.2.here, s32[16]{0:T(128)} %bitcast.48, s32[16,32]{1,0:T(8,128)} %bitcast.38, s32[16,32]{1,0:T(8,128)} %bitcast.43, s32[1,64]{1,0:T(1,128)} %refs_0_.3, bf16[16,32,128,128]{3,2,1,0:T(8,128)(2,1)} %bitcast.23, bf16[32,8192]{1,0:T(8,128)(2,1)} %collective-permute-done.4.refs_2_, ...), custom_call_target="tpu_custom_call" | custom-call | tf_op jit(solution)/shard_map/aggregate_last/pallas_call | solution.py:150
  93.6 5.1 %all-to-all-start.1 = ((bf16[8,32,2048]{2,1,0:T(8,128)(2,1)}), bf16[8,32,2048]{2,1,0:T(8,128)(2,1)}, u32[]{:S(2)}, u32[]{:S(2)}) async-start(bf16[8,32,2048]{2,1,0:T(8,128)(2,1)} %aggregate_last.2), calls=%async_computation.1 | async-start | bytes 2097152 | tf_op jit(solution)/shard_map/all_to_all | solution.py:196
  103.3 11.4 %aggregate_last.3 = bf16[8,32,2048]{2,1,0:T(8,128)(2,1)} custom-call(s32[1]{0:T(128)} %bitcast.2.here, s32[16]{0:T(128)} %bitcast.49, s32[16,32]{1,0:T(8,128)} %bitcast.39, s32[16,32]{1,0:T(8,128)} %bitcast.44, s32[1,64]{1,0:T(1,128)} %refs_0_.3, bf16[16,32,128,128]{3,2,1,0:T(8,128)(2,1)} %bitcast.24, bf16[32,8192]{1,0:T(8,128)(2,1)} %collective-permute-done.12.refs_2_, ...), custom_call_target="tpu_custom_call" | custom-call | tf_op jit(solution)/shard_map/aggregate_last/pallas_call | solution.py:150
  114.8 5.4 %all-to-all-start.2 = ((bf16[8,32,2048]{2,1,0:T(8,128)(2,1)}), bf16[8,32,2048]{2,1,0:T(8,128)(2,1)}, u32[]{:S(2)}, u32[]{:S(2)}) async-start(bf16[8,32,2048]{2,1,0:T(8,128)(2,1)} %aggregate_last.3), calls=%async_computation.2 | async-start | bytes 2097152 | tf_op jit(solution)/shard_map/all_to_all | solution.py:196
  121.4 3.3 %fusion.4 = f32[2048,512]{1,0:T(8,128)} fusion(bf16[512,2048]{1,0:T(8,128)(2,1)S(1)} %bitcast.25, bf16[512,512]{1,0:T(8,128)(2,1)S(1)} %copy-done), kind=kOutput, calls=%fused_computation.7 | convolution fusion | flops 1073741824 | bytes 6815744 | tf_op jit(solution)/shard_map/dot_general | solution.py:201
  124.7 4.0 %fusion.5 = f32[2048,512]{1,0:T(8,128)} fusion(bf16[256,2048]{1,0:T(8,128)(2,1)} %bitcast.7, bf16[256,512]{1,0:T(8,128)(2,1)S(1)} %bitcast.33), kind=kOutput, calls=%fused_computation.8 | convolution fusion | flops 536870912 | bytes 5505024 | tf_op jit(solution)/shard_map/dot_general | solution.py:201
  128.7 6.2 %all-to-all-done.2 = bf16[8,32,2048]{2,1,0:T(8,128)(2,1)} async-done(((bf16[8,32,2048]{2,1,0:T(8,128)(2,1)}), bf16[8,32,2048]{2,1,0:T(8,128)(2,1)}, u32[]{:S(2)}, u32[]{:S(2)}) %all-to-all-start.2) | async-done | bytes 1048608 | tf_op jit(solution)/shard_map/all_to_all | solution.py:196
  134.9 6.3 %fusion = bf16[1,1,2048,512]{3,2,1,0:T(8,128)(2,1)} fusion(bf16[256,2048]{1,0:T(8,128)(2,1)} %bitcast.10, bf16[256,512]{1,0:T(8,128)(2,1)S(1)} %bitcast.32, f32[2048,512]{1,0:T(8,128)} %fusion.4, f32[2048,512]{1,0:T(8,128)} %fusion.5, f32[512]{0:T(512)S(1)} %copy-done.6, pred[2048]{0:T(1024)(128)(4,1)S(1)} %iota_compare_fusion), kind=kOutput, calls=%fused_computation.1 | convolution fusion | flops 543162368 | bytes 11800576 | tf_op jit(solution)/shard_map/dot_general | solution.py:201
  (57 shorter events, 21.2 us)
Async XLA Ops:
  0.0 15.5 %collective-permute-start.3 = (bf16[64,8192]{1,0:T(8,128)(2,1)}, bf16[64,8192]{1,0:T(8,128)(2,1)}, u32[]{:S(2)}, u32[]{:S(2)}) collective-permute-start(bf16[64,8192]{1,0:T(8,128)(2,1)} %bitcast.26), channel_id=1, source_target_pairs={{0,8},{8,0},{16,24},{24,16},{32,40},{40,32},{48,56},{56,48},{64,72... | collective-permute-start | bytes 3145736 | tf_op jit(solution)/shard_map/ppermute | solution.py:24
  1.4 26.6 %collective-permute-start = (bf16[64,8192]{1,0:T(8,128)(2,1)}, bf16[64,8192]{1,0:T(8,128)(2,1)}, u32[]{:S(2)}, u32[]{:S(2)}) collective-permute-start(bf16[64,8192]{1,0:T(8,128)(2,1)} %bitcast.27), channel_id=1, source_target_pairs={{0,64},{8,72},{16,80},{24,88},{32,96},{40,104},{48,112},{56,120},{... | collective-permute-start | bytes 3145736 | tf_op jit(solution)/shard_map/ppermute | solution.py:24
  4.3 26.1 %collective-permute-start.1 = (bf16[64,8192]{1,0:T(8,128)(2,1)}, bf16[64,8192]{1,0:T(8,128)(2,1)}, u32[]{:S(2)}, u32[]{:S(2)}) collective-permute-start(bf16[64,8192]{1,0:T(8,128)(2,1)} %bitcast.28), channel_id=1, source_target_pairs={{0,16},{8,24},{16,32},{24,40},{32,48},{40,56},{48,0},{56,8},{64,80... | collective-permute-start | bytes 3145736 | tf_op jit(solution)/shard_map/ppermute | solution.py:24
  5.6 24.8 %collective-permute-start.2 = (bf16[64,8192]{1,0:T(8,128)(2,1)}, bf16[64,8192]{1,0:T(8,128)(2,1)}, u32[]{:S(2)}, u32[]{:S(2)}) collective-permute-start(bf16[64,8192]{1,0:T(8,128)(2,1)} %bitcast.29), channel_id=1, source_target_pairs={{0,48},{8,56},{16,0},{24,8},{32,16},{40,24},{48,32},{56,40},{64,11... | collective-permute-start | bytes 3145736 | tf_op jit(solution)/shard_map/ppermute | solution.py:24
  10.5 83.2 %all-to-all-start = ((bf16[8,64,2048]{2,1,0:T(8,128)(2,1)}), bf16[8,64,2048]{2,1,0:T(8,128)(2,1)S(1)}, u32[]{:S(2)}, u32[]{:S(2)}) async-start(bf16[8,64,2048]{2,1,0:T(8,128)(2,1)} %place_features.1), calls=%async_computation | async-start | bytes 4194304 | tf_op jit(solution)/shard_map/all_to_all | solution.py:196
  30.4 12.9 %collective-permute-start.9 = (bf16[64,8192]{1,0:T(8,128)(2,1)}, bf16[64,8192]{1,0:T(8,128)(2,1)}, u32[]{:S(2)}, u32[]{:S(2)}) collective-permute-start(bf16[64,8192]{1,0:T(8,128)(2,1)} %collective-permute-done.1.refs_2_), channel_id=1, source_target_pairs={{0,8},{8,0},{16,24},{24,16},{32,40},{40,32},{48,56},{56,48},{64,72... | collective-permute-start | bytes 3145736 | tf_op jit(solution)/shard_map/ppermute | solution.py:24
  33.3 7.3 %collective-permute-start.10 = (bf16[64,8192]{1,0:T(8,128)(2,1)}, bf16[64,8192]{1,0:T(8,128)(2,1)}, u32[]{:S(2)}, u32[]{:S(2)}) collective-permute-start(bf16[64,8192]{1,0:T(8,128)(2,1)} %collective-permute-done.2.refs_3_), channel_id=1, source_target_pairs={{0,8},{8,0},{16,24},{24,16},{32,40},{40,32},{48,56},{56,48},{64,72... | collective-permute-start | bytes 3145736 | tf_op jit(solution)/shard_map/ppermute | solution.py:24
  35.2 5.5 %collective-permute-start.8 = (bf16[64,8192]{1,0:T(8,128)(2,1)}, bf16[64,8192]{1,0:T(8,128)(2,1)}, u32[]{:S(2)}, u32[]{:S(2)}) collective-permute-start(bf16[64,8192]{1,0:T(8,128)(2,1)} %collective-permute-done.refs_1_), channel_id=1, source_target_pairs={{0,8},{8,0},{16,24},{24,16},{32,40},{40,32},{48,56},{56,48},{64,72... | collective-permute-start | bytes 3145736 | tf_op jit(solution)/shard_map/ppermute | solution.py:24
  35.7 20.7 %collective-permute-start.6 = (bf16[32,8192]{1,0:T(8,128)(2,1)}, bf16[32,8192]{1,0:T(8,128)(2,1)}, u32[]{:S(2)}, u32[]{:S(2)}) collective-permute-start(bf16[32,8192]{1,0:T(8,128)(2,1)} %slice.19), channel_id=1, source_target_pairs={{0,16},{8,24},{16,32},{24,40},{32,48},{40,56},{48,0},{56,8},{64,80... | collective-permute-start | bytes 1572872 | tf_op jit(solution)/shard_map/ppermute | solution.py:24
  37.0 19.4 %collective-permute-start.7 = (bf16[32,8192]{1,0:T(8,128)(2,1)}, bf16[32,8192]{1,0:T(8,128)(2,1)S(1)}, u32[]{:S(2)}, u32[]{:S(2)}) collective-permute-start(bf16[32,8192]{1,0:T(8,128)(2,1)} %slice.20), channel_id=1, source_target_pairs={{0,48},{8,56},{16,0},{24,8},{32,16},{40,24},{48,32},{56,40},{64,11... | collective-permute-start | bytes 1572872 | tf_op jit(solution)/shard_map/ppermute | solution.py:24
  40.6 21.4 %collective-permute-start.4 = (bf16[32,8192]{1,0:T(8,128)(2,1)}, bf16[32,8192]{1,0:T(8,128)(2,1)}, u32[]{:S(2)}, u32[]{:S(2)}) collective-permute-start(bf16[32,8192]{1,0:T(8,128)(2,1)} %get-tuple-element.27), channel_id=1, source_target_pairs={{0,16},{8,24},{16,32},{24,40},{32,48},{40,56},{48,0},{56,8},{64,80... | collective-permute-start | bytes 1572872 | tf_op jit(solution)/shard_map/ppermute | solution.py:24
  40.7 22.8 %collective-permute-start.5 = (bf16[32,8192]{1,0:T(8,128)(2,1)}, bf16[32,8192]{1,0:T(8,128)(2,1)}, u32[]{:S(2)}, u32[]{:S(2)}) collective-permute-start(bf16[32,8192]{1,0:T(8,128)(2,1)} %get-tuple-element.27), channel_id=1, source_target_pairs={{0,48},{8,56},{16,0},{24,8},{32,16},{40,24},{48,32},{56,40},{64,11... | collective-permute-start | bytes 1572872 | tf_op jit(solution)/shard_map/ppermute | solution.py:24
  56.5 7.8 %collective-permute-start.14 = (bf16[32,8192]{1,0:T(8,128)(2,1)}, bf16[32,8192]{1,0:T(8,128)(2,1)S(1)}, u32[]{:S(2)}, u32[]{:S(2)}) collective-permute-start(bf16[32,8192]{1,0:T(8,128)(2,1)} %collective-permute-done.6.refs_1_), channel_id=1, source_target_pairs={{0,8},{8,0},{16,24},{24,16},{32,40},{40,32},{48,56},{56,48},{64,72... | collective-permute-start | bytes 1572872 | tf_op jit(solution)/shard_map/ppermute | solution.py:24
  57.0 8.9 %collective-permute-start.15 = (bf16[32,8192]{1,0:T(8,128)(2,1)S(1)}, bf16[32,8192]{1,0:T(8,128)(2,1)S(1)}, u32[]{:S(2)}, u32[]{:S(2)}) collective-permute-start(bf16[32,8192]{1,0:T(8,128)(2,1)S(1)} %collective-permute-done.7.refs_2_), channel_id=1, source_target_pairs={{0,8},{8,0},{16,24},{24,16},{32,40},{40,32},{48,56},{56,48},{64,72... | collective-permute-start | bytes 1572872 | tf_op jit(solution)/shard_map/ppermute | solution.py:24
  57.1 17.1 %collective-permute-start.12 = (bf16[32,8192]{1,0:T(8,128)(2,1)}, bf16[32,8192]{1,0:T(8,128)(2,1)}, u32[]{:S(2)}, u32[]{:S(2)}) collective-permute-start(bf16[32,8192]{1,0:T(8,128)(2,1)} %get-tuple-element.28), channel_id=1, source_target_pairs={{0,16},{8,24},{16,32},{24,40},{32,48},{40,56},{48,0},{56,8},{64,80... | collective-permute-start | bytes 1572872 | tf_op jit(solution)/shard_map/ppermute | solution.py:24
  62.0 12.6 %collective-permute-start.13 = (bf16[32,8192]{1,0:T(8,128)(2,1)}, bf16[32,8192]{1,0:T(8,128)(2,1)}, u32[]{:S(2)}, u32[]{:S(2)}) collective-permute-start(bf16[32,8192]{1,0:T(8,128)(2,1)} %get-tuple-element.28), channel_id=1, source_target_pairs={{0,48},{8,56},{16,0},{24,8},{32,16},{40,24},{48,32},{56,40},{64,11... | collective-permute-start | bytes 1572872 | tf_op jit(solution)/shard_map/ppermute | solution.py:24
  63.5 13.8 %collective-permute-start.11 = (bf16[32,8192]{1,0:T(8,128)(2,1)}, bf16[32,8192]{1,0:T(8,128)(2,1)}, u32[]{:S(2)}, u32[]{:S(2)}) collective-permute-start(bf16[32,8192]{1,0:T(8,128)(2,1)} %collective-permute-done.6.refs_1_), channel_id=1, source_target_pairs={{0,64},{8,72},{16,80},{24,88},{32,96},{40,104},{48,112},{56,120},{... | collective-permute-start | bytes 1572872 | tf_op jit(solution)/shard_map/ppermute | solution.py:24
  64.2 16.2 %collective-permute-start.16 = (bf16[32,8192]{1,0:T(8,128)(2,1)}, bf16[32,8192]{1,0:T(8,128)(2,1)}, u32[]{:S(2)}, u32[]{:S(2)}) collective-permute-start(bf16[32,8192]{1,0:T(8,128)(2,1)} %collective-permute-done.4.refs_2_), channel_id=1, source_target_pairs={{0,8},{8,0},{16,24},{24,16},{32,40},{40,32},{48,56},{56,48},{64,72... | collective-permute-start | bytes 1572872 | tf_op jit(solution)/shard_map/ppermute | solution.py:24
  66.8 13.6 %collective-permute-start.17 = (bf16[32,8192]{1,0:T(8,128)(2,1)}, bf16[32,8192]{1,0:T(8,128)(2,1)}, u32[]{:S(2)}, u32[]{:S(2)}) collective-permute-start(bf16[32,8192]{1,0:T(8,128)(2,1)} %collective-permute-done.5.refs_3_), channel_id=1, source_target_pairs={{0,8},{8,0},{16,24},{24,16},{32,40},{40,32},{48,56},{56,48},{64,72... | collective-permute-start | bytes 1572872 | tf_op jit(solution)/shard_map/ppermute | solution.py:24
  77.3 4.1 %collective-permute-start.18 = (bf16[32,8192]{1,0:T(8,128)(2,1)}, bf16[32,8192]{1,0:T(8,128)(2,1)S(1)}, u32[]{:S(2)}, u32[]{:S(2)}) collective-permute-start(bf16[32,8192]{1,0:T(8,128)(2,1)} %collective-permute-done.11.refs_4_), channel_id=1, source_target_pairs={{0,8},{8,0},{16,24},{24,16},{32,40},{40,32},{48,56},{56,48},{64,72... | collective-permute-start | bytes 1572872 | tf_op jit(solution)/shard_map/ppermute | solution.py:24
  79.6 20.4 %collective-permute-start.19 = (bf16[32,8192]{1,0:T(8,128)(2,1)}, bf16[32,8192]{1,0:T(8,128)(2,1)}, u32[]{:S(2)}, u32[]{:S(2)}) collective-permute-start(bf16[32,8192]{1,0:T(8,128)(2,1)} %copy-done.1), channel_id=1, source_target_pairs={{0,64},{8,72},{16,80},{24,88},{32,96},{40,104},{48,112},{56,120},{... | collective-permute-start | bytes 1572872 | tf_op jit(solution)/shard_map/ppermute | solution.py:24
  93.6 21.1 %all-to-all-start.1 = ((bf16[8,32,2048]{2,1,0:T(8,128)(2,1)}), bf16[8,32,2048]{2,1,0:T(8,128)(2,1)}, u32[]{:S(2)}, u32[]{:S(2)}) async-start(bf16[8,32,2048]{2,1,0:T(8,128)(2,1)} %aggregate_last.2), calls=%async_computation.1 | async-start | bytes 2097152 | tf_op jit(solution)/shard_map/all_to_all | solution.py:196
  100.1 3.3 %collective-permute-start.22 = (bf16[32,8192]{1,0:T(8,128)(2,1)}, bf16[32,8192]{1,0:T(8,128)(2,1)}, u32[]{:S(2)}, u32[]{:S(2)}) collective-permute-start(bf16[32,8192]{1,0:T(8,128)(2,1)} %collective-permute-done.19.refs_4_), channel_id=1, source_target_pairs={{0,8},{8,0},{16,24},{24,16},{32,40},{40,32},{48,56},{56,48},{64,72... | collective-permute-start | bytes 1572872 | tf_op jit(solution)/shard_map/ppermute | solution.py:24
  114.8 20.1 %all-to-all-start.2 = ((bf16[8,32,2048]{2,1,0:T(8,128)(2,1)}), bf16[8,32,2048]{2,1,0:T(8,128)(2,1)}, u32[]{:S(2)}, u32[]{:S(2)}) async-start(bf16[8,32,2048]{2,1,0:T(8,128)(2,1)} %aggregate_last.3), calls=%async_computation.2 | async-start | bytes 2097152 | tf_op jit(solution)/shard_map/all_to_all | solution.py:196
  (9 other events, 170.5 us)

commit v3 on v2

v3 whole, which is shorter than its diff:
```python
import functools

import jax
import jax.numpy as jnp
from jax import lax
from jax.experimental import pallas as pl
from jax.experimental.pallas import tpu as pltpu
from jax.sharding import PartitionSpec as P

TILE = 128
ONES = 16
UNROLL = 8
AHEAD = 3
SPLIT = 8


def spot(position):
    return position // 8, (position // 2) % 4, position % 2


def route(block, dx, dy, dc):
    pairs = []
    for source in range(16):
        x, y, c = spot(source)
        pairs.append((source, ((x + dx) % 2) * 8 + ((y + dy) % 4) * 2 + (c + dc) % 2))
    return lax.ppermute(block, "blk", pairs)


def absorb(acc_ref, halves, source, table, v_ref):
    slots = v_ref.shape[0]
    live = table[source, 2 * slots]
    dummy = acc_ref.shape[0] - 1

    def step(group, carry):
        found = []
        for u in range(UNROLL):
            slot = group * UNROLL + u
            start = pl.multiple_of(table[source, slots + slot] * TILE, TILE)
            parts = [ref[:, pl.ds(start, TILE)] for ref in halves]
            parts.append(jnp.ones((ONES, TILE), jnp.bfloat16))
            left = jnp.concatenate(parts, axis=0)
            prod = lax.dot_general(
                left, v_ref[slot], (((1,), (1,)), ((), ())), preferred_element_type=jnp.float32
            )
            found.append((jnp.where(slot < live, table[source, slot], dummy), prod))
        for target, prod in found:
            acc_ref[target] += prod
        return carry

    lax.fori_loop(0, (live + UNROLL - 1) // UNROLL, step, 0)


def seat(here, dx, dy, dc):
    x, y, c = here // 8, (here // 2) % 4, here % 2
    return ((x + dx) % 2) * 8 + ((y + dy) % 4) * 2 + (c + dc) % 2


def begin(copy):
    copy.start()


def finish(copy):
    copy.wait()


def act_on(act, make, i, q):
    act(make(i, q))


def gather_kernel(layout, offsets, height, first, last, table, *refs):
    refs = list(refs)
    v_hbm = refs.pop(0)
    n_blocks = sum(layout)
    n = len(layout)
    blocks = [refs.pop(0) for i in range(n_blocks)]
    acc_in = None if first else refs.pop(0)
    out_ref = refs.pop(0)
    v_ref, v_sem, b_sem = refs.pop(0), refs.pop(0), refs.pop(0)
    staged = [refs.pop(0) for i in range(n_blocks)]
    acc_ref, a_sem, o_sem = refs.pop(0), refs.pop(0), refs.pop(0)
    made_ref, used = refs if last else (acc_ref, None)
    slots = v_ref.shape[1]
    here = table[0, 2 * slots + 1]
    places = [seat(here, *offsets[i]) for i in range(n)]
    tiles_per = acc_ref.shape[0] - 1
    span = tiles_per // SPLIT
    loads = []
    if not first:
        for k in range(SPLIT):
            part = pl.ds(k * span, span)
            loads.append(pltpu.make_async_copy(acc_in.at[part], acc_ref.at[part], a_sem.at[k]))
    for copy in loads:
        copy.start()
    parts = v_ref.shape[1] // UNROLL
    begins = [sum(layout[:i]) for i in range(n)]

    def values_copy(i, q):
        part = pl.ds(q * UNROLL, UNROLL)
        return pltpu.make_async_copy(
            v_hbm.at[places[i], part], v_ref.at[i, part], v_sem.at[i * parts + q]
        )

    def each(i, act):
        for j in range(begins[i], begins[i] + layout[i]):
            act(pltpu.make_async_copy(blocks[j], staged[j], b_sem.at[j]))
        for q in range(parts):
            pl.when(table[places[i], 2 * slots] > q * UNROLL)(functools.partial(act_on, act, values_copy, i, q))

    for i in range(min(AHEAD, n)):
        each(i, begin)
    if first:
        acc_ref[...] = jnp.zeros_like(acc_ref)
    if last:
        made_ref[...] = jnp.zeros_like(made_ref)
    for copy in loads:
        copy.wait()
    for i, width in enumerate(layout):
        if i + AHEAD < n:
            each(i + AHEAD, begin)
        each(i, finish)
        absorb(
            acc_ref, staged[begins[i] : begins[i] + width], places[i], table, v_ref.at[i]
        )
    if last:

        def tile_of(t):
            inverse = 1.0 / (1.0 + acc_ref[t, height : height + 1, :])
            return (acc_ref[t, 0:height, :] * inverse).astype(jnp.bfloat16)

        place_into(made_ref, table, used, tiles_per, tile_of)
    step = out_ref.shape[0] // SPLIT
    stores = [
        pltpu.make_async_copy(
            made_ref.at[pl.ds(k * step, step)], out_ref.at[pl.ds(k * step, step)], o_sem.at[k]
        )
        for k in range(SPLIT)
    ]
    for copy in stores:
        copy.start()
    for copy in stores:
        copy.wait()


def accumulate(acc, groups, offsets, table, values, tiles_per, last=False, out=None):
    layout = tuple(len(g) for g in groups)
    blocks = [b for g in groups for b in g]
    height = sum(b.shape[0] for b in groups[0])
    first = acc is None
    smem = pl.BlockSpec(memory_space=pltpu.SMEM)
    anywhere = pl.BlockSpec(memory_space=pl.ANY)
    operands = [table]
    specs = [smem] + [anywhere] * (1 + len(blocks))
    operands += [values] + blocks
    if not first:
        operands.append(acc)
        specs.append(anywhere)
    shape = (tiles_per, height + ONES, TILE)
    scratch = [
        pltpu.VMEM((len(groups),) + values.shape[1:], values.dtype),
        pltpu.SemaphoreType.DMA((len(groups) * (values.shape[1] // UNROLL),)),
        pltpu.SemaphoreType.DMA((len(blocks),)),
    ] + [pltpu.VMEM(b.shape, b.dtype) for b in blocks]
    scratch += [
        pltpu.VMEM((tiles_per + 1,) + shape[1:], jnp.float32),
        pltpu.SemaphoreType.DMA((SPLIT,)),
        pltpu.SemaphoreType.DMA((SPLIT,)),
    ]
    if last:
        made = (out[0], height, out[1])
        scratch += [pltpu.VMEM(made, jnp.bfloat16), pltpu.SMEM((out[0],), jnp.int32)]
        result = jax.ShapeDtypeStruct(made, jnp.bfloat16)
    else:
        result = jax.ShapeDtypeStruct(shape, jnp.float32)
    return pl.pallas_call(
        functools.partial(gather_kernel, layout, tuple(offsets), height, first, last),
        in_specs=specs,
        out_specs=anywhere,
        out_shape=result,
        scratch_shapes=scratch,
        cost_estimate=pl.CostEstimate(
            flops=0, transcendentals=0, bytes_accessed=(8 + 3 * len(groups)) * 2**20
        ),
        name="aggregate_last" if last else "aggregate",
    )(*operands)


def place_into(out_ref, mapping, used, tiles_per, tile_of):
    n_bal = out_ref.shape[0]
    out_ref[...] = jnp.zeros_like(out_ref)
    for d in range(n_bal):
        used[d] = 0

    def step(t, carry):
        d = mapping[mapping.shape[0] - 1, t]
        k = used[d]
        used[d] = k + 1
        out_ref[d, :, pl.ds(pl.multiple_of(k * TILE, TILE), TILE)] = tile_of(t)
        return carry

    lax.fori_loop(0, tiles_per, step, 0, unroll=8)


def place_kernel(mapping, x_ref, out_ref, used):
    tiles_per = x_ref.shape[1] // TILE
    place_into(
        out_ref, mapping, used, tiles_per,
        lambda t: x_ref[:, pl.ds(pl.multiple_of(t * TILE, TILE), TILE)],
    )


def place_features(block, mapping, n_bal, capacity):
    return pl.pallas_call(
        place_kernel,
        in_specs=[pl.BlockSpec(memory_space=pltpu.SMEM), pl.BlockSpec(memory_space=pltpu.VMEM)],
        out_specs=pl.BlockSpec(memory_space=pltpu.VMEM),
        out_shape=jax.ShapeDtypeStruct((n_bal, block.shape[0], capacity * TILE), block.dtype),
        scratch_shapes=[pltpu.SMEM((n_bal,), jnp.int32)],
        cost_estimate=pl.CostEstimate(flops=0, transcendentals=0, bytes_accessed=8 * 2**20),
        name="place_features",
    )(mapping, block)


def fit(table):
    return jnp.pad(table, ((0, 0), (0, TILE - table.shape[1])))


def exchange(placed):
    got = lax.all_to_all(placed, "bal", split_axis=0, concat_axis=0, tiled=True)
    return got.reshape(got.shape[0] * got.shape[1], got.shape[2])


def across(left, right):
    return lax.dot_general(
        left, right, (((0,), (0,)), ((), ())), preferred_element_type=jnp.float32
    )


def on_device(
    features, tile_values, tile_rows, tile_cols, tile_counts, w_self, w_neigh, bias, part_map
):
    n_blk = lax.axis_size("blk")
    n_bal = lax.axis_size("bal")
    here = lax.axis_index("blk")
    column = lax.axis_index("bal")
    tiles_per = part_map.shape[1]
    capacity = 2 * tiles_per // n_bal
    width = features.shape[1]
    half = width // 2
    values = tile_values[0]
    table = jnp.concatenate(
        [tile_rows[0], tile_cols[0], tile_counts[0][:, None], jnp.full((n_blk, 1), here)], axis=1
    ).astype(jnp.int32)
    table = jnp.concatenate([fit(table), fit(part_map.astype(jnp.int32))], axis=0)
    own = features.T
    placing = (n_bal, capacity * TILE)

    def gathered(acc, pieces, **extra):
        groups = [list(blocks) for blocks, offset in pieces]
        offsets = [offset for blocks, offset in pieces]
        return accumulate(acc, groups, offsets, table, values, tiles_per, **extra)

    def twin(block):
        return route(block, 0, 0, 1)

    side = route(own, 1, 0, 0)
    up = route(own, 0, 1, 0)
    down = route(own, 0, -1, 0)
    mine = place_features(own, table, n_bal, capacity)
    acc = gathered(None, [([own], (0, 0, 0)), ([twin(own)], (0, 0, 1))])
    side, up, down, mine, acc = lax.optimization_barrier((side, up, down, mine, acc))
    mine = exchange(mine)
    across_up = route(up, 1, 0, 0)
    over = route(up, 0, 1, 0)
    across_down = route(side, 0, -1, 0)
    acc = gathered(
        acc,
        [
            ([side], (1, 0, 0)),
            ([up], (0, -1, 0)),
            ([down], (0, 1, 0)),
            ([twin(side)], (1, 0, 1)),
            ([twin(up)], (0, -1, 1)),
            ([twin(down)], (0, 1, 1)),
        ],
    )
    across_up, over, across_down, acc = lax.optimization_barrier(
        (across_up, over, across_down, acc)
    )
    last = [route(across_up[:half], 0, 1, 0), route(across_down[half:], 0, -1, 0)]
    acc = gathered(
        acc,
        [
            ([over], (0, 2, 0)),
            ([across_up], (1, -1, 0)),
            ([across_down], (1, 1, 0)),
            ([twin(over)], (0, 2, 1)),
            ([twin(across_up)], (1, -1, 1)),
            ([twin(across_down)], (1, 1, 1)),
        ],
    )
    last[0], last[1], acc = lax.optimization_barrier((last[0], last[1], acc))
    placed = gathered(
        acc,
        [(last, (1, 2, 0)), ([twin(b) for b in last], (1, 2, 1))],
        last=True,
        out=placing,
    )
    pre = across(mine, w_self) + across(exchange(placed), w_neigh)
    filled = jnp.sum((part_map[0] == column).astype(jnp.int32)) * TILE
    row = lax.broadcasted_iota(jnp.int32, (capacity * TILE, 1), 0)
    hidden = jnp.where(row < filled, jnp.maximum(pre + bias[None, :], 0.0), 0.0)
    return hidden.astype(jnp.bfloat16)[None, None]


def solution(mesh):
    placed = (
        P("blk", "bal"),
        P("blk", None, None, None, None),
        P("blk", None, None),
        P("blk", None, None),
        P("blk", None),
        P(),
        P(),
        P(),
        P("blk", None),
    )
    return jax.shard_map(
        on_device,
        mesh=mesh,
        in_specs=placed,
        out_specs=P("blk", "bal", None, None),
        check_vma=False,
    )
```

time: 143 us -> 130 us (0.909)
  waiting for transfers between devices: 25.7 us -> 43 us
  Pallas kernels: 52 us -> 38.5 us
  starting transfers between devices: 39.9 us -> 28.7 us
  matrix products: 13.6 us -> 8.88 us
  local copies, waits for them, and re-layouts: 8.66 us -> 6.45 us
  other arithmetic: 0.64 us -> 2.69 us
    all_to_all x3 -> x2, waiting for transfers between devices: 6.2 us -> 22.4 us  [exchange(): got = lax.all_to_all(placed, 'bal', split_axis=0, concat_axis=0, tiled=True)]
    pallas_call x5 -> x4, Pallas kernels: 48.6 us -> 35.4 us  [accumulate(): pl.pallas_call(functools.partial(gather_kernel, layout, tuple(offsets), h...]
    ppermute x23 -> x17, starting transfers between devices: 24.3 us -> 18.5 us  [route(): return lax.ppermute(block, 'blk', pairs)]
    all_to_all x3 -> x2, starting transfers between devices: 15.6 us -> 10.1 us  [exchange(): got = lax.all_to_all(placed, 'bal', split_axis=0, concat_axis=0, tiled=True)]
    dot_general x3 -> x2, matrix products: 13.6 us -> 8.88 us  [across(): lax.dot_general(left, right, (((0,), (0,)), ((), ())), preferred_element_...]
    slice x4 -> x2, local copies, waits for them, and re-layouts: 7.05 us -> 3.82 us  [the longest x1 1.93 us: on_device(): across_up[:half]]
    concatenate x0 -> x2, other arithmetic: none -> 2.05 us  [the longest x1 1.26 us: on_device(): jnp.concatenate([fit(table), fit(part_map.astype(jnp.int32))], axis=0)]
    ppermute x23 -> x17, waiting for transfers between devices: 19.6 us -> 20.7 us  [route(): return lax.ppermute(block, 'blk', pairs)]
  transfers between devices with their start and end apart: 26 -> 19, of which waited for: 10 -> 9; matrix products, arithmetic and copies ran while one was open for 11% -> 8% of each run, Pallas kernels for 37% -> 30%
where the time goes in v3:
time: 130 us; the launch traced here: 129 us
  waiting for transfers between devices  43 us (33%)
  Pallas kernels  38.5 us (30%)
  starting transfers between devices  28.7 us (22%)
  matrix products  8.88 us (7%)
  local copies, waits for them, and re-layouts  6.45 us (5%)
  other arithmetic  2.69 us (2%)
    pallas_call x4, Pallas kernels, accumulate(): pl.pallas_call(functools.partial(gather_kernel, layout, tuple(offsets), h...  35.4 us
    all_to_all x2, waiting for transfers between devices, exchange(): got = lax.all_to_all(placed, 'bal', split_axis=0, concat_axis=0, tiled=True)  22.4 us
    ppermute x17, waiting for transfers between devices, route(): return lax.ppermute(block, 'blk', pairs)  20.7 us
    ppermute x17, starting transfers between devices, route(): return lax.ppermute(block, 'blk', pairs)  18.5 us
    all_to_all x2, starting transfers between devices, exchange(): got = lax.all_to_all(placed, 'bal', split_axis=0, concat_axis=0, tiled=True)  10.1 us
    dot_general x2, matrix products, across(): lax.dot_general(left, right, (((0,), (0,)), ((), ())), preferred_element_...  8.88 us
    pallas_call x1, Pallas kernels, place_features(): pl.pallas_call(place_kernel, in_specs=[pl.BlockSpec(memory_space=pltpu.SM...  3.13 us
  transfers between devices with their start and end apart: 19, of which 9 were waited for; matrix products, arithmetic and copies ran while one was open for 8% of the time, Pallas kernels for 30%

profile of v3, /device:TPU:1, one launch (start us, length us, event | category | flops | bytes accessed | tf_op | source)
XLA Modules:
  0.0 129.0 jit_solution(10399274826539818003)
XLA Ops:
  0.0 1.4 %collective-permute-start.3 = (bf16[64,8192]{1,0:T(8,128)(2,1)}, bf16[64,8192]{1,0:T(8,128)(2,1)S(1)}, u32[]{:S(2)}, u32[]{:S(2)}) collective-permute-start(bf16[64,8192]{1,0:T(8,128)(2,1)} %bitcast.19), channel_id=1, source_target_pairs={{0,8},{8,0},{16,24},{24,16},{32,40},{40,32},{48,56},{56,48},{64,72... | collective-permute-start | bytes 3145736 | tf_op jit(solution)/shard_map/ppermute | solution.py:26
  1.4 2.8 %collective-permute-start = (bf16[64,8192]{1,0:T(8,128)(2,1)}, bf16[64,8192]{1,0:T(8,128)(2,1)}, u32[]{:S(2)}, u32[]{:S(2)}) collective-permute-start(bf16[64,8192]{1,0:T(8,128)(2,1)} %bitcast.20), channel_id=1, source_target_pairs={{0,64},{8,72},{16,80},{24,88},{32,96},{40,104},{48,112},{56,120},{... | collective-permute-start | bytes 3145736 | tf_op jit(solution)/shard_map/ppermute | solution.py:26
  4.3 1.3 %collective-permute-start.1 = (bf16[64,8192]{1,0:T(8,128)(2,1)}, bf16[64,8192]{1,0:T(8,128)(2,1)}, u32[]{:S(2)}, u32[]{:S(2)}) collective-permute-start(bf16[64,8192]{1,0:T(8,128)(2,1)} %bitcast.21), channel_id=1, source_target_pairs={{0,16},{8,24},{16,32},{24,40},{32,48},{40,56},{48,0},{56,8},{64,80... | collective-permute-start | bytes 3145736 | tf_op jit(solution)/shard_map/ppermute | solution.py:26
  5.6 1.4 %collective-permute-start.2 = (bf16[64,8192]{1,0:T(8,128)(2,1)}, bf16[64,8192]{1,0:T(8,128)(2,1)}, u32[]{:S(2)}, u32[]{:S(2)}) collective-permute-start(bf16[64,8192]{1,0:T(8,128)(2,1)} %bitcast.22), channel_id=1, source_target_pairs={{0,48},{8,56},{16,0},{24,8},{32,16},{40,24},{48,32},{56,40},{64,11... | collective-permute-start | bytes 3145736 | tf_op jit(solution)/shard_map/ppermute | solution.py:26
  9.9 3.1 %place_features.1 = bf16[8,64,2048]{2,1,0:T(8,128)(2,1)} custom-call(s32[17,128]{1,0:T(8,128)} %pad_add_fusion.mapping.table, bf16[64,8192]{1,0:T(8,128)(2,1)} %bitcast.23), custom_call_target="tpu_custom_call" | custom-call | bytes 8388608 | tf_op jit(solution)/shard_map/place_features/pallas_call | solution.py:212
  14.0 6.8 %aggregate.3.refs_7_ = f32[64,80,128]{2,1,0:T(8,128)} custom-call(s32[17,128]{1,0:T(8,128)} %pad_add_fusion.mapping.table, bf16[16,32,128,128]{3,2,1,0:T(8,128)(2,1)} %bitcast.14, bf16[64,8192]{1,0:T(8,128)(2,1)} %bitcast.24, bf16[64,8192]{1,0:T(8,128)(2,1)} %copy-done.1), custom_call_target="tpu_custom_call" | custom-call | bytes 14680064 | tf_op jit(solution)/shard_map/aggregate/pallas_call | solution.py:174
  20.8 7.3 %collective-permute-done.refs_1_ = bf16[64,8192]{1,0:T(8,128)(2,1)} collective-permute-done((bf16[64,8192]{1,0:T(8,128)(2,1)}, bf16[64,8192]{1,0:T(8,128)(2,1)}, u32[]{:S(2)}, u32[]{:S(2)}) %collective-permute-start) | collective-permute-done | bytes 1048608 | tf_op jit(solution)/shard_map/ppermute | solution.py:26
  28.0 2.4 %collective-permute-done.1.refs_2_ = bf16[64,8192]{1,0:T(8,128)(2,1)} collective-permute-done((bf16[64,8192]{1,0:T(8,128)(2,1)}, bf16[64,8192]{1,0:T(8,128)(2,1)}, u32[]{:S(2)}, u32[]{:S(2)}) %collective-permute-start.1) | collective-permute-done | bytes 1048608 | tf_op jit(solution)/shard_map/ppermute | solution.py:26
  32.2 1.3 %collective-permute-start.5 = (bf16[64,8192]{1,0:T(8,128)(2,1)}, bf16[64,8192]{1,0:T(8,128)(2,1)}, u32[]{:S(2)}, u32[]{:S(2)}) collective-permute-start(bf16[64,8192]{1,0:T(8,128)(2,1)} %collective-permute-done.1.refs_2_), channel_id=1, source_target_pairs={{0,16},{8,24},{16,32},{24,40},{32,48},{40,56},{48,0},{56,8},{64,80... | collective-permute-start | bytes 3145736 | tf_op jit(solution)/shard_map/ppermute | solution.py:26
  34.1 2.6 %collective-permute-start.6 = (bf16[64,8192]{1,0:T(8,128)(2,1)}, bf16[64,8192]{1,0:T(8,128)(2,1)}, u32[]{:S(2)}, u32[]{:S(2)}) collective-permute-start(bf16[64,8192]{1,0:T(8,128)(2,1)} %collective-permute-done.refs_1_), channel_id=1, source_target_pairs={{0,48},{8,56},{16,0},{24,8},{32,16},{40,24},{48,32},{56,40},{64,11... | collective-permute-start | bytes 3145736 | tf_op jit(solution)/shard_map/ppermute | solution.py:26
  36.7 5.1 %all-to-all-start = ((bf16[8,64,2048]{2,1,0:T(8,128)(2,1)}), bf16[8,64,2048]{2,1,0:T(8,128)(2,1)S(1)}, u32[]{:S(2)}, u32[]{:S(2)}) async-start(bf16[8,64,2048]{2,1,0:T(8,128)(2,1)} %place_features.1), calls=%async_computation | async-start | bytes 4194304 | tf_op jit(solution)/shard_map/all_to_all | solution.py:228
  41.8 10.7 %aggregate.4.refs_7_ = f32[64,80,128]{2,1,0:T(8,128)} custom-call(s32[17,128]{1,0:T(8,128)} %pad_add_fusion.mapping.table, bf16[16,32,128,128]{3,2,1,0:T(8,128)(2,1)} %bitcast.15, bf16[64,8192]{1,0:T(8,128)(2,1)} %collective-permute-done.refs_1_, bf16[64,8192]{1,0:T(8,128)(2,1)} %collective-permute-done.1.refs_2_, ...), custom_call_target="tpu_custom_call" | custom-call | bytes 27262976 | tf_op jit(solution)/shard_map/aggregate/pallas_call | solution.py:174
  52.6 6.0 %collective-permute-done.4.refs_2_ = bf16[64,8192]{1,0:T(8,128)(2,1)} collective-permute-done((bf16[64,8192]{1,0:T(8,128)(2,1)}, bf16[64,8192]{1,0:T(8,128)(2,1)}, u32[]{:S(2)}, u32[]{:S(2)}) %collective-permute-start.4) | collective-permute-done | bytes 1048608 | tf_op jit(solution)/shard_map/ppermute | solution.py:26
  60.9 1.9 %slice.6 = bf16[32,8192]{1,0:T(8,128)(2,1)} slice(bf16[64,8192]{1,0:T(8,128)(2,1)} %collective-permute-done.4.refs_2_), slice={[0:32], [0:8192]} | slice | bytes 1048576 | tf_op jit(solution)/shard_map/slice | solution.py:289
  62.9 1.9 %slice.7 = bf16[32,8192]{1,0:T(8,128)(2,1)} slice(bf16[64,8192]{1,0:T(8,128)(2,1)} %collective-permute-done.6.refs_3_), slice={[32:64], [0:8192]} | slice | bytes 1048576 | tf_op jit(solution)/shard_map/slice | solution.py:289
  65.6 2.6 %collective-permute-start.11 = (bf16[32,8192]{1,0:T(8,128)(2,1)}, bf16[32,8192]{1,0:T(8,128)(2,1)}, u32[]{:S(2)}, u32[]{:S(2)}) collective-permute-start(bf16[32,8192]{1,0:T(8,128)(2,1)} %slice.7), channel_id=1, source_target_pairs={{0,48},{8,56},{16,0},{24,8},{32,16},{40,24},{48,32},{56,40},{64,11... | collective-permute-start | bytes 1572872 | tf_op jit(solution)/shard_map/ppermute | solution.py:26
  68.2 10.5 %aggregate.5.refs_5_ = f32[64,80,128]{2,1,0:T(8,128)} custom-call(s32[17,128]{1,0:T(8,128)} %pad_add_fusion.mapping.table, bf16[16,32,128,128]{3,2,1,0:T(8,128)(2,1)} %bitcast.16, bf16[64,8192]{1,0:T(8,128)(2,1)} %collective-permute-done.5.refs_1_, bf16[64,8192]{1,0:T(8,128)(2,1)} %collective-permute-done.4.refs_2_, ...), custom_call_target="tpu_custom_call" | custom-call | bytes 27262976 | tf_op jit(solution)/shard_map/aggregate/pallas_call | solution.py:174
  78.7 2.0 %collective-permute-done.10.refs_1_ = bf16[32,8192]{1,0:T(8,128)(2,1)S(1)} collective-permute-done((bf16[32,8192]{1,0:T(8,128)(2,1)}, bf16[32,8192]{1,0:T(8,128)(2,1)S(1)}, u32[]{:S(2)}, u32[]{:S(2)}) %collective-permute-start.10) | collective-permute-done | bytes 524320 | tf_op jit(solution)/shard_map/ppermute | solution.py:26
  81.3 1.5 %collective-permute-done.15.refs_3_ = bf16[32,8192]{1,0:T(8,128)(2,1)S(1)} collective-permute-done((bf16[32,8192]{1,0:T(8,128)(2,1)S(1)}, bf16[32,8192]{1,0:T(8,128)(2,1)S(1)}, u32[]{:S(2)}, u32[]{:S(2)}) %collective-permute-start.15) | collective-permute-done | bytes 524320 | tf_op jit(solution)/shard_map/ppermute | solution.py:26
  83.9 7.4 %aggregate_last.1 = bf16[8,64,2048]{2,1,0:T(8,128)(2,1)} custom-call(s32[17,128]{1,0:T(8,128)} %pad_add_fusion.mapping.table, bf16[16,32,128,128]{3,2,1,0:T(8,128)(2,1)} %bitcast.17, bf16[32,8192]{1,0:T(8,128)(2,1)} %copy-done.2, bf16[32,8192]{1,0:T(8,128)(2,1)} %collective-permute-done.11.refs_2_, bf16[32,8192]{1,0:T(8,128)(2,1)} %copy-done.3, ...), custom_call_target="tpu_custom_call" | custom-call | bytes 14680064 | tf_op jit(solution)/shard_map/aggregate_last/pallas_call | solution.py:174
  91.3 5.1 %all-to-all-start.1 = ((bf16[8,64,2048]{2,1,0:T(8,128)(2,1)}), bf16[8,64,2048]{2,1,0:T(8,128)(2,1)}, u32[]{:S(2)}, u32[]{:S(2)}) async-start(bf16[8,64,2048]{2,1,0:T(8,128)(2,1)} %aggregate_last.1), calls=%async_computation.1 | async-start | bytes 4194304 | tf_op jit(solution)/shard_map/all_to_all | solution.py:228
  97.7 3.2 %fusion.2 = f32[2048,512]{1,0:T(8,128)} fusion(bf16[512,2048]{1,0:T(8,128)(2,1)S(1)} %bitcast.18, bf16[512,512]{1,0:T(8,128)(2,1)S(1)} %copy-done), kind=kOutput, calls=%fused_computation.7 | convolution fusion | flops 1073741824 | bytes 6815744 | tf_op jit(solution)/shard_map/dot_general | solution.py:233
  100.9 22.4 %all-to-all-done.1 = bf16[8,64,2048]{2,1,0:T(8,128)(2,1)} async-done(((bf16[8,64,2048]{2,1,0:T(8,128)(2,1)}), bf16[8,64,2048]{2,1,0:T(8,128)(2,1)}, u32[]{:S(2)}, u32[]{:S(2)}) %all-to-all-start.1) | async-done | bytes 2097184 | tf_op jit(solution)/shard_map/all_to_all | solution.py:228
  123.3 5.6 %fusion = bf16[1,1,2048,512]{3,2,1,0:T(8,128)(2,1)} fusion(f32[2048,512]{1,0:T(8,128)} %fusion.2, bf16[512,2048]{1,0:T(8,128)(2,1)} %bitcast.6, bf16[512,512]{1,0:T(8,128)(2,1)S(1)} %copy-done.5, f32[512]{0:T(512)S(1)} %copy-done.6, pred[2048]{0:T(1024)(128)(4,1)S(1)} %iota_compare_fusion), kind=kOutput, calls=%fused_computation.1 | convolution fusion | flops 1078984704 | bytes 8916992 | tf_op jit(solution)/shard_map/dot_general | solution.py:233
  (43 shorter events, 11.9 us)
Async XLA Ops:
  0.0 97.7 %copy-start = (bf16[512,512]{1,0:T(8,128)(2,1)S(1)}, bf16[512,512]{1,0:T(8,128)(2,1)}, u32[]{:S(2)}) copy-start(bf16[512,512]{1,0:T(8,128)(2,1)} %param.14) | copy-start | bytes 1572868
  0.0 13.0 %collective-permute-start.3 = (bf16[64,8192]{1,0:T(8,128)(2,1)}, bf16[64,8192]{1,0:T(8,128)(2,1)S(1)}, u32[]{:S(2)}, u32[]{:S(2)}) collective-permute-start(bf16[64,8192]{1,0:T(8,128)(2,1)} %bitcast.19), channel_id=1, source_target_pairs={{0,8},{8,0},{16,24},{24,16},{32,40},{40,32},{48,56},{56,48},{64,72... | collective-permute-start | bytes 3145736 | tf_op jit(solution)/shard_map/ppermute | solution.py:26
  1.4 26.6 %collective-permute-start = (bf16[64,8192]{1,0:T(8,128)(2,1)}, bf16[64,8192]{1,0:T(8,128)(2,1)}, u32[]{:S(2)}, u32[]{:S(2)}) collective-permute-start(bf16[64,8192]{1,0:T(8,128)(2,1)} %bitcast.20), channel_id=1, source_target_pairs={{0,64},{8,72},{16,80},{24,88},{32,96},{40,104},{48,112},{56,120},{... | collective-permute-start | bytes 3145736 | tf_op jit(solution)/shard_map/ppermute | solution.py:26
  4.3 26.1 %collective-permute-start.1 = (bf16[64,8192]{1,0:T(8,128)(2,1)}, bf16[64,8192]{1,0:T(8,128)(2,1)}, u32[]{:S(2)}, u32[]{:S(2)}) collective-permute-start(bf16[64,8192]{1,0:T(8,128)(2,1)} %bitcast.21), channel_id=1, source_target_pairs={{0,16},{8,24},{16,32},{24,40},{32,48},{40,56},{48,0},{56,8},{64,80... | collective-permute-start | bytes 3145736 | tf_op jit(solution)/shard_map/ppermute | solution.py:26
  5.6 24.8 %collective-permute-start.2 = (bf16[64,8192]{1,0:T(8,128)(2,1)}, bf16[64,8192]{1,0:T(8,128)(2,1)}, u32[]{:S(2)}, u32[]{:S(2)}) collective-permute-start(bf16[64,8192]{1,0:T(8,128)(2,1)} %bitcast.22), channel_id=1, source_target_pairs={{0,48},{8,56},{16,0},{24,8},{32,16},{40,24},{48,32},{56,40},{64,11... | collective-permute-start | bytes 3145736 | tf_op jit(solution)/shard_map/ppermute | solution.py:26
  30.4 3.7 %collective-permute-start.8 = (bf16[64,8192]{1,0:T(8,128)(2,1)}, bf16[64,8192]{1,0:T(8,128)(2,1)}, u32[]{:S(2)}, u32[]{:S(2)}) collective-permute-start(bf16[64,8192]{1,0:T(8,128)(2,1)} %collective-permute-done.1.refs_2_), channel_id=1, source_target_pairs={{0,8},{8,0},{16,24},{24,16},{32,40},{40,32},{48,56},{56,48},{64,72... | collective-permute-start | bytes 3145736 | tf_op jit(solution)/shard_map/ppermute | solution.py:26
  31.5 10.3 %collective-permute-start.7 = (bf16[64,8192]{1,0:T(8,128)(2,1)}, bf16[64,8192]{1,0:T(8,128)(2,1)}, u32[]{:S(2)}, u32[]{:S(2)}) collective-permute-start(bf16[64,8192]{1,0:T(8,128)(2,1)} %collective-permute-done.refs_1_), channel_id=1, source_target_pairs={{0,8},{8,0},{16,24},{24,16},{32,40},{40,32},{48,56},{56,48},{64,72... | collective-permute-start | bytes 3145736 | tf_op jit(solution)/shard_map/ppermute | solution.py:26
  31.5 10.3 %collective-permute-start.9 = (bf16[64,8192]{1,0:T(8,128)(2,1)}, bf16[64,8192]{1,0:T(8,128)(2,1)}, u32[]{:S(2)}, u32[]{:S(2)}) collective-permute-start(bf16[64,8192]{1,0:T(8,128)(2,1)} %collective-permute-done.2.refs_3_), channel_id=1, source_target_pairs={{0,8},{8,0},{16,24},{24,16},{32,40},{40,32},{48,56},{56,48},{64,72... | collective-permute-start | bytes 3145736 | tf_op jit(solution)/shard_map/ppermute | solution.py:26
  32.0 26.6 %collective-permute-start.4 = (bf16[64,8192]{1,0:T(8,128)(2,1)}, bf16[64,8192]{1,0:T(8,128)(2,1)}, u32[]{:S(2)}, u32[]{:S(2)}) collective-permute-start(bf16[64,8192]{1,0:T(8,128)(2,1)} %collective-permute-done.1.refs_2_), channel_id=1, source_target_pairs={{0,64},{8,72},{16,80},{24,88},{32,96},{40,104},{48,112},{56,120},{... | collective-permute-start | bytes 3145736 | tf_op jit(solution)/shard_map/ppermute | solution.py:26
  32.2 26.4 %collective-permute-start.5 = (bf16[64,8192]{1,0:T(8,128)(2,1)}, bf16[64,8192]{1,0:T(8,128)(2,1)}, u32[]{:S(2)}, u32[]{:S(2)}) collective-permute-start(bf16[64,8192]{1,0:T(8,128)(2,1)} %collective-permute-done.1.refs_2_), channel_id=1, source_target_pairs={{0,16},{8,24},{16,32},{24,40},{32,48},{40,56},{48,0},{56,8},{64,80... | collective-permute-start | bytes 3145736 | tf_op jit(solution)/shard_map/ppermute | solution.py:26
  34.1 25.1 %collective-permute-start.6 = (bf16[64,8192]{1,0:T(8,128)(2,1)}, bf16[64,8192]{1,0:T(8,128)(2,1)}, u32[]{:S(2)}, u32[]{:S(2)}) collective-permute-start(bf16[64,8192]{1,0:T(8,128)(2,1)} %collective-permute-done.refs_1_), channel_id=1, source_target_pairs={{0,48},{8,56},{16,0},{24,8},{32,16},{40,24},{48,32},{56,40},{64,11... | collective-permute-start | bytes 3145736 | tf_op jit(solution)/shard_map/ppermute | solution.py:26
  36.7 54.6 %all-to-all-start = ((bf16[8,64,2048]{2,1,0:T(8,128)(2,1)}), bf16[8,64,2048]{2,1,0:T(8,128)(2,1)S(1)}, u32[]{:S(2)}, u32[]{:S(2)}) async-start(bf16[8,64,2048]{2,1,0:T(8,128)(2,1)} %place_features.1), calls=%async_computation | async-start | bytes 4194304 | tf_op jit(solution)/shard_map/all_to_all | solution.py:228
  59.2 8.9 %collective-permute-start.12 = (bf16[64,8192]{1,0:T(8,128)(2,1)}, bf16[64,8192]{1,0:T(8,128)(2,1)}, u32[]{:S(2)}, u32[]{:S(2)}) collective-permute-start(bf16[64,8192]{1,0:T(8,128)(2,1)} %collective-permute-done.5.refs_1_), channel_id=1, source_target_pairs={{0,8},{8,0},{16,24},{24,16},{32,40},{40,32},{48,56},{56,48},{64,72... | collective-permute-start | bytes 3145736 | tf_op jit(solution)/shard_map/ppermute | solution.py:26
  60.4 7.8 %collective-permute-start.13 = (bf16[64,8192]{1,0:T(8,128)(2,1)}, bf16[64,8192]{1,0:T(8,128)(2,1)}, u32[]{:S(2)}, u32[]{:S(2)}) collective-permute-start(bf16[64,8192]{1,0:T(8,128)(2,1)} %collective-permute-done.4.refs_2_), channel_id=1, source_target_pairs={{0,8},{8,0},{16,24},{24,16},{32,40},{40,32},{48,56},{56,48},{64,72... | collective-permute-start | bytes 3145736 | tf_op jit(solution)/shard_map/ppermute | solution.py:26
  60.4 7.8 %collective-permute-start.14 = (bf16[64,8192]{1,0:T(8,128)(2,1)}, bf16[64,8192]{1,0:T(8,128)(2,1)}, u32[]{:S(2)}, u32[]{:S(2)}) collective-permute-start(bf16[64,8192]{1,0:T(8,128)(2,1)} %collective-permute-done.6.refs_3_), channel_id=1, source_target_pairs={{0,8},{8,0},{16,24},{24,16},{32,40},{40,32},{48,56},{56,48},{64,72... | collective-permute-start | bytes 3145736 | tf_op jit(solution)/shard_map/ppermute | solution.py:26
  64.8 15.9 %collective-permute-start.10 = (bf16[32,8192]{1,0:T(8,128)(2,1)}, bf16[32,8192]{1,0:T(8,128)(2,1)S(1)}, u32[]{:S(2)}, u32[]{:S(2)}) collective-permute-start(bf16[32,8192]{1,0:T(8,128)(2,1)} %slice.6), channel_id=1, source_target_pairs={{0,16},{8,24},{16,32},{24,40},{32,48},{40,56},{48,0},{56,8},{64,80... | collective-permute-start | bytes 1572872 | tf_op jit(solution)/shard_map/ppermute | solution.py:26
  65.6 15.1 %collective-permute-start.11 = (bf16[32,8192]{1,0:T(8,128)(2,1)}, bf16[32,8192]{1,0:T(8,128)(2,1)}, u32[]{:S(2)}, u32[]{:S(2)}) collective-permute-start(bf16[32,8192]{1,0:T(8,128)(2,1)} %slice.7), channel_id=1, source_target_pairs={{0,48},{8,56},{16,0},{24,8},{32,16},{40,24},{48,32},{56,40},{64,11... | collective-permute-start | bytes 1572872 | tf_op jit(solution)/shard_map/ppermute | solution.py:26
  80.7 3.2 %copy-start.2 = (bf16[32,8192]{1,0:T(8,128)(2,1)}, bf16[32,8192]{1,0:T(8,128)(2,1)S(1)}, u32[]{:S(2)}) copy-start(bf16[32,8192]{1,0:T(8,128)(2,1)S(1)} %collective-permute-done.10.refs_1_) | copy-start | bytes 1572868
  80.7 2.1 %collective-permute-start.15 = (bf16[32,8192]{1,0:T(8,128)(2,1)S(1)}, bf16[32,8192]{1,0:T(8,128)(2,1)S(1)}, u32[]{:S(2)}, u32[]{:S(2)}) collective-permute-start(bf16[32,8192]{1,0:T(8,128)(2,1)S(1)} %collective-permute-done.10.refs_1_), channel_id=1, source_target_pairs={{0,8},{8,0},{16,24},{24,16},{32,40},{40,32},{48,56},{56,48},{64,72... | collective-permute-start | bytes 1572872 | tf_op jit(solution)/shard_map/ppermute | solution.py:26
  81.3 2.6 %collective-permute-start.16 = (bf16[32,8192]{1,0:T(8,128)(2,1)}, bf16[32,8192]{1,0:T(8,128)(2,1)}, u32[]{:S(2)}, u32[]{:S(2)}) collective-permute-start(bf16[32,8192]{1,0:T(8,128)(2,1)} %collective-permute-done.11.refs_2_), channel_id=1, source_target_pairs={{0,8},{8,0},{16,24},{24,16},{32,40},{40,32},{48,56},{56,48},{64,72... | collective-permute-start | bytes 1572872 | tf_op jit(solution)/shard_map/ppermute | solution.py:26
  91.3 5.1 %copy-start.4 = (s32[1,64]{1,0:T(1,128)S(1)}, s32[1,64]{1,0:T(1,128)}, u32[]{:S(2)}) copy-start(s32[1,64]{1,0:T(1,128)} %param.17) | copy-start | bytes 772
  91.3 32.0 %all-to-all-start.1 = ((bf16[8,64,2048]{2,1,0:T(8,128)(2,1)}), bf16[8,64,2048]{2,1,0:T(8,128)(2,1)}, u32[]{:S(2)}, u32[]{:S(2)}) async-start(bf16[8,64,2048]{2,1,0:T(8,128)(2,1)} %aggregate_last.1), calls=%async_computation.1 | async-start | bytes 4194304 | tf_op jit(solution)/shard_map/all_to_all | solution.py:228
  97.7 25.6 %copy-start.5 = (bf16[512,512]{1,0:T(8,128)(2,1)S(1)}, bf16[512,512]{1,0:T(8,128)(2,1)}, u32[]{:S(2)}) copy-start(bf16[512,512]{1,0:T(8,128)(2,1)} %param.15) | copy-start | bytes 1572868
  97.7 25.6 %copy-start.6 = (f32[512]{0:T(512)S(1)}, f32[512]{0:T(512)}, u32[]{:S(2)}) copy-start(f32[512]{0:T(512)} %param.16) | copy-start | bytes 6148
  (2 other events, 1.8 us)

commit v4 on v3

--- a/solution.py
+++ b/solution.py
@@ -184,6 +184,43 @@
     )(*operands)
 
 
+def cut_kernel(up_ref, down_ref, *refs):
+    top_ref, bottom_ref, held, in_sem, out_sem = refs
+    rows = held.shape[1]
+    half = top_ref.shape[0]
+    loads, stores = [], []
+    for k in range(held.shape[0]):
+        at = k * rows
+        source, target = (up_ref, top_ref) if at < half else (down_ref, bottom_ref)
+        loads.append(
+            pltpu.make_async_copy(source.at[pl.ds(at, rows)], held.at[k], in_sem.at[k])
+        )
+        stores.append(
+            pltpu.make_async_copy(held.at[k], target.at[pl.ds(at % half, rows)], out_sem.at[k])
+        )
+    for copy in loads:
+        copy.start()
+    for load, store in zip(loads, stores):
+        load.wait()
+        store.start()
+    for copy in stores:
+        copy.wait()
+
+
+def cut(up, down):
+    anywhere = pl.BlockSpec(memory_space=pl.ANY)
+    piece = jax.ShapeDtypeStruct((up.shape[0] // 2, up.shape[1]), up.dtype)
+    return pl.pallas_call(
+        cut_kernel,
+        in_specs=[anywhere] * 2,
+        out_specs=[anywhere] * 2,
+        out_shape=[piece] * 2,
+        scratch_shapes=[pltpu.VMEM((4, up.shape[0] // 4, up.shape[1]), up.dtype)]
+        + [pltpu.SemaphoreType.DMA((4,))] * 2,
+        name="cut",
+    )(up, down)
+
+
 def place_into(out_ref, mapping, used, tiles_per, tile_of):
     n_bal = out_ref.shape[0]
     out_ref[...] = jnp.zeros_like(out_ref)
@@ -245,7 +282,6 @@
     tiles_per = part_map.shape[1]
     capacity = 2 * tiles_per // n_bal
     width = features.shape[1]
-    half = width // 2
     values = tile_values[0]
     table = jnp.concatenate(
         [tile_rows[0], tile_cols[0], tile_counts[0][:, None], jnp.full((n_blk, 1), here)], axis=1
@@ -286,7 +322,8 @@
     across_up, over, across_down, acc = lax.optimization_barrier(
         (across_up, over, across_down, acc)
     )
-    last = [route(across_up[:half], 0, 1, 0), route(across_down[half:], 0, -1, 0)]
+    top, bottom = cut(across_up, across_down)
+    last = [route(top, 0, 1, 0), route(bottom, 0, -1, 0)]
     acc = gathered(
         acc,
         [
@@ -305,7 +342,8 @@
         last=True,
         out=placing,
     )
-    pre = across(mine, w_self) + across(exchange(placed), w_neigh)
+    means, mine = lax.optimization_barrier((exchange(placed), mine))
+    pre = across(means, w_neigh) + across(mine, w_self)
     filled = jnp.sum((part_map[0] == column).astype(jnp.int32)) * TILE
     row = lax.broadcasted_iota(jnp.int32, (capacity * TILE, 1), 0)
     hidden = jnp.where(row < filled, jnp.maximum(pre + bias[None, :], 0.0), 0.0)

time: 130 us -> 129 us (level)
  local copies, waits for them, and re-layouts: 6.45 us -> 2.61 us
  Pallas kernels: 38.5 us -> 41.8 us
  matrix products: 8.88 us -> 5.82 us
  waiting for transfers between devices: 43 us -> 45.8 us
    slice x2 -> x0, local copies, waits for them, and re-layouts: 3.82 us -> none  [the longest x1 1.93 us: on_device(): across_up[:half]]
    dot_general x2, matrix products: 8.88 us -> 5.82 us  [across(): lax.dot_general(left, right, (((0,), (0,)), ((), ())), preferred_element_...]
    all_to_all x2, waiting for transfers between devices: 22.4 us -> 25 us  [exchange(): got = lax.all_to_all(placed, 'bal', split_axis=0, concat_axis=0, tiled=True)]
    pallas_call x0 -> x1, Pallas kernels: none -> 2.01 us  [cut(): pl.pallas_call(cut_kernel, in_specs=[anywhere] * 2, out_specs=[anywhere]...]
  transfers between devices with their start and end apart: 19 -> 19, of which waited for: 9 -> 8; matrix products, arithmetic and copies ran while one was open for 8% -> 3% of each run, Pallas kernels for 30% -> 33%
where the time goes in v4:
time: 129 us; the launch traced here: 128 us
  waiting for transfers between devices  45.8 us (36%)
  Pallas kernels  41.8 us (32%)
  starting transfers between devices  28.6 us (22%)
  matrix products  5.82 us (5%)
  other arithmetic  2.71 us (2%)
  local copies, waits for them, and re-layouts  2.61 us (2%)
    pallas_call x4, Pallas kernels, accumulate(): pl.pallas_call(functools.partial(gather_kernel, layout, tuple(offsets), h...  36.6 us
    all_to_all x2, waiting for transfers between devices, exchange(): got = lax.all_to_all(placed, 'bal', split_axis=0, concat_axis=0, tiled=True)  25 us
    ppermute x17, waiting for transfers between devices, route(): return lax.ppermute(block, 'blk', pairs)  20.8 us
    ppermute x17, starting transfers between devices, route(): return lax.ppermute(block, 'blk', pairs)  18.5 us
    all_to_all x2, starting transfers between devices, exchange(): got = lax.all_to_all(placed, 'bal', split_axis=0, concat_axis=0, tiled=True)  10.1 us
    dot_general x2, matrix products, across(): lax.dot_general(left, right, (((0,), (0,)), ((), ())), preferred_element_...  5.82 us
    pallas_call x1, Pallas kernels, place_features(): pl.pallas_call(place_kernel, in_specs=[pl.BlockSpec(memory_space=pltpu.SM...  3.14 us
  transfers between devices with their start and end apart: 19, of which 8 were waited for; matrix products, arithmetic and copies ran while one was open for 3% of the time, Pallas kernels for 33%

profile of v4, /device:TPU:1, one launch (start us, length us, event | category | flops | bytes accessed | tf_op | source)
XLA Modules:
  0.0 128.1 jit_solution(1425237410665628773)
XLA Ops:
  0.0 1.4 %collective-permute-start.3 = (bf16[64,8192]{1,0:T(8,128)(2,1)}, bf16[64,8192]{1,0:T(8,128)(2,1)S(1)}, u32[]{:S(2)}, u32[]{:S(2)}) collective-permute-start(bf16[64,8192]{1,0:T(8,128)(2,1)} %bitcast.19), channel_id=1, source_target_pairs={{0,8},{8,0},{16,24},{24,16},{32,40},{40,32},{48,56},{56,48},{64,72... | collective-permute-start | bytes 3145736 | tf_op jit(solution)/shard_map/ppermute | solution.py:26
  1.4 2.8 %collective-permute-start = (bf16[64,8192]{1,0:T(8,128)(2,1)}, bf16[64,8192]{1,0:T(8,128)(2,1)}, u32[]{:S(2)}, u32[]{:S(2)}) collective-permute-start(bf16[64,8192]{1,0:T(8,128)(2,1)} %bitcast.20), channel_id=1, source_target_pairs={{0,64},{8,72},{16,80},{24,88},{32,96},{40,104},{48,112},{56,120},{... | collective-permute-start | bytes 3145736 | tf_op jit(solution)/shard_map/ppermute | solution.py:26
  4.3 1.3 %collective-permute-start.1 = (bf16[64,8192]{1,0:T(8,128)(2,1)}, bf16[64,8192]{1,0:T(8,128)(2,1)}, u32[]{:S(2)}, u32[]{:S(2)}) collective-permute-start(bf16[64,8192]{1,0:T(8,128)(2,1)} %bitcast.21), channel_id=1, source_target_pairs={{0,16},{8,24},{16,32},{24,40},{32,48},{40,56},{48,0},{56,8},{64,80... | collective-permute-start | bytes 3145736 | tf_op jit(solution)/shard_map/ppermute | solution.py:26
  5.6 1.4 %collective-permute-start.2 = (bf16[64,8192]{1,0:T(8,128)(2,1)}, bf16[64,8192]{1,0:T(8,128)(2,1)}, u32[]{:S(2)}, u32[]{:S(2)}) collective-permute-start(bf16[64,8192]{1,0:T(8,128)(2,1)} %bitcast.22), channel_id=1, source_target_pairs={{0,48},{8,56},{16,0},{24,8},{32,16},{40,24},{48,32},{56,40},{64,11... | collective-permute-start | bytes 3145736 | tf_op jit(solution)/shard_map/ppermute | solution.py:26
  8.6 1.3 pad_add_fusion.mapping.table
  9.9 3.1 %place_features.1 = bf16[8,64,2048]{2,1,0:T(8,128)(2,1)} custom-call(s32[17,128]{1,0:T(8,128)} %pad_add_fusion.mapping.table, bf16[64,8192]{1,0:T(8,128)(2,1)} %bitcast.23), custom_call_target="tpu_custom_call" | custom-call | bytes 8388608 | tf_op jit(solution)/shard_map/place_features/pallas_call | solution.py:249
  14.0 5.6 %aggregate.3.refs_7_ = f32[64,80,128]{2,1,0:T(8,128)} custom-call(s32[17,128]{1,0:T(8,128)} %pad_add_fusion.mapping.table, bf16[16,32,128,128]{3,2,1,0:T(8,128)(2,1)} %bitcast.14, bf16[64,8192]{1,0:T(8,128)(2,1)} %bitcast.24, bf16[64,8192]{1,0:T(8,128)(2,1)} %copy-done.3), custom_call_target="tpu_custom_call" | custom-call | bytes 14680064 | tf_op jit(solution)/shard_map/aggregate/pallas_call | solution.py:174
  19.6 8.4 %collective-permute-done.refs_1_ = bf16[64,8192]{1,0:T(8,128)(2,1)} collective-permute-done((bf16[64,8192]{1,0:T(8,128)(2,1)}, bf16[64,8192]{1,0:T(8,128)(2,1)}, u32[]{:S(2)}, u32[]{:S(2)}) %collective-permute-start) | collective-permute-done | bytes 1048608 | tf_op jit(solution)/shard_map/ppermute | solution.py:26
  28.0 2.4 %collective-permute-done.1.refs_2_ = bf16[64,8192]{1,0:T(8,128)(2,1)} collective-permute-done((bf16[64,8192]{1,0:T(8,128)(2,1)}, bf16[64,8192]{1,0:T(8,128)(2,1)}, u32[]{:S(2)}, u32[]{:S(2)}) %collective-permute-start.1) | collective-permute-done | bytes 1048608 | tf_op jit(solution)/shard_map/ppermute | solution.py:26
  32.2 1.3 %collective-permute-start.5 = (bf16[64,8192]{1,0:T(8,128)(2,1)}, bf16[64,8192]{1,0:T(8,128)(2,1)}, u32[]{:S(2)}, u32[]{:S(2)}) collective-permute-start(bf16[64,8192]{1,0:T(8,128)(2,1)} %collective-permute-done.1.refs_2_), channel_id=1, source_target_pairs={{0,16},{8,24},{16,32},{24,40},{32,48},{40,56},{48,0},{56,8},{64,80... | collective-permute-start | bytes 3145736 | tf_op jit(solution)/shard_map/ppermute | solution.py:26
  34.1 2.6 %collective-permute-start.6 = (bf16[64,8192]{1,0:T(8,128)(2,1)}, bf16[64,8192]{1,0:T(8,128)(2,1)S(1)}, u32[]{:S(2)}, u32[]{:S(2)}) collective-permute-start(bf16[64,8192]{1,0:T(8,128)(2,1)} %collective-permute-done.refs_1_), channel_id=1, source_target_pairs={{0,48},{8,56},{16,0},{24,8},{32,16},{40,24},{48,32},{56,40},{64,11... | collective-permute-start | bytes 3145736 | tf_op jit(solution)/shard_map/ppermute | solution.py:26
  36.7 5.1 %all-to-all-start.1 = ((bf16[8,64,2048]{2,1,0:T(8,128)(2,1)}), bf16[8,64,2048]{2,1,0:T(8,128)(2,1)}, u32[]{:S(2)}, u32[]{:S(2)}) async-start(bf16[8,64,2048]{2,1,0:T(8,128)(2,1)} %place_features.1), calls=%async_computation.1 | async-start | bytes 4194304 | tf_op jit(solution)/shard_map/all_to_all | solution.py:265
  41.8 10.4 %aggregate.4.refs_7_ = f32[64,80,128]{2,1,0:T(8,128)} custom-call(s32[17,128]{1,0:T(8,128)} %pad_add_fusion.mapping.table, bf16[16,32,128,128]{3,2,1,0:T(8,128)(2,1)} %bitcast.15, bf16[64,8192]{1,0:T(8,128)(2,1)} %collective-permute-done.refs_1_, bf16[64,8192]{1,0:T(8,128)(2,1)} %collective-permute-done.1.refs_2_, ...), custom_call_target="tpu_custom_call" | custom-call | bytes 27262976 | tf_op jit(solution)/shard_map/aggregate/pallas_call | solution.py:174
  52.2 6.3 %collective-permute-done.4.up_ref.refs_2_ = bf16[64,8192]{1,0:T(8,128)(2,1)S(1)} collective-permute-done((bf16[64,8192]{1,0:T(8,128)(2,1)}, bf16[64,8192]{1,0:T(8,128)(2,1)S(1)}, u32[]{:S(2)}, u32[]{:S(2)}) %collective-permute-start.4) | collective-permute-done | bytes 1048608 | tf_op jit(solution)/shard_map/ppermute | solution.py:26
  59.2 1.2 collective-permute-start.12
  60.9 2.0 %cut.1 = (bf16[32,8192]{1,0:T(8,128)(2,1)}, bf16[32,8192]{1,0:T(8,128)(2,1)}) custom-call(bf16[64,8192]{1,0:T(8,128)(2,1)} %copy-done.1, bf16[64,8192]{1,0:T(8,128)(2,1)} %copy-done.2), custom_call_target="tpu_custom_call" | custom-call | tf_op jit(solution)/shard_map/cut/pallas_call | solution.py:213
  63.8 2.6 %collective-permute-start.11 = (bf16[32,8192]{1,0:T(8,128)(2,1)}, bf16[32,8192]{1,0:T(8,128)(2,1)}, u32[]{:S(2)}, u32[]{:S(2)}) collective-permute-start(bf16[32,8192]{1,0:T(8,128)(2,1)} %get-tuple-element.28), channel_id=1, source_target_pairs={{0,48},{8,56},{16,0},{24,8},{32,16},{40,24},{48,32},{56,40},{64,11... | collective-permute-start | bytes 1572872 | tf_op jit(solution)/shard_map/ppermute | solution.py:26
  66.4 12.6 %aggregate.5.refs_5_ = f32[64,80,128]{2,1,0:T(8,128)} custom-call(s32[17,128]{1,0:T(8,128)} %pad_add_fusion.mapping.table, bf16[16,32,128,128]{3,2,1,0:T(8,128)(2,1)} %bitcast.16, bf16[64,8192]{1,0:T(8,128)(2,1)} %collective-permute-done.5.refs_1_, bf16[64,8192]{1,0:T(8,128)(2,1)} %copy-done.1, bf16[64,8192]{1,0:T(8,128)(2,1)} %copy-done.2, ...), custom_call_target="tpu_custom_call" | custom-call | bytes 27262976 | tf_op jit(solution)/shard_map/aggregate/pallas_call | solution.py:174
  79.6 1.4 %collective-permute-done.15.refs_3_ = bf16[32,8192]{1,0:T(8,128)(2,1)S(1)} collective-permute-done((bf16[32,8192]{1,0:T(8,128)(2,1)S(1)}, bf16[32,8192]{1,0:T(8,128)(2,1)S(1)}, u32[]{:S(2)}, u32[]{:S(2)}) %collective-permute-start.15) | collective-permute-done | bytes 524320 | tf_op jit(solution)/shard_map/ppermute | solution.py:26
  82.8 8.0 %aggregate_last.1 = bf16[8,64,2048]{2,1,0:T(8,128)(2,1)} custom-call(s32[17,128]{1,0:T(8,128)} %pad_add_fusion.mapping.table, bf16[16,32,128,128]{3,2,1,0:T(8,128)(2,1)} %bitcast.17, bf16[32,8192]{1,0:T(8,128)(2,1)} %copy-done.4, bf16[32,8192]{1,0:T(8,128)(2,1)} %collective-permute-done.11.refs_2_, bf16[32,8192]{1,0:T(8,128)(2,1)} %copy-done.5, ...), custom_call_target="tpu_custom_call" | custom-call | bytes 14680064 | tf_op jit(solution)/shard_map/aggregate_last/pallas_call | solution.py:174
  90.9 5.1 %all-to-all-start = ((bf16[8,64,2048]{2,1,0:T(8,128)(2,1)}), bf16[8,64,2048]{2,1,0:T(8,128)(2,1)S(1)}, u32[]{:S(2)}, u32[]{:S(2)}) async-start(bf16[8,64,2048]{2,1,0:T(8,128)(2,1)} %aggregate_last.1), calls=%async_computation | async-start | bytes 4194304 | tf_op jit(solution)/shard_map/all_to_all | solution.py:265
  97.3 25.0 %all-to-all-done = bf16[8,64,2048]{2,1,0:T(8,128)(2,1)S(1)} async-done(((bf16[8,64,2048]{2,1,0:T(8,128)(2,1)}), bf16[8,64,2048]{2,1,0:T(8,128)(2,1)S(1)}, u32[]{:S(2)}, u32[]{:S(2)}) %all-to-all-start) | async-done | bytes 2097184 | tf_op jit(solution)/shard_map/all_to_all | solution.py:265
  122.2 1.3 %fusion.2 = f32[2048,512]{1,0:T(8,128)S(1)} fusion(bf16[512,2048]{1,0:T(8,128)(2,1)S(1)} %bitcast.18, bf16[512,512]{1,0:T(8,128)(2,1)S(1)} %copy-done), kind=kOutput, calls=%fused_computation.7 | convolution fusion | flops 1073741824 | bytes 6815744 | tf_op jit(solution)/shard_map/dot_general | solution.py:270
  123.6 4.5 %fusion = bf16[1,1,2048,512]{3,2,1,0:T(8,128)(2,1)} fusion(f32[2048,512]{1,0:T(8,128)S(1)} %fusion.2, bf16[512,2048]{1,0:T(8,128)(2,1)} %bitcast.6, bf16[512,512]{1,0:T(8,128)(2,1)S(1)} %copy-done.8, f32[512]{0:T(512)S(1)} %copy-done.9, pred[2048]{0:T(1024)(128)(4,1)S(1)} %iota_compare_fusion), kind=kOutput, calls=%fused_computation.1 | convolution fusion | flops 1078984704 | bytes 8916992 | tf_op jit(solution)/shard_map/dot_general | solution.py:270
  (48 shorter events, 10.1 us)
Async XLA Ops:
  0.0 122.2 %copy-start = (bf16[512,512]{1,0:T(8,128)(2,1)S(1)}, bf16[512,512]{1,0:T(8,128)(2,1)}, u32[]{:S(2)}) copy-start(bf16[512,512]{1,0:T(8,128)(2,1)} %param.15) | copy-start | bytes 1572868
  0.0 13.0 %collective-permute-start.3 = (bf16[64,8192]{1,0:T(8,128)(2,1)}, bf16[64,8192]{1,0:T(8,128)(2,1)S(1)}, u32[]{:S(2)}, u32[]{:S(2)}) collective-permute-start(bf16[64,8192]{1,0:T(8,128)(2,1)} %bitcast.19), channel_id=1, source_target_pairs={{0,8},{8,0},{16,24},{24,16},{32,40},{40,32},{48,56},{56,48},{64,72... | collective-permute-start | bytes 3145736 | tf_op jit(solution)/shard_map/ppermute | solution.py:26
  1.4 26.6 %collective-permute-start = (bf16[64,8192]{1,0:T(8,128)(2,1)}, bf16[64,8192]{1,0:T(8,128)(2,1)}, u32[]{:S(2)}, u32[]{:S(2)}) collective-permute-start(bf16[64,8192]{1,0:T(8,128)(2,1)} %bitcast.20), channel_id=1, source_target_pairs={{0,64},{8,72},{16,80},{24,88},{32,96},{40,104},{48,112},{56,120},{... | collective-permute-start | bytes 3145736 | tf_op jit(solution)/shard_map/ppermute | solution.py:26
  4.3 26.1 %collective-permute-start.1 = (bf16[64,8192]{1,0:T(8,128)(2,1)}, bf16[64,8192]{1,0:T(8,128)(2,1)}, u32[]{:S(2)}, u32[]{:S(2)}) collective-permute-start(bf16[64,8192]{1,0:T(8,128)(2,1)} %bitcast.21), channel_id=1, source_target_pairs={{0,16},{8,24},{16,32},{24,40},{32,48},{40,56},{48,0},{56,8},{64,80... | collective-permute-start | bytes 3145736 | tf_op jit(solution)/shard_map/ppermute | solution.py:26
  5.6 24.8 %collective-permute-start.2 = (bf16[64,8192]{1,0:T(8,128)(2,1)}, bf16[64,8192]{1,0:T(8,128)(2,1)}, u32[]{:S(2)}, u32[]{:S(2)}) collective-permute-start(bf16[64,8192]{1,0:T(8,128)(2,1)} %bitcast.22), channel_id=1, source_target_pairs={{0,48},{8,56},{16,0},{24,8},{32,16},{40,24},{48,32},{56,40},{64,11... | collective-permute-start | bytes 3145736 | tf_op jit(solution)/shard_map/ppermute | solution.py:26
  30.4 3.7 %collective-permute-start.8 = (bf16[64,8192]{1,0:T(8,128)(2,1)}, bf16[64,8192]{1,0:T(8,128)(2,1)}, u32[]{:S(2)}, u32[]{:S(2)}) collective-permute-start(bf16[64,8192]{1,0:T(8,128)(2,1)} %collective-permute-done.1.refs_2_), channel_id=1, source_target_pairs={{0,8},{8,0},{16,24},{24,16},{32,40},{40,32},{48,56},{56,48},{64,72... | collective-permute-start | bytes 3145736 | tf_op jit(solution)/shard_map/ppermute | solution.py:26
  31.5 10.3 %collective-permute-start.7 = (bf16[64,8192]{1,0:T(8,128)(2,1)}, bf16[64,8192]{1,0:T(8,128)(2,1)}, u32[]{:S(2)}, u32[]{:S(2)}) collective-permute-start(bf16[64,8192]{1,0:T(8,128)(2,1)} %collective-permute-done.refs_1_), channel_id=1, source_target_pairs={{0,8},{8,0},{16,24},{24,16},{32,40},{40,32},{48,56},{56,48},{64,72... | collective-permute-start | bytes 3145736 | tf_op jit(solution)/shard_map/ppermute | solution.py:26
  31.5 10.3 %collective-permute-start.9 = (bf16[64,8192]{1,0:T(8,128)(2,1)}, bf16[64,8192]{1,0:T(8,128)(2,1)}, u32[]{:S(2)}, u32[]{:S(2)}) collective-permute-start(bf16[64,8192]{1,0:T(8,128)(2,1)} %collective-permute-done.2.refs_3_), channel_id=1, source_target_pairs={{0,8},{8,0},{16,24},{24,16},{32,40},{40,32},{48,56},{56,48},{64,72... | collective-permute-start | bytes 3145736 | tf_op jit(solution)/shard_map/ppermute | solution.py:26
  32.0 26.5 %collective-permute-start.4 = (bf16[64,8192]{1,0:T(8,128)(2,1)}, bf16[64,8192]{1,0:T(8,128)(2,1)S(1)}, u32[]{:S(2)}, u32[]{:S(2)}) collective-permute-start(bf16[64,8192]{1,0:T(8,128)(2,1)} %collective-permute-done.1.refs_2_), channel_id=1, source_target_pairs={{0,64},{8,72},{16,80},{24,88},{32,96},{40,104},{48,112},{56,120},{... | collective-permute-start | bytes 3145736 | tf_op jit(solution)/shard_map/ppermute | solution.py:26
  32.2 26.3 %collective-permute-start.5 = (bf16[64,8192]{1,0:T(8,128)(2,1)}, bf16[64,8192]{1,0:T(8,128)(2,1)}, u32[]{:S(2)}, u32[]{:S(2)}) collective-permute-start(bf16[64,8192]{1,0:T(8,128)(2,1)} %collective-permute-done.1.refs_2_), channel_id=1, source_target_pairs={{0,16},{8,24},{16,32},{24,40},{32,48},{40,56},{48,0},{56,8},{64,80... | collective-permute-start | bytes 3145736 | tf_op jit(solution)/shard_map/ppermute | solution.py:26
  34.1 25.1 %collective-permute-start.6 = (bf16[64,8192]{1,0:T(8,128)(2,1)}, bf16[64,8192]{1,0:T(8,128)(2,1)S(1)}, u32[]{:S(2)}, u32[]{:S(2)}) collective-permute-start(bf16[64,8192]{1,0:T(8,128)(2,1)} %collective-permute-done.refs_1_), channel_id=1, source_target_pairs={{0,48},{8,56},{16,0},{24,8},{32,16},{40,24},{48,32},{56,40},{64,11... | collective-permute-start | bytes 3145736 | tf_op jit(solution)/shard_map/ppermute | solution.py:26
  36.7 54.1 %all-to-all-start.1 = ((bf16[8,64,2048]{2,1,0:T(8,128)(2,1)}), bf16[8,64,2048]{2,1,0:T(8,128)(2,1)}, u32[]{:S(2)}, u32[]{:S(2)}) async-start(bf16[8,64,2048]{2,1,0:T(8,128)(2,1)} %place_features.1), calls=%async_computation.1 | async-start | bytes 4194304 | tf_op jit(solution)/shard_map/all_to_all | solution.py:265
  58.5 2.5 %copy-start.1 = (bf16[64,8192]{1,0:T(8,128)(2,1)}, bf16[64,8192]{1,0:T(8,128)(2,1)S(1)}, u32[]{:S(2)}) copy-start(bf16[64,8192]{1,0:T(8,128)(2,1)S(1)} %collective-permute-done.4.up_ref.refs_2_) | copy-start | bytes 3145732
  59.2 1.7 %copy-start.2 = (bf16[64,8192]{1,0:T(8,128)(2,1)}, bf16[64,8192]{1,0:T(8,128)(2,1)S(1)}, u32[]{:S(2)}) copy-start(bf16[64,8192]{1,0:T(8,128)(2,1)S(1)} %collective-permute-done.6.down_ref.refs_3_) | copy-start | bytes 3145732
  59.2 7.2 %collective-permute-start.12 = (bf16[64,8192]{1,0:T(8,128)(2,1)}, bf16[64,8192]{1,0:T(8,128)(2,1)}, u32[]{:S(2)}, u32[]{:S(2)}) collective-permute-start(bf16[64,8192]{1,0:T(8,128)(2,1)} %collective-permute-done.5.refs_1_), channel_id=1, source_target_pairs={{0,8},{8,0},{16,24},{24,16},{32,40},{40,32},{48,56},{56,48},{64,72... | collective-permute-start | bytes 3145736 | tf_op jit(solution)/shard_map/ppermute | solution.py:26
  60.4 6.0 %collective-permute-start.13 = (bf16[64,8192]{1,0:T(8,128)(2,1)S(1)}, bf16[64,8192]{1,0:T(8,128)(2,1)}, u32[]{:S(2)}, u32[]{:S(2)}) collective-permute-start(bf16[64,8192]{1,0:T(8,128)(2,1)S(1)} %collective-permute-done.4.up_ref.refs_2_), channel_id=1, source_target_pairs={{0,8},{8,0},{16,24},{24,16},{32,40},{40,32},{48,56},{56,48},{64,72... | collective-permute-start | bytes 3145736 | tf_op jit(solution)/shard_map/ppermute | solution.py:26
  60.4 6.0 %collective-permute-start.14 = (bf16[64,8192]{1,0:T(8,128)(2,1)S(1)}, bf16[64,8192]{1,0:T(8,128)(2,1)}, u32[]{:S(2)}, u32[]{:S(2)}) collective-permute-start(bf16[64,8192]{1,0:T(8,128)(2,1)S(1)} %collective-permute-done.6.down_ref.refs_3_), channel_id=1, source_target_pairs={{0,8},{8,0},{16,24},{24,16},{32,40},{40,32},{48,56},{56,48},{64,72... | collective-permute-start | bytes 3145736 | tf_op jit(solution)/shard_map/ppermute | solution.py:26
  63.0 16.0 %collective-permute-start.10 = (bf16[32,8192]{1,0:T(8,128)(2,1)}, bf16[32,8192]{1,0:T(8,128)(2,1)S(1)}, u32[]{:S(2)}, u32[]{:S(2)}) collective-permute-start(bf16[32,8192]{1,0:T(8,128)(2,1)} %get-tuple-element.27), channel_id=1, source_target_pairs={{0,16},{8,24},{16,32},{24,40},{32,48},{40,56},{48,0},{56,8},{64,80... | collective-permute-start | bytes 1572872 | tf_op jit(solution)/shard_map/ppermute | solution.py:26
  63.8 15.3 %collective-permute-start.11 = (bf16[32,8192]{1,0:T(8,128)(2,1)}, bf16[32,8192]{1,0:T(8,128)(2,1)}, u32[]{:S(2)}, u32[]{:S(2)}) collective-permute-start(bf16[32,8192]{1,0:T(8,128)(2,1)} %get-tuple-element.28), channel_id=1, source_target_pairs={{0,48},{8,56},{16,0},{24,8},{32,16},{40,24},{48,32},{56,40},{64,11... | collective-permute-start | bytes 1572872 | tf_op jit(solution)/shard_map/ppermute | solution.py:26
  79.0 3.0 %copy-start.4 = (bf16[32,8192]{1,0:T(8,128)(2,1)}, bf16[32,8192]{1,0:T(8,128)(2,1)S(1)}, u32[]{:S(2)}) copy-start(bf16[32,8192]{1,0:T(8,128)(2,1)S(1)} %collective-permute-done.10.refs_1_) | copy-start | bytes 1572868
  79.0 2.0 %collective-permute-start.15 = (bf16[32,8192]{1,0:T(8,128)(2,1)S(1)}, bf16[32,8192]{1,0:T(8,128)(2,1)S(1)}, u32[]{:S(2)}, u32[]{:S(2)}) collective-permute-start(bf16[32,8192]{1,0:T(8,128)(2,1)S(1)} %collective-permute-done.10.refs_1_), channel_id=1, source_target_pairs={{0,8},{8,0},{16,24},{24,16},{32,40},{40,32},{48,56},{56,48},{64,72... | collective-permute-start | bytes 1572872 | tf_op jit(solution)/shard_map/ppermute | solution.py:26
  79.4 2.5 %collective-permute-start.16 = (bf16[32,8192]{1,0:T(8,128)(2,1)}, bf16[32,8192]{1,0:T(8,128)(2,1)S(1)}, u32[]{:S(2)}, u32[]{:S(2)}) collective-permute-start(bf16[32,8192]{1,0:T(8,128)(2,1)} %collective-permute-done.11.refs_2_), channel_id=1, source_target_pairs={{0,8},{8,0},{16,24},{24,16},{32,40},{40,32},{48,56},{56,48},{64,72... | collective-permute-start | bytes 1572872 | tf_op jit(solution)/shard_map/ppermute | solution.py:26
  90.8 5.1 %copy-start.7 = (s32[1,64]{1,0:T(1,128)S(1)}, s32[1,64]{1,0:T(1,128)}, u32[]{:S(2)}) copy-start(s32[1,64]{1,0:T(1,128)} %param.17) | copy-start | bytes 772
  90.9 31.4 %all-to-all-start = ((bf16[8,64,2048]{2,1,0:T(8,128)(2,1)}), bf16[8,64,2048]{2,1,0:T(8,128)(2,1)S(1)}, u32[]{:S(2)}, u32[]{:S(2)}) async-start(bf16[8,64,2048]{2,1,0:T(8,128)(2,1)} %aggregate_last.1), calls=%async_computation | async-start | bytes 4194304 | tf_op jit(solution)/shard_map/all_to_all | solution.py:265
  (5 other events, 5.4 us)

commit v5 on v4

--- a/solution.py
+++ b/solution.py
@@ -149,7 +149,12 @@
     smem = pl.BlockSpec(memory_space=pltpu.SMEM)
     anywhere = pl.BlockSpec(memory_space=pl.ANY)
     operands = [table]
-    specs = [smem] + [anywhere] * (1 + len(blocks))
+    held = [last and offset[2] == 1 for g, offset in zip(groups, offsets) for b in g]
+    near = pl.BlockSpec(memory_space=pltpu.VMEM)
+    specs = [smem, anywhere] + [near if h else anywhere for h in held]
+    blocks = [
+        pltpu.with_memory_space_constraint(b, pltpu.VMEM) if h else b for b, h in zip(blocks, held)
+    ]
     operands += [values] + blocks
     if not first:
         operands.append(acc)
@@ -342,8 +347,7 @@
         last=True,
         out=placing,
     )
-    means, mine = lax.optimization_barrier((exchange(placed), mine))
-    pre = across(means, w_neigh) + across(mine, w_self)
+    pre = across(mine, w_self) + across(exchange(placed), w_neigh)
     filled = jnp.sum((part_map[0] == column).astype(jnp.int32)) * TILE
     row = lax.broadcasted_iota(jnp.int32, (capacity * TILE, 1), 0)
     hidden = jnp.where(row < filled, jnp.maximum(pre + bias[None, :], 0.0), 0.0)

time: 129 us -> 126 us (0.977)
  waiting for transfers between devices: 45.8 us -> 41.2 us
  matrix products: 5.82 us -> 9.12 us
  Pallas kernels: 41.8 us -> 39.2 us
    all_to_all x2, waiting for transfers between devices: 25 us -> 19.9 us  [exchange(): got = lax.all_to_all(placed, 'bal', split_axis=0, concat_axis=0, tiled=True)]
    dot_general x2, matrix products: 5.82 us -> 9.12 us  [across(): lax.dot_general(left, right, (((0,), (0,)), ((), ())), preferred_element_...]
    pallas_call x4, Pallas kernels: 36.6 us -> 34.1 us  [accumulate(): pl.pallas_call(functools.partial(gather_kernel, layout, tuple(offsets), h...]
  transfers between devices with their start and end apart: 19 -> 19, of which waited for: 8 -> 9; matrix products, arithmetic and copies ran while one was open for 3% -> 7% of each run, Pallas kernels for 33% -> 32%
where the time goes in v5:
time: 126 us; the launch traced here: 124 us
  waiting for transfers between devices  41.2 us (33%)
  Pallas kernels  39.2 us (31%)
  starting transfers between devices  29.2 us (23%)
  matrix products  9.12 us (7%)
  other arithmetic  2.68 us (2%)
  local copies, waits for them, and re-layouts  1.91 us (2%)
    pallas_call x4, Pallas kernels, accumulate(): pl.pallas_call(functools.partial(gather_kernel, layout, tuple(offsets), h...  34.1 us
    ppermute x17, waiting for transfers between devices, route(): return lax.ppermute(block, 'blk', pairs)  21.3 us
    all_to_all x2, waiting for transfers between devices, exchange(): got = lax.all_to_all(placed, 'bal', split_axis=0, concat_axis=0, tiled=True)  19.9 us
    ppermute x17, starting transfers between devices, route(): return lax.ppermute(block, 'blk', pairs)  19.1 us
    all_to_all x2, starting transfers between devices, exchange(): got = lax.all_to_all(placed, 'bal', split_axis=0, concat_axis=0, tiled=True)  10.1 us
    dot_general x2, matrix products, across(): lax.dot_general(left, right, (((0,), (0,)), ((), ())), preferred_element_...  9.12 us
    pallas_call x1, Pallas kernels, place_features(): pl.pallas_call(place_kernel, in_specs=[pl.BlockSpec(memory_space=pltpu.SM...  3.13 us
  transfers between devices with their start and end apart: 19, of which 9 were waited for; matrix products, arithmetic and copies ran while one was open for 7% of the time, Pallas kernels for 32%

profile of v5, /device:TPU:1, one launch (start us, length us, event | category | flops | bytes accessed | tf_op | source)
XLA Modules:
  0.0 124.1 jit_solution(16505614023124009081)
XLA Ops:
  0.0 1.4 %collective-permute-start.3 = (bf16[64,8192]{1,0:T(8,128)(2,1)}, bf16[64,8192]{1,0:T(8,128)(2,1)S(1)}, u32[]{:S(2)}, u32[]{:S(2)}) collective-permute-start(bf16[64,8192]{1,0:T(8,128)(2,1)} %bitcast.18), channel_id=1, source_target_pairs={{0,8},{8,0},{16,24},{24,16},{32,40},{40,32},{48,56},{56,48},{64,72... | collective-permute-start | bytes 3145736 | tf_op jit(solution)/shard_map/ppermute | solution.py:26
  1.4 2.8 %collective-permute-start = (bf16[64,8192]{1,0:T(8,128)(2,1)}, bf16[64,8192]{1,0:T(8,128)(2,1)}, u32[]{:S(2)}, u32[]{:S(2)}) collective-permute-start(bf16[64,8192]{1,0:T(8,128)(2,1)} %bitcast.19), channel_id=1, source_target_pairs={{0,64},{8,72},{16,80},{24,88},{32,96},{40,104},{48,112},{56,120},{... | collective-permute-start | bytes 3145736 | tf_op jit(solution)/shard_map/ppermute | solution.py:26
  4.3 1.3 %collective-permute-start.1 = (bf16[64,8192]{1,0:T(8,128)(2,1)}, bf16[64,8192]{1,0:T(8,128)(2,1)}, u32[]{:S(2)}, u32[]{:S(2)}) collective-permute-start(bf16[64,8192]{1,0:T(8,128)(2,1)} %bitcast.20), channel_id=1, source_target_pairs={{0,16},{8,24},{16,32},{24,40},{32,48},{40,56},{48,0},{56,8},{64,80... | collective-permute-start | bytes 3145736 | tf_op jit(solution)/shard_map/ppermute | solution.py:26
  5.6 1.4 %collective-permute-start.2 = (bf16[64,8192]{1,0:T(8,128)(2,1)}, bf16[64,8192]{1,0:T(8,128)(2,1)}, u32[]{:S(2)}, u32[]{:S(2)}) collective-permute-start(bf16[64,8192]{1,0:T(8,128)(2,1)} %bitcast.21), channel_id=1, source_target_pairs={{0,48},{8,56},{16,0},{24,8},{32,16},{40,24},{48,32},{56,40},{64,11... | collective-permute-start | bytes 3145736 | tf_op jit(solution)/shard_map/ppermute | solution.py:26
  8.6 1.3 %pad_add_fusion.mapping.table = s32[17,128]{1,0:T(8,128)} fusion(s32[1,64]{1,0:T(1,128)} %param.17, s32[16,66]{1,0:T(8,128)S(1)} %add_add_fusion), kind=kLoop, calls=%fused_computation.2 | loop fusion | flops 2176 | bytes 13184 | tf_op jit(solution)/shard_map/concatenate | solution.py:294
  9.9 3.1 %place_features.1 = bf16[8,64,2048]{2,1,0:T(8,128)(2,1)} custom-call(s32[17,128]{1,0:T(8,128)} %pad_add_fusion.mapping.table, bf16[64,8192]{1,0:T(8,128)(2,1)} %bitcast.22), custom_call_target="tpu_custom_call" | custom-call | bytes 8388608 | tf_op jit(solution)/shard_map/place_features/pallas_call | solution.py:254
  14.1 5.6 %aggregate.3.refs_7_ = f32[64,80,128]{2,1,0:T(8,128)} custom-call(s32[17,128]{1,0:T(8,128)} %pad_add_fusion.mapping.table, bf16[16,32,128,128]{3,2,1,0:T(8,128)(2,1)} %bitcast.14, bf16[64,8192]{1,0:T(8,128)(2,1)} %bitcast.23, bf16[64,8192]{1,0:T(8,128)(2,1)} %copy-done.3), custom_call_target="tpu_custom_call" | custom-call | bytes 14680064 | tf_op jit(solution)/shard_map/aggregate/pallas_call | solution.py:179
  19.7 8.3 %collective-permute-done.refs_1_ = bf16[64,8192]{1,0:T(8,128)(2,1)} collective-permute-done((bf16[64,8192]{1,0:T(8,128)(2,1)}, bf16[64,8192]{1,0:T(8,128)(2,1)}, u32[]{:S(2)}, u32[]{:S(2)}) %collective-permute-start) | collective-permute-done | bytes 1048608 | tf_op jit(solution)/shard_map/ppermute | solution.py:26
  28.0 2.4 %collective-permute-done.1.refs_2_ = bf16[64,8192]{1,0:T(8,128)(2,1)} collective-permute-done((bf16[64,8192]{1,0:T(8,128)(2,1)}, bf16[64,8192]{1,0:T(8,128)(2,1)}, u32[]{:S(2)}, u32[]{:S(2)}) %collective-permute-start.1) | collective-permute-done | bytes 1048608 | tf_op jit(solution)/shard_map/ppermute | solution.py:26
  32.2 1.3 %collective-permute-start.5 = (bf16[64,8192]{1,0:T(8,128)(2,1)}, bf16[64,8192]{1,0:T(8,128)(2,1)}, u32[]{:S(2)}, u32[]{:S(2)}) collective-permute-start(bf16[64,8192]{1,0:T(8,128)(2,1)} %collective-permute-done.1.refs_2_), channel_id=1, source_target_pairs={{0,16},{8,24},{16,32},{24,40},{32,48},{40,56},{48,0},{56,8},{64,80... | collective-permute-start | bytes 3145736 | tf_op jit(solution)/shard_map/ppermute | solution.py:26
  34.1 2.6 %collective-permute-start.6 = (bf16[64,8192]{1,0:T(8,128)(2,1)}, bf16[64,8192]{1,0:T(8,128)(2,1)S(1)}, u32[]{:S(2)}, u32[]{:S(2)}) collective-permute-start(bf16[64,8192]{1,0:T(8,128)(2,1)} %collective-permute-done.refs_1_), channel_id=1, source_target_pairs={{0,48},{8,56},{16,0},{24,8},{32,16},{40,24},{48,32},{56,40},{64,11... | collective-permute-start | bytes 3145736 | tf_op jit(solution)/shard_map/ppermute | solution.py:26
  36.7 5.1 %all-to-all-start = ((bf16[8,64,2048]{2,1,0:T(8,128)(2,1)}), bf16[8,64,2048]{2,1,0:T(8,128)(2,1)}, u32[]{:S(2)}, u32[]{:S(2)}) async-start(bf16[8,64,2048]{2,1,0:T(8,128)(2,1)} %place_features.1), calls=%async_computation | async-start | bytes 4194304 | tf_op jit(solution)/shard_map/all_to_all | solution.py:270
  41.8 11.5 %aggregate.4.refs_7_ = f32[64,80,128]{2,1,0:T(8,128)} custom-call(s32[17,128]{1,0:T(8,128)} %pad_add_fusion.mapping.table, bf16[16,32,128,128]{3,2,1,0:T(8,128)(2,1)} %bitcast.15, bf16[64,8192]{1,0:T(8,128)(2,1)} %collective-permute-done.refs_1_, bf16[64,8192]{1,0:T(8,128)(2,1)} %collective-permute-done.1.refs_2_, ...), custom_call_target="tpu_custom_call" | custom-call | bytes 27262976 | tf_op jit(solution)/shard_map/aggregate/pallas_call | solution.py:179
  53.3 5.1 %collective-permute-done.4.up_ref.refs_2_ = bf16[64,8192]{1,0:T(8,128)(2,1)S(1)} collective-permute-done((bf16[64,8192]{1,0:T(8,128)(2,1)}, bf16[64,8192]{1,0:T(8,128)(2,1)S(1)}, u32[]{:S(2)}, u32[]{:S(2)}) %collective-permute-start.4) | collective-permute-done | bytes 1048608 | tf_op jit(solution)/shard_map/ppermute | solution.py:26
  60.9 2.0 %cut.1 = (bf16[32,8192]{1,0:T(8,128)(2,1)}, bf16[32,8192]{1,0:T(8,128)(2,1)}) custom-call(bf16[64,8192]{1,0:T(8,128)(2,1)} %copy-done.1, bf16[64,8192]{1,0:T(8,128)(2,1)} %copy-done.2), custom_call_target="tpu_custom_call" | custom-call | tf_op jit(solution)/shard_map/cut/pallas_call | solution.py:218
  63.7 2.6 %collective-permute-start.11 = (bf16[32,8192]{1,0:T(8,128)(2,1)}, bf16[32,8192]{1,0:T(8,128)(2,1)}, u32[]{:S(2)}, u32[]{:S(2)}) collective-permute-start(bf16[32,8192]{1,0:T(8,128)(2,1)} %get-tuple-element.27), channel_id=1, source_target_pairs={{0,48},{8,56},{16,0},{24,8},{32,16},{40,24},{48,32},{56,40},{64,11... | collective-permute-start | bytes 1572872 | tf_op jit(solution)/shard_map/ppermute | solution.py:26
  66.4 10.2 %aggregate.5.refs_5_ = f32[64,80,128]{2,1,0:T(8,128)} custom-call(s32[17,128]{1,0:T(8,128)} %pad_add_fusion.mapping.table, bf16[16,32,128,128]{3,2,1,0:T(8,128)(2,1)} %bitcast.16, bf16[64,8192]{1,0:T(8,128)(2,1)} %collective-permute-done.5.refs_1_, bf16[64,8192]{1,0:T(8,128)(2,1)} %copy-done.1, bf16[64,8192]{1,0:T(8,128)(2,1)} %copy-done.2, ...), custom_call_target="tpu_custom_call" | custom-call | bytes 27262976 | tf_op jit(solution)/shard_map/aggregate/pallas_call | solution.py:179
  76.6 1.7 %collective-permute-done.10.refs_1_ = bf16[32,8192]{1,0:T(8,128)(2,1)S(1)} collective-permute-done((bf16[32,8192]{1,0:T(8,128)(2,1)}, bf16[32,8192]{1,0:T(8,128)(2,1)S(1)}, u32[]{:S(2)}, u32[]{:S(2)}) %collective-permute-start.10) | collective-permute-done | bytes 524320 | tf_op jit(solution)/shard_map/ppermute | solution.py:26
  79.5 1.5 %collective-permute-done.15.refs_3_ = bf16[32,8192]{1,0:T(8,128)(2,1)S(1)} collective-permute-done((bf16[32,8192]{1,0:T(8,128)(2,1)S(1)}, bf16[32,8192]{1,0:T(8,128)(2,1)S(1)}, u32[]{:S(2)}, u32[]{:S(2)}) %collective-permute-start.15) | collective-permute-done | bytes 524320 | tf_op jit(solution)/shard_map/ppermute | solution.py:26
  81.9 6.8 %aggregate_last.1 = bf16[8,64,2048]{2,1,0:T(8,128)(2,1)} custom-call(s32[17,128]{1,0:T(8,128)} %pad_add_fusion.mapping.table, bf16[16,32,128,128]{3,2,1,0:T(8,128)(2,1)} %bitcast.17, bf16[32,8192]{1,0:T(8,128)(2,1)} %copy-done.4, bf16[32,8192]{1,0:T(8,128)(2,1)} %collective-permute-done.11.refs_2_, bf16[32,8192]{1,0:T(8,128)(2,1)S(1)} %collective-permute-done.15.refs_3_, ...), custom_call_target="tpu_custom_call" | custom-call | bytes 14680064 | tf_op jit(solution)/shard_map/aggregate_last/pallas_call | solution.py:179
  88.7 5.1 %all-to-all-start.1 = ((bf16[8,64,2048]{2,1,0:T(8,128)(2,1)}), bf16[8,64,2048]{2,1,0:T(8,128)(2,1)S(1)}, u32[]{:S(2)}, u32[]{:S(2)}) async-start(bf16[8,64,2048]{2,1,0:T(8,128)(2,1)} %aggregate_last.1), calls=%async_computation.1 | async-start | bytes 4194304 | tf_op jit(solution)/shard_map/all_to_all | solution.py:270
  95.1 4.9 %fusion.2 = f32[2048,512]{1,0:T(8,128)} fusion(bf16[512,2048]{1,0:T(8,128)(2,1)} %bitcast.5, bf16[512,512]{1,0:T(8,128)(2,1)S(1)} %copy-done), kind=kOutput, calls=%fused_computation.7 | convolution fusion | flops 1073741824 | bytes 6815744 | tf_op jit(solution)/shard_map/dot_general | solution.py:275
  100.0 19.9 %all-to-all-done.1 = bf16[8,64,2048]{2,1,0:T(8,128)(2,1)S(1)} async-done(((bf16[8,64,2048]{2,1,0:T(8,128)(2,1)}), bf16[8,64,2048]{2,1,0:T(8,128)(2,1)S(1)}, u32[]{:S(2)}, u32[]{:S(2)}) %all-to-all-start.1) | async-done | bytes 2097184 | tf_op jit(solution)/shard_map/all_to_all | solution.py:270
  119.9 4.2 %fusion = bf16[1,1,2048,512]{3,2,1,0:T(8,128)(2,1)} fusion(f32[2048,512]{1,0:T(8,128)} %fusion.2, bf16[512,2048]{1,0:T(8,128)(2,1)S(1)} %bitcast.24, bf16[512,512]{1,0:T(8,128)(2,1)S(1)} %copy-done.6, f32[512]{0:T(512)S(1)} %copy-done.7, pred[2048]{0:T(1024)(128)(4,1)S(1)} %iota_compare_fusion), kind=kOutput, calls=%fused_computation.1 | convolution fusion | flops 1078984704 | bytes 8916992 | tf_op jit(solution)/shard_map/dot_general | solution.py:275
  (44 shorter events, 11.2 us)
Async XLA Ops:
  0.0 95.1 %copy-start = (bf16[512,512]{1,0:T(8,128)(2,1)S(1)}, bf16[512,512]{1,0:T(8,128)(2,1)}, u32[]{:S(2)}) copy-start(bf16[512,512]{1,0:T(8,128)(2,1)} %param.14) | copy-start | bytes 1572868
  0.0 13.0 %collective-permute-start.3 = (bf16[64,8192]{1,0:T(8,128)(2,1)}, bf16[64,8192]{1,0:T(8,128)(2,1)S(1)}, u32[]{:S(2)}, u32[]{:S(2)}) collective-permute-start(bf16[64,8192]{1,0:T(8,128)(2,1)} %bitcast.18), channel_id=1, source_target_pairs={{0,8},{8,0},{16,24},{24,16},{32,40},{40,32},{48,56},{56,48},{64,72... | collective-permute-start | bytes 3145736 | tf_op jit(solution)/shard_map/ppermute | solution.py:26
  1.4 26.6 %collective-permute-start = (bf16[64,8192]{1,0:T(8,128)(2,1)}, bf16[64,8192]{1,0:T(8,128)(2,1)}, u32[]{:S(2)}, u32[]{:S(2)}) collective-permute-start(bf16[64,8192]{1,0:T(8,128)(2,1)} %bitcast.19), channel_id=1, source_target_pairs={{0,64},{8,72},{16,80},{24,88},{32,96},{40,104},{48,112},{56,120},{... | collective-permute-start | bytes 3145736 | tf_op jit(solution)/shard_map/ppermute | solution.py:26
  4.3 26.1 %collective-permute-start.1 = (bf16[64,8192]{1,0:T(8,128)(2,1)}, bf16[64,8192]{1,0:T(8,128)(2,1)}, u32[]{:S(2)}, u32[]{:S(2)}) collective-permute-start(bf16[64,8192]{1,0:T(8,128)(2,1)} %bitcast.20), channel_id=1, source_target_pairs={{0,16},{8,24},{16,32},{24,40},{32,48},{40,56},{48,0},{56,8},{64,80... | collective-permute-start | bytes 3145736 | tf_op jit(solution)/shard_map/ppermute | solution.py:26
  5.6 24.8 %collective-permute-start.2 = (bf16[64,8192]{1,0:T(8,128)(2,1)}, bf16[64,8192]{1,0:T(8,128)(2,1)}, u32[]{:S(2)}, u32[]{:S(2)}) collective-permute-start(bf16[64,8192]{1,0:T(8,128)(2,1)} %bitcast.21), channel_id=1, source_target_pairs={{0,48},{8,56},{16,0},{24,8},{32,16},{40,24},{48,32},{56,40},{64,11... | collective-permute-start | bytes 3145736 | tf_op jit(solution)/shard_map/ppermute | solution.py:26
  30.4 3.7 %collective-permute-start.8 = (bf16[64,8192]{1,0:T(8,128)(2,1)}, bf16[64,8192]{1,0:T(8,128)(2,1)}, u32[]{:S(2)}, u32[]{:S(2)}) collective-permute-start(bf16[64,8192]{1,0:T(8,128)(2,1)} %collective-permute-done.1.refs_2_), channel_id=1, source_target_pairs={{0,8},{8,0},{16,24},{24,16},{32,40},{40,32},{48,56},{56,48},{64,72... | collective-permute-start | bytes 3145736 | tf_op jit(solution)/shard_map/ppermute | solution.py:26
  31.5 10.3 %collective-permute-start.7 = (bf16[64,8192]{1,0:T(8,128)(2,1)}, bf16[64,8192]{1,0:T(8,128)(2,1)}, u32[]{:S(2)}, u32[]{:S(2)}) collective-permute-start(bf16[64,8192]{1,0:T(8,128)(2,1)} %collective-permute-done.refs_1_), channel_id=1, source_target_pairs={{0,8},{8,0},{16,24},{24,16},{32,40},{40,32},{48,56},{56,48},{64,72... | collective-permute-start | bytes 3145736 | tf_op jit(solution)/shard_map/ppermute | solution.py:26
  31.5 10.3 %collective-permute-start.9 = (bf16[64,8192]{1,0:T(8,128)(2,1)}, bf16[64,8192]{1,0:T(8,128)(2,1)}, u32[]{:S(2)}, u32[]{:S(2)}) collective-permute-start(bf16[64,8192]{1,0:T(8,128)(2,1)} %collective-permute-done.2.refs_3_), channel_id=1, source_target_pairs={{0,8},{8,0},{16,24},{24,16},{32,40},{40,32},{48,56},{56,48},{64,72... | collective-permute-start | bytes 3145736 | tf_op jit(solution)/shard_map/ppermute | solution.py:26
  32.0 26.5 %collective-permute-start.4 = (bf16[64,8192]{1,0:T(8,128)(2,1)}, bf16[64,8192]{1,0:T(8,128)(2,1)S(1)}, u32[]{:S(2)}, u32[]{:S(2)}) collective-permute-start(bf16[64,8192]{1,0:T(8,128)(2,1)} %collective-permute-done.1.refs_2_), channel_id=1, source_target_pairs={{0,64},{8,72},{16,80},{24,88},{32,96},{40,104},{48,112},{56,120},{... | collective-permute-start | bytes 3145736 | tf_op jit(solution)/shard_map/ppermute | solution.py:26
  32.2 26.3 %collective-permute-start.5 = (bf16[64,8192]{1,0:T(8,128)(2,1)}, bf16[64,8192]{1,0:T(8,128)(2,1)}, u32[]{:S(2)}, u32[]{:S(2)}) collective-permute-start(bf16[64,8192]{1,0:T(8,128)(2,1)} %collective-permute-done.1.refs_2_), channel_id=1, source_target_pairs={{0,16},{8,24},{16,32},{24,40},{32,48},{40,56},{48,0},{56,8},{64,80... | collective-permute-start | bytes 3145736 | tf_op jit(solution)/shard_map/ppermute | solution.py:26
  34.1 25.1 %collective-permute-start.6 = (bf16[64,8192]{1,0:T(8,128)(2,1)}, bf16[64,8192]{1,0:T(8,128)(2,1)S(1)}, u32[]{:S(2)}, u32[]{:S(2)}) collective-permute-start(bf16[64,8192]{1,0:T(8,128)(2,1)} %collective-permute-done.refs_1_), channel_id=1, source_target_pairs={{0,48},{8,56},{16,0},{24,8},{32,16},{40,24},{48,32},{56,40},{64,11... | collective-permute-start | bytes 3145736 | tf_op jit(solution)/shard_map/ppermute | solution.py:26
  36.7 52.0 %all-to-all-start = ((bf16[8,64,2048]{2,1,0:T(8,128)(2,1)}), bf16[8,64,2048]{2,1,0:T(8,128)(2,1)}, u32[]{:S(2)}, u32[]{:S(2)}) async-start(bf16[8,64,2048]{2,1,0:T(8,128)(2,1)} %place_features.1), calls=%async_computation | async-start | bytes 4194304 | tf_op jit(solution)/shard_map/all_to_all | solution.py:270
  59.2 7.2 %collective-permute-start.12 = (bf16[64,8192]{1,0:T(8,128)(2,1)}, bf16[64,8192]{1,0:T(8,128)(2,1)}, u32[]{:S(2)}, u32[]{:S(2)}) collective-permute-start(bf16[64,8192]{1,0:T(8,128)(2,1)} %collective-permute-done.5.refs_1_), channel_id=1, source_target_pairs={{0,8},{8,0},{16,24},{24,16},{32,40},{40,32},{48,56},{56,48},{64,72... | collective-permute-start | bytes 3145736 | tf_op jit(solution)/shard_map/ppermute | solution.py:26
  60.4 6.0 %collective-permute-start.13 = (bf16[64,8192]{1,0:T(8,128)(2,1)S(1)}, bf16[64,8192]{1,0:T(8,128)(2,1)}, u32[]{:S(2)}, u32[]{:S(2)}) collective-permute-start(bf16[64,8192]{1,0:T(8,128)(2,1)S(1)} %collective-permute-done.4.up_ref.refs_2_), channel_id=1, source_target_pairs={{0,8},{8,0},{16,24},{24,16},{32,40},{40,32},{48,56},{56,48},{64,72... | collective-permute-start | bytes 3145736 | tf_op jit(solution)/shard_map/ppermute | solution.py:26
  60.4 6.0 %collective-permute-start.14 = (bf16[64,8192]{1,0:T(8,128)(2,1)S(1)}, bf16[64,8192]{1,0:T(8,128)(2,1)}, u32[]{:S(2)}, u32[]{:S(2)}) collective-permute-start(bf16[64,8192]{1,0:T(8,128)(2,1)S(1)} %collective-permute-done.6.down_ref.refs_3_), channel_id=1, source_target_pairs={{0,8},{8,0},{16,24},{24,16},{32,40},{40,32},{48,56},{56,48},{64,72... | collective-permute-start | bytes 3145736 | tf_op jit(solution)/shard_map/ppermute | solution.py:26
  62.9 15.4 %collective-permute-start.10 = (bf16[32,8192]{1,0:T(8,128)(2,1)}, bf16[32,8192]{1,0:T(8,128)(2,1)S(1)}, u32[]{:S(2)}, u32[]{:S(2)}) collective-permute-start(bf16[32,8192]{1,0:T(8,128)(2,1)} %get-tuple-element.26), channel_id=1, source_target_pairs={{0,16},{8,24},{16,32},{24,40},{32,48},{40,56},{48,0},{56,8},{64,80... | collective-permute-start | bytes 1572872 | tf_op jit(solution)/shard_map/ppermute | solution.py:26
  63.7 14.6 %collective-permute-start.11 = (bf16[32,8192]{1,0:T(8,128)(2,1)}, bf16[32,8192]{1,0:T(8,128)(2,1)}, u32[]{:S(2)}, u32[]{:S(2)}) collective-permute-start(bf16[32,8192]{1,0:T(8,128)(2,1)} %get-tuple-element.27), channel_id=1, source_target_pairs={{0,48},{8,56},{16,0},{24,8},{32,16},{40,24},{48,32},{56,40},{64,11... | collective-permute-start | bytes 1572872 | tf_op jit(solution)/shard_map/ppermute | solution.py:26
  78.3 3.6 %copy-start.4 = (bf16[32,8192]{1,0:T(8,128)(2,1)}, bf16[32,8192]{1,0:T(8,128)(2,1)S(1)}, u32[]{:S(2)}) copy-start(bf16[32,8192]{1,0:T(8,128)(2,1)S(1)} %collective-permute-done.10.refs_1_) | copy-start | bytes 1572868
  78.3 2.6 %collective-permute-start.15 = (bf16[32,8192]{1,0:T(8,128)(2,1)S(1)}, bf16[32,8192]{1,0:T(8,128)(2,1)S(1)}, u32[]{:S(2)}, u32[]{:S(2)}) collective-permute-start(bf16[32,8192]{1,0:T(8,128)(2,1)S(1)} %collective-permute-done.10.refs_1_), channel_id=1, source_target_pairs={{0,8},{8,0},{16,24},{24,16},{32,40},{40,32},{48,56},{56,48},{64,72... | collective-permute-start | bytes 1572872 | tf_op jit(solution)/shard_map/ppermute | solution.py:26
  79.4 2.5 %collective-permute-start.16 = (bf16[32,8192]{1,0:T(8,128)(2,1)}, bf16[32,8192]{1,0:T(8,128)(2,1)S(1)}, u32[]{:S(2)}, u32[]{:S(2)}) collective-permute-start(bf16[32,8192]{1,0:T(8,128)(2,1)} %collective-permute-done.11.refs_2_), channel_id=1, source_target_pairs={{0,8},{8,0},{16,24},{24,16},{32,40},{40,32},{48,56},{56,48},{64,72... | collective-permute-start | bytes 1572872 | tf_op jit(solution)/shard_map/ppermute | solution.py:26
  88.7 5.1 %copy-start.5 = (s32[1,64]{1,0:T(1,128)S(1)}, s32[1,64]{1,0:T(1,128)}, u32[]{:S(2)}) copy-start(s32[1,64]{1,0:T(1,128)} %param.17) | copy-start | bytes 772
  88.7 31.2 %all-to-all-start.1 = ((bf16[8,64,2048]{2,1,0:T(8,128)(2,1)}), bf16[8,64,2048]{2,1,0:T(8,128)(2,1)S(1)}, u32[]{:S(2)}, u32[]{:S(2)}) async-start(bf16[8,64,2048]{2,1,0:T(8,128)(2,1)} %aggregate_last.1), calls=%async_computation.1 | async-start | bytes 4194304 | tf_op jit(solution)/shard_map/all_to_all | solution.py:270
  95.1 24.8 %copy-start.6 = (bf16[512,512]{1,0:T(8,128)(2,1)S(1)}, bf16[512,512]{1,0:T(8,128)(2,1)}, u32[]{:S(2)}) copy-start(bf16[512,512]{1,0:T(8,128)(2,1)} %param.15) | copy-start | bytes 1572868
  95.1 24.8 %copy-start.7 = (f32[512]{0:T(512)S(1)}, f32[512]{0:T(512)}, u32[]{:S(2)}) copy-start(f32[512]{0:T(512)} %param.16) | copy-start | bytes 6148
  (3 other events, 5.2 us)

commit v6 on v5

--- a/solution.py
+++ b/solution.py
@@ -189,41 +189,34 @@
     )(*operands)
 
 
-def cut_kernel(up_ref, down_ref, *refs):
-    top_ref, bottom_ref, held, in_sem, out_sem = refs
-    rows = held.shape[1]
+def cut_kernel(up_ref, down_ref, top_ref, bottom_ref, sems):
     half = top_ref.shape[0]
-    loads, stores = [], []
-    for k in range(held.shape[0]):
+    rows = half // 2
+    copies = []
+    for k in range(4):
         at = k * rows
         source, target = (up_ref, top_ref) if at < half else (down_ref, bottom_ref)
-        loads.append(
-            pltpu.make_async_copy(source.at[pl.ds(at, rows)], held.at[k], in_sem.at[k])
+        copies.append(
+            pltpu.make_async_copy(
+                source.at[pl.ds(at, rows)], target.at[pl.ds(at % half, rows)], sems.at[k]
+            )
         )
-        stores.append(
-            pltpu.make_async_copy(held.at[k], target.at[pl.ds(at % half, rows)], out_sem.at[k])
-        )
-    for copy in loads:
+    for copy in copies:
         copy.start()
-    for load, store in zip(loads, stores):
-        load.wait()
-        store.start()
-    for copy in stores:
+    for copy in copies:
         copy.wait()
 
 
 def cut(up, down):
-    anywhere = pl.BlockSpec(memory_space=pl.ANY)
     piece = jax.ShapeDtypeStruct((up.shape[0] // 2, up.shape[1]), up.dtype)
     return pl.pallas_call(
         cut_kernel,
-        in_specs=[anywhere] * 2,
-        out_specs=[anywhere] * 2,
+        in_specs=[pl.BlockSpec(memory_space=pltpu.VMEM)] * 2,
+        out_specs=[pl.BlockSpec(memory_space=pl.ANY)] * 2,
         out_shape=[piece] * 2,
-        scratch_shapes=[pltpu.VMEM((4, up.shape[0] // 4, up.shape[1]), up.dtype)]
-        + [pltpu.SemaphoreType.DMA((4,))] * 2,
+        scratch_shapes=[pltpu.SemaphoreType.DMA((4,))],
         name="cut",
-    )(up, down)
+    )(*[pltpu.with_memory_space_constraint(b, pltpu.VMEM) for b in (up, down)])
 
 
 def place_into(out_ref, mapping, used, tiles_per, tile_of):

time: 126 us -> 124 us (0.984)
  Pallas kernels: 39.2 us -> 36.5 us
  waiting for transfers between devices: 41.2 us -> 43.6 us
    ppermute x17, waiting for transfers between devices: 21.3 us -> 23.7 us  [route(): return lax.ppermute(block, 'blk', pairs)]
    pallas_call x4, Pallas kernels: 34.1 us -> 32.4 us  [accumulate(): pl.pallas_call(functools.partial(gather_kernel, layout, tuple(offsets), h...]
  transfers between devices with their start and end apart: 19 -> 19, of which waited for: 9 -> 10; matrix products, arithmetic and copies ran while one was open for 7% -> 7% of each run, Pallas kernels for 32% -> 30%
where the time goes in v6:
time: 124 us; the launch traced here: 123 us
  waiting for transfers between devices  43.6 us (35%)
  Pallas kernels  36.5 us (29%)
  starting transfers between devices  28.6 us (23%)
  matrix products  9.1 us (7%)
  other arithmetic  2.68 us (2%)
  local copies, waits for them, and re-layouts  1.91 us (2%)
    pallas_call x4, Pallas kernels, accumulate(): pl.pallas_call(functools.partial(gather_kernel, layout, tuple(offsets), h...  32.4 us
    ppermute x17, waiting for transfers between devices, route(): return lax.ppermute(block, 'blk', pairs)  23.7 us
    all_to_all x2, waiting for transfers between devices, exchange(): got = lax.all_to_all(placed, 'bal', split_axis=0, concat_axis=0, tiled=True)  19.9 us
    ppermute x17, starting transfers between devices, route(): return lax.ppermute(block, 'blk', pairs)  18.5 us
    all_to_all x2, starting transfers between devices, exchange(): got = lax.all_to_all(placed, 'bal', split_axis=0, concat_axis=0, tiled=True)  10.1 us
    dot_general x2, matrix products, across(): lax.dot_general(left, right, (((0,), (0,)), ((), ())), preferred_element_...  9.1 us
    pallas_call x1, Pallas kernels, place_features(): pl.pallas_call(place_kernel, in_specs=[pl.BlockSpec(memory_space=pltpu.SM...  3.13 us
  transfers between devices with their start and end apart: 19, of which 10 were waited for; matrix products, arithmetic and copies ran while one was open for 7% of the time, Pallas kernels for 30%

profile of v6, /device:TPU:1, one launch (start us, length us, event | category | flops | bytes accessed | tf_op | source)
XLA Modules:
  0.0 123.1 jit_solution(10543642709206883388)
XLA Ops:
  0.0 1.4 %collective-permute-start.3 = (bf16[64,8192]{1,0:T(8,128)(2,1)}, bf16[64,8192]{1,0:T(8,128)(2,1)S(1)}, u32[]{:S(2)}, u32[]{:S(2)}) collective-permute-start(bf16[64,8192]{1,0:T(8,128)(2,1)} %bitcast.18), channel_id=1, source_target_pairs={{0,8},{8,0},{16,24},{24,16},{32,40},{40,32},{48,56},{56,48},{64,72... | collective-permute-start | bytes 3145736 | tf_op jit(solution)/shard_map/ppermute | solution.py:26
  1.4 2.8 %collective-permute-start = (bf16[64,8192]{1,0:T(8,128)(2,1)}, bf16[64,8192]{1,0:T(8,128)(2,1)}, u32[]{:S(2)}, u32[]{:S(2)}) collective-permute-start(bf16[64,8192]{1,0:T(8,128)(2,1)} %bitcast.19), channel_id=1, source_target_pairs={{0,64},{8,72},{16,80},{24,88},{32,96},{40,104},{48,112},{56,120},{... | collective-permute-start | bytes 3145736 | tf_op jit(solution)/shard_map/ppermute | solution.py:26
  4.3 1.3 %collective-permute-start.1 = (bf16[64,8192]{1,0:T(8,128)(2,1)}, bf16[64,8192]{1,0:T(8,128)(2,1)}, u32[]{:S(2)}, u32[]{:S(2)}) collective-permute-start(bf16[64,8192]{1,0:T(8,128)(2,1)} %bitcast.20), channel_id=1, source_target_pairs={{0,16},{8,24},{16,32},{24,40},{32,48},{40,56},{48,0},{56,8},{64,80... | collective-permute-start | bytes 3145736 | tf_op jit(solution)/shard_map/ppermute | solution.py:26
  5.6 1.4 %collective-permute-start.2 = (bf16[64,8192]{1,0:T(8,128)(2,1)}, bf16[64,8192]{1,0:T(8,128)(2,1)}, u32[]{:S(2)}, u32[]{:S(2)}) collective-permute-start(bf16[64,8192]{1,0:T(8,128)(2,1)} %bitcast.21), channel_id=1, source_target_pairs={{0,48},{8,56},{16,0},{24,8},{32,16},{40,24},{48,32},{56,40},{64,11... | collective-permute-start | bytes 3145736 | tf_op jit(solution)/shard_map/ppermute | solution.py:26
  8.6 1.3 %pad_add_fusion.mapping.table = s32[17,128]{1,0:T(8,128)} fusion(s32[1,64]{1,0:T(1,128)} %param.17, s32[16,66]{1,0:T(8,128)S(1)} %add_add_fusion), kind=kLoop, calls=%fused_computation.2 | loop fusion | flops 2176 | bytes 13184 | tf_op jit(solution)/shard_map/concatenate | solution.py:287
  9.9 3.1 %place_features.1 = bf16[8,64,2048]{2,1,0:T(8,128)(2,1)} custom-call(s32[17,128]{1,0:T(8,128)} %pad_add_fusion.mapping.table, bf16[64,8192]{1,0:T(8,128)(2,1)} %bitcast.22), custom_call_target="tpu_custom_call" | custom-call | bytes 8388608 | tf_op jit(solution)/shard_map/place_features/pallas_call | solution.py:247
  14.1 5.7 %aggregate.3.refs_7_ = f32[64,80,128]{2,1,0:T(8,128)} custom-call(s32[17,128]{1,0:T(8,128)} %pad_add_fusion.mapping.table, bf16[16,32,128,128]{3,2,1,0:T(8,128)(2,1)} %bitcast.14, bf16[64,8192]{1,0:T(8,128)(2,1)} %bitcast.23, bf16[64,8192]{1,0:T(8,128)(2,1)} %copy-done.3), custom_call_target="tpu_custom_call" | custom-call | bytes 14680064 | tf_op jit(solution)/shard_map/aggregate/pallas_call | solution.py:179
  19.8 8.2 %collective-permute-done.refs_1_ = bf16[64,8192]{1,0:T(8,128)(2,1)} collective-permute-done((bf16[64,8192]{1,0:T(8,128)(2,1)}, bf16[64,8192]{1,0:T(8,128)(2,1)}, u32[]{:S(2)}, u32[]{:S(2)}) %collective-permute-start) | collective-permute-done | bytes 1048608 | tf_op jit(solution)/shard_map/ppermute | solution.py:26
  28.0 2.4 %collective-permute-done.1.refs_2_ = bf16[64,8192]{1,0:T(8,128)(2,1)} collective-permute-done((bf16[64,8192]{1,0:T(8,128)(2,1)}, bf16[64,8192]{1,0:T(8,128)(2,1)}, u32[]{:S(2)}, u32[]{:S(2)}) %collective-permute-start.1) | collective-permute-done | bytes 1048608 | tf_op jit(solution)/shard_map/ppermute | solution.py:26
  32.2 1.3 %collective-permute-start.5 = (bf16[64,8192]{1,0:T(8,128)(2,1)}, bf16[64,8192]{1,0:T(8,128)(2,1)}, u32[]{:S(2)}, u32[]{:S(2)}) collective-permute-start(bf16[64,8192]{1,0:T(8,128)(2,1)} %collective-permute-done.1.refs_2_), channel_id=1, source_target_pairs={{0,16},{8,24},{16,32},{24,40},{32,48},{40,56},{48,0},{56,8},{64,80... | collective-permute-start | bytes 3145736 | tf_op jit(solution)/shard_map/ppermute | solution.py:26
  34.1 2.6 %collective-permute-start.6 = (bf16[64,8192]{1,0:T(8,128)(2,1)}, bf16[64,8192]{1,0:T(8,128)(2,1)S(1)}, u32[]{:S(2)}, u32[]{:S(2)}) collective-permute-start(bf16[64,8192]{1,0:T(8,128)(2,1)} %collective-permute-done.refs_1_), channel_id=1, source_target_pairs={{0,48},{8,56},{16,0},{24,8},{32,16},{40,24},{48,32},{56,40},{64,11... | collective-permute-start | bytes 3145736 | tf_op jit(solution)/shard_map/ppermute | solution.py:26
  36.7 5.1 %all-to-all-start = ((bf16[8,64,2048]{2,1,0:T(8,128)(2,1)}), bf16[8,64,2048]{2,1,0:T(8,128)(2,1)}, u32[]{:S(2)}, u32[]{:S(2)}) async-start(bf16[8,64,2048]{2,1,0:T(8,128)(2,1)} %place_features.1), calls=%async_computation | async-start | bytes 4194304 | tf_op jit(solution)/shard_map/all_to_all | solution.py:263
  41.8 9.2 %aggregate.4.refs_7_ = f32[64,80,128]{2,1,0:T(8,128)} custom-call(s32[17,128]{1,0:T(8,128)} %pad_add_fusion.mapping.table, bf16[16,32,128,128]{3,2,1,0:T(8,128)(2,1)} %bitcast.15, bf16[64,8192]{1,0:T(8,128)(2,1)} %collective-permute-done.refs_1_, bf16[64,8192]{1,0:T(8,128)(2,1)} %collective-permute-done.1.refs_2_, ...), custom_call_target="tpu_custom_call" | custom-call | bytes 27262976 | tf_op jit(solution)/shard_map/aggregate/pallas_call | solution.py:179
  51.0 7.5 %collective-permute-done.4.up_ref.refs_2_ = bf16[64,8192]{1,0:T(8,128)(2,1)S(1)} collective-permute-done((bf16[64,8192]{1,0:T(8,128)(2,1)}, bf16[64,8192]{1,0:T(8,128)(2,1)S(1)}, u32[]{:S(2)}, u32[]{:S(2)}) %collective-permute-start.4) | collective-permute-done | bytes 1048608 | tf_op jit(solution)/shard_map/ppermute | solution.py:26
  59.2 1.2 collective-permute-start.12
  62.8 2.6 %collective-permute-start.11 = (bf16[32,8192]{1,0:T(8,128)(2,1)}, bf16[32,8192]{1,0:T(8,128)(2,1)}, u32[]{:S(2)}, u32[]{:S(2)}) collective-permute-start(bf16[32,8192]{1,0:T(8,128)(2,1)} %get-tuple-element.27), channel_id=1, source_target_pairs={{0,48},{8,56},{16,0},{24,8},{32,16},{40,24},{48,32},{56,40},{64,11... | collective-permute-start | bytes 1572872 | tf_op jit(solution)/shard_map/ppermute | solution.py:26
  65.9 10.7 %aggregate.5.refs_5_ = f32[64,80,128]{2,1,0:T(8,128)} custom-call(s32[17,128]{1,0:T(8,128)} %pad_add_fusion.mapping.table, bf16[16,32,128,128]{3,2,1,0:T(8,128)(2,1)} %bitcast.16, bf16[64,8192]{1,0:T(8,128)(2,1)} %collective-permute-done.5.refs_1_, bf16[64,8192]{1,0:T(8,128)(2,1)} %copy-done.1, bf16[64,8192]{1,0:T(8,128)(2,1)} %copy-done.2, ...), custom_call_target="tpu_custom_call" | custom-call | bytes 27262976 | tf_op jit(solution)/shard_map/aggregate/pallas_call | solution.py:179
  76.6 1.4 %collective-permute-done.10.refs_1_ = bf16[32,8192]{1,0:T(8,128)(2,1)S(1)} collective-permute-done((bf16[32,8192]{1,0:T(8,128)(2,1)}, bf16[32,8192]{1,0:T(8,128)(2,1)S(1)}, u32[]{:S(2)}, u32[]{:S(2)}) %collective-permute-start.10) | collective-permute-done | bytes 524320 | tf_op jit(solution)/shard_map/ppermute | solution.py:26
  78.5 1.5 %collective-permute-done.15.refs_3_ = bf16[32,8192]{1,0:T(8,128)(2,1)S(1)} collective-permute-done((bf16[32,8192]{1,0:T(8,128)(2,1)S(1)}, bf16[32,8192]{1,0:T(8,128)(2,1)S(1)}, u32[]{:S(2)}, u32[]{:S(2)}) %collective-permute-start.15) | collective-permute-done | bytes 524320 | tf_op jit(solution)/shard_map/ppermute | solution.py:26
  80.9 6.8 %aggregate_last.1 = bf16[8,64,2048]{2,1,0:T(8,128)(2,1)} custom-call(s32[17,128]{1,0:T(8,128)} %pad_add_fusion.mapping.table, bf16[16,32,128,128]{3,2,1,0:T(8,128)(2,1)} %bitcast.17, bf16[32,8192]{1,0:T(8,128)(2,1)} %copy-done.4, bf16[32,8192]{1,0:T(8,128)(2,1)} %collective-permute-done.11.refs_2_, bf16[32,8192]{1,0:T(8,128)(2,1)S(1)} %collective-permute-done.15.refs_3_, ...), custom_call_target="tpu_custom_call" | custom-call | bytes 14680064 | tf_op jit(solution)/shard_map/aggregate_last/pallas_call | solution.py:179
  87.7 5.1 %all-to-all-start.1 = ((bf16[8,64,2048]{2,1,0:T(8,128)(2,1)}), bf16[8,64,2048]{2,1,0:T(8,128)(2,1)S(1)}, u32[]{:S(2)}, u32[]{:S(2)}) async-start(bf16[8,64,2048]{2,1,0:T(8,128)(2,1)} %aggregate_last.1), calls=%async_computation.1 | async-start | bytes 4194304 | tf_op jit(solution)/shard_map/all_to_all | solution.py:263
  94.1 4.9 %fusion.2 = f32[2048,512]{1,0:T(8,128)} fusion(bf16[512,2048]{1,0:T(8,128)(2,1)} %bitcast.5, bf16[512,512]{1,0:T(8,128)(2,1)S(1)} %copy-done), kind=kOutput, calls=%fused_computation.7 | convolution fusion | flops 1073741824 | bytes 6815744 | tf_op jit(solution)/shard_map/dot_general | solution.py:268
  99.0 19.9 %all-to-all-done.1 = bf16[8,64,2048]{2,1,0:T(8,128)(2,1)S(1)} async-done(((bf16[8,64,2048]{2,1,0:T(8,128)(2,1)}), bf16[8,64,2048]{2,1,0:T(8,128)(2,1)S(1)}, u32[]{:S(2)}, u32[]{:S(2)}) %all-to-all-start.1) | async-done | bytes 2097184 | tf_op jit(solution)/shard_map/all_to_all | solution.py:263
  118.9 4.2 %fusion = bf16[1,1,2048,512]{3,2,1,0:T(8,128)(2,1)} fusion(f32[2048,512]{1,0:T(8,128)} %fusion.2, bf16[512,2048]{1,0:T(8,128)(2,1)S(1)} %bitcast.24, bf16[512,512]{1,0:T(8,128)(2,1)S(1)} %copy-done.6, f32[512]{0:T(512)S(1)} %copy-done.7, pred[2048]{0:T(1024)(128)(4,1)S(1)} %iota_compare_fusion), kind=kOutput, calls=%fused_computation.1 | convolution fusion | flops 1078984704 | bytes 8916992 | tf_op jit(solution)/shard_map/dot_general | solution.py:268
  (44 shorter events, 10.8 us)
Async XLA Ops:
  0.0 94.1 %copy-start = (bf16[512,512]{1,0:T(8,128)(2,1)S(1)}, bf16[512,512]{1,0:T(8,128)(2,1)}, u32[]{:S(2)}) copy-start(bf16[512,512]{1,0:T(8,128)(2,1)} %param.14) | copy-start | bytes 1572868
  0.0 13.0 %collective-permute-start.3 = (bf16[64,8192]{1,0:T(8,128)(2,1)}, bf16[64,8192]{1,0:T(8,128)(2,1)S(1)}, u32[]{:S(2)}, u32[]{:S(2)}) collective-permute-start(bf16[64,8192]{1,0:T(8,128)(2,1)} %bitcast.18), channel_id=1, source_target_pairs={{0,8},{8,0},{16,24},{24,16},{32,40},{40,32},{48,56},{56,48},{64,72... | collective-permute-start | bytes 3145736 | tf_op jit(solution)/shard_map/ppermute | solution.py:26
  1.4 26.6 %collective-permute-start = (bf16[64,8192]{1,0:T(8,128)(2,1)}, bf16[64,8192]{1,0:T(8,128)(2,1)}, u32[]{:S(2)}, u32[]{:S(2)}) collective-permute-start(bf16[64,8192]{1,0:T(8,128)(2,1)} %bitcast.19), channel_id=1, source_target_pairs={{0,64},{8,72},{16,80},{24,88},{32,96},{40,104},{48,112},{56,120},{... | collective-permute-start | bytes 3145736 | tf_op jit(solution)/shard_map/ppermute | solution.py:26
  4.3 26.1 %collective-permute-start.1 = (bf16[64,8192]{1,0:T(8,128)(2,1)}, bf16[64,8192]{1,0:T(8,128)(2,1)}, u32[]{:S(2)}, u32[]{:S(2)}) collective-permute-start(bf16[64,8192]{1,0:T(8,128)(2,1)} %bitcast.20), channel_id=1, source_target_pairs={{0,16},{8,24},{16,32},{24,40},{32,48},{40,56},{48,0},{56,8},{64,80... | collective-permute-start | bytes 3145736 | tf_op jit(solution)/shard_map/ppermute | solution.py:26
  5.6 24.8 %collective-permute-start.2 = (bf16[64,8192]{1,0:T(8,128)(2,1)}, bf16[64,8192]{1,0:T(8,128)(2,1)}, u32[]{:S(2)}, u32[]{:S(2)}) collective-permute-start(bf16[64,8192]{1,0:T(8,128)(2,1)} %bitcast.21), channel_id=1, source_target_pairs={{0,48},{8,56},{16,0},{24,8},{32,16},{40,24},{48,32},{56,40},{64,11... | collective-permute-start | bytes 3145736 | tf_op jit(solution)/shard_map/ppermute | solution.py:26
  30.4 3.7 %collective-permute-start.8 = (bf16[64,8192]{1,0:T(8,128)(2,1)}, bf16[64,8192]{1,0:T(8,128)(2,1)}, u32[]{:S(2)}, u32[]{:S(2)}) collective-permute-start(bf16[64,8192]{1,0:T(8,128)(2,1)} %collective-permute-done.1.refs_2_), channel_id=1, source_target_pairs={{0,8},{8,0},{16,24},{24,16},{32,40},{40,32},{48,56},{56,48},{64,72... | collective-permute-start | bytes 3145736 | tf_op jit(solution)/shard_map/ppermute | solution.py:26
  31.5 10.3 %collective-permute-start.7 = (bf16[64,8192]{1,0:T(8,128)(2,1)}, bf16[64,8192]{1,0:T(8,128)(2,1)}, u32[]{:S(2)}, u32[]{:S(2)}) collective-permute-start(bf16[64,8192]{1,0:T(8,128)(2,1)} %collective-permute-done.refs_1_), channel_id=1, source_target_pairs={{0,8},{8,0},{16,24},{24,16},{32,40},{40,32},{48,56},{56,48},{64,72... | collective-permute-start | bytes 3145736 | tf_op jit(solution)/shard_map/ppermute | solution.py:26
  31.5 10.3 %collective-permute-start.9 = (bf16[64,8192]{1,0:T(8,128)(2,1)}, bf16[64,8192]{1,0:T(8,128)(2,1)}, u32[]{:S(2)}, u32[]{:S(2)}) collective-permute-start(bf16[64,8192]{1,0:T(8,128)(2,1)} %collective-permute-done.2.refs_3_), channel_id=1, source_target_pairs={{0,8},{8,0},{16,24},{24,16},{32,40},{40,32},{48,56},{56,48},{64,72... | collective-permute-start | bytes 3145736 | tf_op jit(solution)/shard_map/ppermute | solution.py:26
  32.0 26.5 %collective-permute-start.4 = (bf16[64,8192]{1,0:T(8,128)(2,1)}, bf16[64,8192]{1,0:T(8,128)(2,1)S(1)}, u32[]{:S(2)}, u32[]{:S(2)}) collective-permute-start(bf16[64,8192]{1,0:T(8,128)(2,1)} %collective-permute-done.1.refs_2_), channel_id=1, source_target_pairs={{0,64},{8,72},{16,80},{24,88},{32,96},{40,104},{48,112},{56,120},{... | collective-permute-start | bytes 3145736 | tf_op jit(solution)/shard_map/ppermute | solution.py:26
  32.2 26.3 %collective-permute-start.5 = (bf16[64,8192]{1,0:T(8,128)(2,1)}, bf16[64,8192]{1,0:T(8,128)(2,1)}, u32[]{:S(2)}, u32[]{:S(2)}) collective-permute-start(bf16[64,8192]{1,0:T(8,128)(2,1)} %collective-permute-done.1.refs_2_), channel_id=1, source_target_pairs={{0,16},{8,24},{16,32},{24,40},{32,48},{40,56},{48,0},{56,8},{64,80... | collective-permute-start | bytes 3145736 | tf_op jit(solution)/shard_map/ppermute | solution.py:26
  34.1 25.1 %collective-permute-start.6 = (bf16[64,8192]{1,0:T(8,128)(2,1)}, bf16[64,8192]{1,0:T(8,128)(2,1)S(1)}, u32[]{:S(2)}, u32[]{:S(2)}) collective-permute-start(bf16[64,8192]{1,0:T(8,128)(2,1)} %collective-permute-done.refs_1_), channel_id=1, source_target_pairs={{0,48},{8,56},{16,0},{24,8},{32,16},{40,24},{48,32},{56,40},{64,11... | collective-permute-start | bytes 3145736 | tf_op jit(solution)/shard_map/ppermute | solution.py:26
  36.7 51.0 %all-to-all-start = ((bf16[8,64,2048]{2,1,0:T(8,128)(2,1)}), bf16[8,64,2048]{2,1,0:T(8,128)(2,1)}, u32[]{:S(2)}, u32[]{:S(2)}) async-start(bf16[8,64,2048]{2,1,0:T(8,128)(2,1)} %place_features.1), calls=%async_computation | async-start | bytes 4194304 | tf_op jit(solution)/shard_map/all_to_all | solution.py:263
  58.5 7.4 %copy-start.1 = (bf16[64,8192]{1,0:T(8,128)(2,1)}, bf16[64,8192]{1,0:T(8,128)(2,1)S(1)}, u32[]{:S(2)}) copy-start(bf16[64,8192]{1,0:T(8,128)(2,1)S(1)} %collective-permute-done.4.up_ref.refs_2_) | copy-start | bytes 3145732
  59.2 6.6 %copy-start.2 = (bf16[64,8192]{1,0:T(8,128)(2,1)}, bf16[64,8192]{1,0:T(8,128)(2,1)S(1)}, u32[]{:S(2)}) copy-start(bf16[64,8192]{1,0:T(8,128)(2,1)S(1)} %collective-permute-done.6.down_ref.refs_3_) | copy-start | bytes 3145732
  59.2 6.2 %collective-permute-start.12 = (bf16[64,8192]{1,0:T(8,128)(2,1)}, bf16[64,8192]{1,0:T(8,128)(2,1)}, u32[]{:S(2)}, u32[]{:S(2)}) collective-permute-start(bf16[64,8192]{1,0:T(8,128)(2,1)} %collective-permute-done.5.refs_1_), channel_id=1, source_target_pairs={{0,8},{8,0},{16,24},{24,16},{32,40},{40,32},{48,56},{56,48},{64,72... | collective-permute-start | bytes 3145736 | tf_op jit(solution)/shard_map/ppermute | solution.py:26
  60.4 5.0 %collective-permute-start.13 = (bf16[64,8192]{1,0:T(8,128)(2,1)S(1)}, bf16[64,8192]{1,0:T(8,128)(2,1)}, u32[]{:S(2)}, u32[]{:S(2)}) collective-permute-start(bf16[64,8192]{1,0:T(8,128)(2,1)S(1)} %collective-permute-done.4.up_ref.refs_2_), channel_id=1, source_target_pairs={{0,8},{8,0},{16,24},{24,16},{32,40},{40,32},{48,56},{56,48},{64,72... | collective-permute-start | bytes 3145736 | tf_op jit(solution)/shard_map/ppermute | solution.py:26
  60.4 5.4 %collective-permute-start.14 = (bf16[64,8192]{1,0:T(8,128)(2,1)S(1)}, bf16[64,8192]{1,0:T(8,128)(2,1)}, u32[]{:S(2)}, u32[]{:S(2)}) collective-permute-start(bf16[64,8192]{1,0:T(8,128)(2,1)S(1)} %collective-permute-done.6.down_ref.refs_3_), channel_id=1, source_target_pairs={{0,8},{8,0},{16,24},{24,16},{32,40},{40,32},{48,56},{56,48},{64,72... | collective-permute-start | bytes 3145736 | tf_op jit(solution)/shard_map/ppermute | solution.py:26
  61.9 16.0 %collective-permute-start.10 = (bf16[32,8192]{1,0:T(8,128)(2,1)}, bf16[32,8192]{1,0:T(8,128)(2,1)S(1)}, u32[]{:S(2)}, u32[]{:S(2)}) collective-permute-start(bf16[32,8192]{1,0:T(8,128)(2,1)} %get-tuple-element.26), channel_id=1, source_target_pairs={{0,16},{8,24},{16,32},{24,40},{32,48},{40,56},{48,0},{56,8},{64,80... | collective-permute-start | bytes 1572872 | tf_op jit(solution)/shard_map/ppermute | solution.py:26
  62.8 15.2 %collective-permute-start.11 = (bf16[32,8192]{1,0:T(8,128)(2,1)}, bf16[32,8192]{1,0:T(8,128)(2,1)}, u32[]{:S(2)}, u32[]{:S(2)}) collective-permute-start(bf16[32,8192]{1,0:T(8,128)(2,1)} %get-tuple-element.27), channel_id=1, source_target_pairs={{0,48},{8,56},{16,0},{24,8},{32,16},{40,24},{48,32},{56,40},{64,11... | collective-permute-start | bytes 1572872 | tf_op jit(solution)/shard_map/ppermute | solution.py:26
  77.9 2.0 %collective-permute-start.15 = (bf16[32,8192]{1,0:T(8,128)(2,1)S(1)}, bf16[32,8192]{1,0:T(8,128)(2,1)S(1)}, u32[]{:S(2)}, u32[]{:S(2)}) collective-permute-start(bf16[32,8192]{1,0:T(8,128)(2,1)S(1)} %collective-permute-done.10.refs_1_), channel_id=1, source_target_pairs={{0,8},{8,0},{16,24},{24,16},{32,40},{40,32},{48,56},{56,48},{64,72... | collective-permute-start | bytes 1572872 | tf_op jit(solution)/shard_map/ppermute | solution.py:26
  78.4 2.5 %collective-permute-start.16 = (bf16[32,8192]{1,0:T(8,128)(2,1)}, bf16[32,8192]{1,0:T(8,128)(2,1)S(1)}, u32[]{:S(2)}, u32[]{:S(2)}) collective-permute-start(bf16[32,8192]{1,0:T(8,128)(2,1)} %collective-permute-done.11.refs_2_), channel_id=1, source_target_pairs={{0,8},{8,0},{16,24},{24,16},{32,40},{40,32},{48,56},{56,48},{64,72... | collective-permute-start | bytes 1572872 | tf_op jit(solution)/shard_map/ppermute | solution.py:26
  87.7 31.2 %all-to-all-start.1 = ((bf16[8,64,2048]{2,1,0:T(8,128)(2,1)}), bf16[8,64,2048]{2,1,0:T(8,128)(2,1)S(1)}, u32[]{:S(2)}, u32[]{:S(2)}) async-start(bf16[8,64,2048]{2,1,0:T(8,128)(2,1)} %aggregate_last.1), calls=%async_computation.1 | async-start | bytes 4194304 | tf_op jit(solution)/shard_map/all_to_all | solution.py:263
  94.1 24.8 %copy-start.6 = (bf16[512,512]{1,0:T(8,128)(2,1)S(1)}, bf16[512,512]{1,0:T(8,128)(2,1)}, u32[]{:S(2)}) copy-start(bf16[512,512]{1,0:T(8,128)(2,1)} %param.15) | copy-start | bytes 1572868
  94.1 24.8 %copy-start.7 = (f32[512]{0:T(512)S(1)}, f32[512]{0:T(512)}, u32[]{:S(2)}) copy-start(f32[512]{0:T(512)} %param.16) | copy-start | bytes 6148
  (3 other events, 9.2 us)
